TPU v7x, 256 devices: a whole 4x4x8 slice. The times are simulated.
256 devices in a mesh: island: 8 (over x, z_hi), own: 32 (over z_lo, y, core).
Axes of the slice: x: 4, y: 4, z: 8 (z_hi: 2, z_lo: 4; z = z_hi * 4 + z_lo), core: 2. Of those that a mesh axis runs over, the one named last changes fastest.
Arguments:
- master: float32 [8, 2048, 8192], P(None, ('island', 'own')), may hold values from -6 to 6
- momentum: float32 [8, 2048, 8192], P(None, ('island', 'own')), may hold values from -6 to 6
- deltas: float32 [8, 2048, 8192], P('island', None, 'own'), may hold values from -6 to 6
- old_path: int32 [8], replicated, may hold values from 0 to 255
- new_path: int32 [8], replicated, may hold values from 0 to 255
- path_module: int32 [256], replicated, may hold values from 0 to 7
- island_steps: int32 [8], replicated, may hold values from 1 to 9
Outputs:
- new_master: float32 [8, 2048, 8192], P(None, ('island', 'own'))
- new_momentum: float32 [8, 2048, 8192], P(None, ('island', 'own'))
- new_module: float32 [8, 2048, 8192], P('island', None, 'own')
All inputs are finite; a program needn't handle non-finite values.
Results may differ from a plain program's by a relative error of at most 0.00007.
Values sent between devices are 32-bit elements; how exact they have to be, the bound alone decides.
No kernel may reach another device: no remote copies, remote signals or barrier semaphores. Data moves between devices by JAX's collectives and lax.ppermute only.
A program may use at most 64 MiB of HBM per device.

v0:
```python
import jax
import jax.numpy as jnp
from jax import lax
from jax.sharding import PartitionSpec as P


def cut_along(value, dim, length):
    dims = value.shape
    pieces = value.reshape(*dims[:dim], length, dims[dim] // length, *dims[dim + 1 :])
    return jnp.moveaxis(pieces, dim, 0)


def laid_out(pieces, dim):
    dims = list(pieces.shape[1:])
    dims[dim] *= pieces.shape[0]
    return jnp.moveaxis(pieces, 0, dim).reshape(dims)


def joined_exchange(value, axis, axes, splits, concats):
    sizes = [lax.axis_size(a) for a in axes]
    pieces = cut_along(value, splits[0], sizes[0])
    pieces = jnp.moveaxis(cut_along(pieces, splits[1] + 1, sizes[1]), 0, 1)
    inside = pieces.shape[2:]
    pieces = pieces.reshape(-1, *inside)
    pieces = lax.all_to_all(pieces, axis, split_axis=0, concat_axis=0, tiled=True)
    pieces = laid_out(pieces.reshape(*sizes, *inside), concats[0] + 1)
    return laid_out(pieces, concats[1])


def shards(master, momentum, deltas, old_path, new_path, path_module, island_steps):
    modules = master.shape[0]
    received = joined_exchange(deltas, ("island", "own"), ("island", "own"), (1, 1), (0, 2))
    old_module = path_module[old_path]
    chosen = old_module[None, :] == jnp.arange(modules, dtype=jnp.int32)[:, None]
    mixing = chosen.astype(jnp.float32) * island_steps.astype(jnp.float32)[None, :]
    divisor = jnp.maximum(jnp.sum(mixing, axis=1), 1.0)
    average = jnp.einsum("kj,jrc->krc", mixing, received, precision=lax.Precision.HIGHEST)
    average = average / divisor[:, None, None]
    new_momentum = 0.9 * momentum + average
    new_master = master - 0.7 * (average + 0.9 * new_momentum)
    new_index = path_module[new_path]
    picked = jnp.take(new_master, new_index, axis=0)
    isles = picked.shape[0]
    rows_block = picked.shape[1]
    sectioned = picked.reshape(isles, 1, rows_block, picked.shape[2])
    landed = joined_exchange(sectioned, ("island", "own"), ("island", "own"), (0, 3), (1, 2))
    new_module = landed.reshape(1, landed.shape[1] * landed.shape[2], landed.shape[3])
    return (new_master, new_momentum, new_module)


def solution(mesh):
    return jax.shard_map(
        shards,
        mesh=mesh,
        in_specs=(
            P(None, ("island", "own"), None),
            P(None, ("island", "own"), None),
            P("island", None, "own"),
            P(),
            P(),
            P(),
            P(),
        ),
        out_specs=(
            P(None, ("island", "own"), None),
            P(None, ("island", "own"), None),
            P("island", None, "own"),
        ),
        check_vma=False,
    )
```

profile of v0, /device:TPU:8, one launch (start us, length us, event | category | flops | bytes accessed | tf_op | source)
XLA Modules:
  0.0 144.5 jit_solution(1303924290530480557)
XLA Ops:
  0.6 0.0 copy-start
  0.6 0.0 copy-start.4
  0.7 0.0 copy-start.5
  0.7 0.0 copy-start.6
  0.7 14.6 %all-to-all-start = ((f32[256,1,8,256]{3,2,1,0:T(8,128)}), f32[256,1,8,256]{3,2,1,0:T(8,128)S(1)}, u32[]{:S(2)}, u32[]{:S(2)}) async-start(f32[256,1,8,256]{3,2,1,0:T(8,128)} %bitcast.38), calls=%async_computation | async-start | bytes 4194304 | tf_op jit(solution)/shard_map/all_to_all | solution.py:25
  15.3 0.0 copy-done.4
  15.3 0.0 copy-done.5
  15.4 0.6 gather_fusion.1
  16.0 0.6 gather_fusion
  16.7 0.1 select_reduce_fusion
  16.8 52.1 %all-to-all-done = f32[256,1,8,256]{3,2,1,0:T(8,128)S(1)} async-done(((f32[256,1,8,256]{3,2,1,0:T(8,128)}), f32[256,1,8,256]{3,2,1,0:T(8,128)S(1)}, u32[]{:S(2)}, u32[]{:S(2)}) %all-to-all-start) | async-done | bytes 2097184 | tf_op jit(solution)/shard_map/all_to_all | solution.py:25
  69.0 1.2 copy.20
  70.2 0.4 copy-done.2
  70.6 0.6 copy-done.3
  71.2 5.7 %fusion = (f32[8,8,8192]{2,0,1:T(8,128)}, f32[8,8,8192]{2,0,1:T(8,128)S(1)}) fusion(f32[8,8,8192]{2,1,0:T(8,128)S(1)} %copy-done.2, f32[8,8,8192]{2,1,0:T(8,128)S(1)} %copy-done.3, f32[8]{0:T(128)S(1)} %broadcast_maximum_fusion, f32[8,8,8192]{2,0,1:T(8,128)S(1)} %bitcast.39, f32[8]{0:T(128)S(1)} %convert_element_type.4, s32[8]{0:T(128)S(1)} %gather_fusion), kind=kOutput, calls=%fused_computation.6 | convolution fusion | flops 54001792 | bytes 10485856 | tf_op jit(solution)/shard_map/kj,jrc->krc/dot_general | solution.py:37
  76.9 1.2 copy.25
  78.1 0.0 copy-start.1
  78.1 2.1 %gather_fusion.2 = f32[8,8,8192]{2,1,0:T(8,128)} fusion(f32[8,8,8192]{2,1,0:T(8,128)S(1)} %copy.25, s32[1024]{0:T(1024)S(1)} %pad_clamp_fusion), kind=kCustom, calls=%fused_computation.2 | custom fusion | bytes 4194336 | tf_op jit(solution)/shard_map/jit(_take)/gather | solution.py:42
  80.2 0.0 copy-done.1
  80.2 3.2 %broadcast_select_fusion = f32[8,1,1,8,32,256]{5,3,4,0,2,1:T(8,128)} fusion(f32[8,1,1,8,32,256]{5,3,4,0,2,1:T(8,128)} %bitcast.37, pred[8]{0:T(512)(128)(4,1)S(1)} %compare_and_fusion), kind=kLoop, calls=%fused_computation.7 | loop fusion | flops 524288 | bytes 4194312 | tf_op jit(solution)/shard_map/jit(_take)/select_n | solution.py:42
  83.4 6.1 %all-to-all-start.1 = ((f32[256,1,1,8,256]{4,3,2,1,0:T(8,128)}), f32[256,1,1,8,256]{4,3,2,1,0:T(8,128)S(1)}, u32[]{:S(2)}, u32[]{:S(2)}) async-start(f32[256,1,1,8,256]{4,3,2,1,0:T(8,128)} %bitcast.36), calls=%async_computation.1 | async-start | bytes 4194304 | tf_op jit(solution)/shard_map/all_to_all | solution.py:25
  89.5 4.1 %copy.26 = f32[8,8,8192]{2,1,0:T(8,128)} copy(f32[8,8,8192]{2,0,1:T(8,128)} %get-tuple-element.12) | data formatting | bytes 4194304
  93.6 49.5 %all-to-all-done.1 = f32[256,1,1,8,256]{4,3,2,1,0:T(8,128)S(1)} async-done(((f32[256,1,1,8,256]{4,3,2,1,0:T(8,128)}), f32[256,1,1,8,256]{4,3,2,1,0:T(8,128)S(1)}, u32[]{:S(2)}, u32[]{:S(2)}) %all-to-all-start.1) | async-done | bytes 2097184 | tf_op jit(solution)/shard_map/all_to_all | solution.py:25
  143.2 1.3 copy.34
  (13 shorter events, 0.1 us)
Async XLA Ops:
  0.6 14.7 %copy-start = (s32[256]{0:T(256)S(1)}, s32[256]{0:T(256)}, u32[]{:S(2)}) copy-start(s32[256]{0:T(256)} %param.12) | copy-start | bytes 3076
  0.6 14.7 %copy-start.4 = (s32[8]{0:T(128)S(1)}, s32[8]{0:T(128)}, u32[]{:S(2)}) copy-start(s32[8]{0:T(128)} %param.13) | copy-start | bytes 100
  0.7 14.7 %copy-start.5 = (s32[8]{0:T(128)S(1)}, s32[8]{0:T(128)}, u32[]{:S(2)}) copy-start(s32[8]{0:T(128)} %param.11) | copy-start | bytes 100
  0.7 15.3 %copy-start.6 = (s32[8]{0:T(128)S(1)}, s32[8]{0:T(128)}, u32[]{:S(2)}) copy-start(s32[8]{0:T(128)} %param.10) | copy-start | bytes 100
  0.7 68.3 %all-to-all-start = ((f32[256,1,8,256]{3,2,1,0:T(8,128)}), f32[256,1,8,256]{3,2,1,0:T(8,128)S(1)}, u32[]{:S(2)}, u32[]{:S(2)}) async-start(f32[256,1,8,256]{3,2,1,0:T(8,128)} %bitcast.38), calls=%async_computation | async-start | bytes 4194304 | tf_op jit(solution)/shard_map/all_to_all | solution.py:25
  69.0 1.6 %copy-start.2 = (f32[8,8,8192]{2,1,0:T(8,128)S(1)}, f32[8,8,8192]{2,1,0:T(8,128)}, u32[]{:S(2)}) copy-start(f32[8,8,8192]{2,1,0:T(8,128)} %param.8) | copy-start | bytes 6291460
  69.0 2.2 %copy-start.3 = (f32[8,8,8192]{2,1,0:T(8,128)S(1)}, f32[8,8,8192]{2,1,0:T(8,128)}, u32[]{:S(2)}) copy-start(f32[8,8,8192]{2,1,0:T(8,128)} %param.7) | copy-start | bytes 6291460
  78.1 2.1 %copy-start.1 = (f32[8,8,8192]{2,1,0:T(8,128)}, f32[8,8,8192]{2,1,0:T(8,128)S(1)}, u32[]{:S(2)}) copy-start(f32[8,8,8192]{2,1,0:T(8,128)S(1)} %copy.25) | copy-start | bytes 6291460
  83.4 59.8 %all-to-all-start.1 = ((f32[256,1,1,8,256]{4,3,2,1,0:T(8,128)}), f32[256,1,1,8,256]{4,3,2,1,0:T(8,128)S(1)}, u32[]{:S(2)}, u32[]{:S(2)}) async-start(f32[256,1,1,8,256]{4,3,2,1,0:T(8,128)} %bitcast.36), calls=%async_computation.1 | async-start | bytes 4194304 | tf_op jit(solution)/shard_map/all_to_all | solution.py:25
where the time goes:
time: 146 us; the launch traced here: 144 us
  waiting for transfers between devices  102 us (70%)
  starting transfers between devices  20.7 us (14%)
  local copies, waits for them, and re-layouts  12.3 us (8%)
  matrix products  5.66 us (4%)
  other arithmetic  3.38 us (2%)
    all_to_all x2, waiting for transfers between devices, joined_exchange(): lax.all_to_all(pieces, axis, split_axis=0, concat_axis=0, tiled=True)  102 us
    all_to_all x2, starting transfers between devices, joined_exchange(): lax.all_to_all(pieces, axis, split_axis=0, concat_axis=0, tiled=True)  20.7 us
    unnamed x17, local copies, waits for them, and re-layouts  7.7 us
    dot_general x1, matrix products, shards(): jnp.einsum('kj,jrc->krc', mixing, received, precision=lax.Precision.HIGHEST)  5.66 us
    select_n x2, other arithmetic, shards(): picked = jnp.take(new_master, new_index, axis=0)  3.23 us
  transfers between devices with their start and end apart: 2, of which 2 were waited for; matrix products, arithmetic and copies ran while one was open for 4% of the time, Pallas kernels for 0%

commit v1 on v0

v1 whole, which is shorter than its diff:
```python
import math

import jax
import jax.numpy as jnp
from jax import lax
from jax.experimental import pallas as pl
from jax.experimental.pallas import tpu as pltpu
from jax.sharding import Mesh
from jax.sharding import PartitionSpec as P

Z = ("zh", "zl")
PLANE = ("x", "y", "c")
NX, NZ, NYC = 4, 8, 8
NP = NX * NYC
SHIFTS = (4, 3, 5, 2, 6, 1, 7)
TILE = (8, 128)
F32 = jnp.float32
MIB = 1 << 20


def tiles(value):
    lead, rows, cols = value.shape[:-2], value.shape[-2], value.shape[-1]
    value = value.reshape(*lead, rows // 8, 8, cols // 128, 128)
    return jnp.swapaxes(value, -3, -2)


def call(body, ins, outs, scalars=1, limit=16 * MIB, **kw):
    smem = pl.BlockSpec(memory_space=pltpu.SMEM)
    vmem = pl.BlockSpec(memory_space=pltpu.VMEM)
    moved = 4 * (sum(a.size for a in ins[scalars:]) + sum(math.prod(s) for s in outs))
    return pl.pallas_call(
        body,
        out_shape=[jax.ShapeDtypeStruct(s, F32) for s in outs],
        in_specs=[smem] * scalars + [vmem] * (len(ins) - scalars),
        out_specs=[vmem] * len(outs),
        cost_estimate=pl.CostEstimate(flops=moved, bytes_accessed=moved, transcendentals=0),
        compiler_params=pltpu.CompilerParams(vmem_limit_bytes=limit),
        **kw,
    )(*ins)


def part(x):
    return pl.ds(x * NYC, NYC)


def cut_kernel(z_ref, d_ref, *outs):
    z = z_ref[0]
    for d in range(NZ):
        to = lax.rem(z + d, NZ)
        for x in range(NX):
            rows = pl.ds(x * NZ * NYC + to * NYC, NYC)
            outs[d][part(x)] = d_ref[rows, 0]
            outs[NZ][part(x), d] = d_ref[rows, 1]


def stack_kernel(*refs):
    for d in range(NZ):
        refs[NZ][:, d] = refs[d][...]


def unstack_kernel(src, *outs):
    for d in range(NZ):
        outs[d][...] = src[:, d]


def weights(modules, old_ref, pm_ref, steps_ref, k):
    mix = []
    total = jnp.int32(0)
    for j in range(steps_ref.shape[0]):
        w = jnp.where(pm_ref[old_ref[j]] == k, steps_ref[j], 0)
        total += w
        mix.append(w)
    inverse = 1.0 / jnp.full(TILE, jnp.maximum(total, 1), jnp.int32).astype(F32)
    return [w.astype(F32) for w in mix], inverse


def average(read, mix, inverse, d, same):
    total = None
    for x in range(NX):
        for e in range(2):
            lo, hi = mix[2 * x], mix[2 * x + 1]
            w = jnp.where(same == e, lo, hi)
            term = w * read(x, d + 4 * e)
            total = term if total is None else total + term
    return total * inverse


def held_by(z, d):
    other = lax.rem(z - d + NZ, NZ)
    return other >> 2, other & 3


def step(m, v, avg):
    v = 0.9 * v + avg
    return m - 0.7 * (avg + 0.9 * v), v


def pick_kernel(half, split, z_ref, old_ref, new_ref, pm_ref, steps_ref, *refs):
    z = z_ref[0]
    n = NZ if split else 1
    src, (m_ref, v_ref), outs = refs[:n], refs[n : n + 2], refs[n + 2 :]
    read = lambda x, d: src[d][part(x)] if split else src[0][part(x), d]
    for j in range(steps_ref.shape[0]):
        k = pm_ref[new_ref[j]]
        mix, inverse = weights(m_ref.shape[0], old_ref, pm_ref, steps_ref, k)
        for d in range(4):
            same, place = held_by(z, d)
            avg = average(read, mix, inverse, d, same)
            new, _ = step(m_ref[k, place, :, half], v_ref[k, place, :, half], avg)
            near, far = (NZ - d) % NZ, (NZ + 4 - d) % NZ
            here = j % 2 == same
            if split:
                for way, pick in ((near, here), (far, jnp.logical_not(here))):

                    @pl.when(pick)
                    def _():
                        outs[way][part(j // 2)] = new
            else:
                outs[0][part(j // 2), jnp.where(here, near, far)] = new


def owner_kernel(z_ref, old_ref, pm_ref, steps_ref, *refs):
    z = z_ref[0]
    a_ref, b_refs, (m_ref, v_ref, nm_ref, nv_ref) = refs[0], refs[1 : 1 + NZ], refs[1 + NZ :]
    reads = (lambda x, d: a_ref[part(x), d], lambda x, d: b_refs[d][part(x)])
    for k in range(m_ref.shape[0]):
        mix, inverse = weights(m_ref.shape[0], old_ref, pm_ref, steps_ref, k)
        for d in range(4):
            same, place = held_by(z, d)
            for half in range(2):
                avg = average(reads[half], mix, inverse, d, same)
                new, mom = step(m_ref[k, place, :, half], v_ref[k, place, :, half], avg)
                nm_ref[k, place, :, half] = new
                nv_ref[k, place, :, half] = mom


def join_kernel(z_ref, b_ref, *refs):
    z = z_ref[0]
    for d in range(NZ):
        source = lax.rem(z - d + NZ, NZ)
        for x in range(NX):
            rows = pl.ds(x * NZ * NYC + source * NYC, NYC)
            refs[NZ][rows, 0] = refs[d][part(x)]
            refs[NZ][rows, 1] = b_ref[part(x), d]


def along_z(pieces):
    got = [pieces[0]] + [None] * (NZ - 1)
    for d in SHIFTS:
        got[d] = lax.ppermute(pieces[d], Z, [(i, (i + d) % NZ) for i in range(NZ)])
    return got


def in_plane(value):
    return lax.all_to_all(value, PLANE, split_axis=0, concat_axis=0, tiled=True)


def shards(master, momentum, deltas, old_path, new_path, path_module, island_steps):
    modules = master.shape[0]
    z = lax.axis_index(Z).astype(jnp.int32).reshape(1)
    piece, packed = (NP, *TILE), (NP, NZ, *TILE)
    owner = (modules, 4, NYC, 2, *TILE)
    m = tiles(master).reshape(owner)
    v = tiles(momentum).reshape(owner)
    d = tiles(deltas[0])

    *a, b = call(cut_kernel, [z, d], [piece] * NZ + [packed])
    a = along_z(a)
    b = in_plane(b)
    [a] = call(stack_kernel, a, [packed], scalars=0)
    b = call(unstack_kernel, [b], [piece] * NZ, scalars=0)
    b = along_z(b)
    a = in_plane(a)

    def pick(half, split, *src):
        body = lambda *refs: pick_kernel(half, split, *refs)
        outs = [piece] * NZ if split else [packed]
        return call(body, [z, old_path, new_path, path_module, island_steps, *src, m, v], outs, scalars=5)

    [pa] = pick(0, False, a)
    pb = pick(1, True, *b)
    nm, nv = call(owner_kernel, [z, old_path, path_module, island_steps, a, *b, m, v], [owner] * 2, scalars=4, limit=24 * MIB)
    pa = in_plane(pa)
    pb = along_z(pb)
    pa = call(unstack_kernel, [pa], [piece] * NZ, scalars=0)
    [pb] = call(stack_kernel, pb, [packed], scalars=0)
    pa = along_z(pa)
    pb = in_plane(pb)
    [out] = call(join_kernel, [z, pb, *pa], [d.shape])

    def whole(value):
        return jnp.swapaxes(value.reshape(modules, 64, *TILE), 1, 2).reshape(master.shape)

    new_module = jnp.swapaxes(out, 1, 2).reshape(deltas.shape)
    return whole(nm), whole(nv), new_module


def solution(mesh):
    fine = Mesh(mesh.devices.reshape(4, 2, 4, 4, 2), ("x", "zh", "zl", "y", "c"))
    owners = P(None, ("x", "zh", "zl", "y", "c"), None)
    island = P(("x", "zh"), None, ("zl", "y", "c"))
    return jax.shard_map(
        shards,
        mesh=fine,
        in_specs=(owners, owners, island, P(), P(), P(), P()),
        out_specs=(owners, owners, island),
        check_vma=False,
    )
```

time: 146 us -> 208 us (1.42)
  starting transfers between devices: 20.7 us -> 81.5 us
  waiting for transfers between devices: 102 us -> 69.8 us
  blocking collectives: 0 us -> 23 us
  Pallas kernels: 0 us -> 14.3 us
  matrix products: 5.66 us -> 0 us
  local copies, waits for them, and re-layouts: 12.3 us -> 17.6 us
  other arithmetic: 3.38 us -> 0 us
    all_to_all x2 -> x3, waiting for transfers between devices: 102 us -> 11.6 us  [in_plane(): return lax.all_to_all(value, PLANE, split_axis=0, concat_axis=0, tiled=True)]
    ppermute x0 -> x28, starting transfers between devices: none -> 62.4 us  [along_z(): got[d] = lax.ppermute(pieces[d], Z, [(i, (i + d) % NZ) for i in range(NZ)])]
    ppermute x0 -> x28, waiting for transfers between devices: none -> 58.3 us  [along_z(): got[d] = lax.ppermute(pieces[d], Z, [(i, (i + d) % NZ) for i in range(NZ)])]
    all_to_all x0 -> x1, blocking collectives: none -> 23 us  [in_plane(): return lax.all_to_all(value, PLANE, split_axis=0, concat_axis=0, tiled=True)]
    pallas_call x0 -> x9, Pallas kernels: none -> 14.3 us  [call(): pl.pallas_call(body, out_shape=[jax.ShapeDtypeStruct(s, F32) for s in out...]
    unnamed x17 -> x56, local copies, waits for them, and re-layouts: 7.7 us -> 17.6 us
    dot_general x1 -> x0, matrix products: 5.66 us -> none  [shards(): jnp.einsum('kj,jrc->krc', mixing, received, precision=lax.Precision.HIGHEST)]
    gather x3 -> x0, local copies, waits for them, and re-layouts: 3.38 us -> none  [the longest x1 2.09 us: shards(): picked = jnp.take(new_master, new_index, axis=0)]
  transfers between devices with their start and end apart: 2 -> 31, of which waited for: 2 -> 20; matrix products, arithmetic and copies ran while one was open for 4% -> 0% of each run, Pallas kernels for 0% -> 5%
where the time goes in v1:
time: 208 us; the launch traced here: 207 us
  starting transfers between devices  81.5 us (39%)
  waiting for transfers between devices  69.8 us (34%)
  blocking collectives  23 us (11%)
  local copies, waits for them, and re-layouts  17.6 us (8%)
  Pallas kernels  14.3 us (7%)
    ppermute x28, starting transfers between devices, along_z(): got[d] = lax.ppermute(pieces[d], Z, [(i, (i + d) % NZ) for i in range(NZ)])  62.4 us
    ppermute x28, waiting for transfers between devices, along_z(): got[d] = lax.ppermute(pieces[d], Z, [(i, (i + d) % NZ) for i in range(NZ)])  58.3 us
    all_to_all x1, blocking collectives, in_plane(): return lax.all_to_all(value, PLANE, split_axis=0, concat_axis=0, tiled=True)  23 us
    all_to_all x3, starting transfers between devices, in_plane(): return lax.all_to_all(value, PLANE, split_axis=0, concat_axis=0, tiled=True)  19 us
    unnamed x56, local copies, waits for them, and re-layouts  17.6 us
    pallas_call x9, Pallas kernels, call(): pl.pallas_call(body, out_shape=[jax.ShapeDtypeStruct(s, F32) for s in out...  14.3 us
    all_to_all x3, waiting for transfers between devices, in_plane(): return lax.all_to_all(value, PLANE, split_axis=0, concat_axis=0, tiled=True)  11.6 us
  transfers between devices with their start and end apart: 31, of which 20 were waited for; matrix products, arithmetic and copies ran while one was open for 0% of the time, Pallas kernels for 5%

profile of v1, /device:TPU:8, one launch (start us, length us, event | category | flops | bytes accessed | tf_op | source)
XLA Modules:
  0.0 207.2 jit_solution(2189226445190205466)
XLA Ops:
  4.4 3.3 %collective-permute-start.1 = (f32[32,8,128]{2,1,0:T(8,128)S(1)}, f32[32,8,128]{2,1,0:T(8,128)S(1)}, u32[]{:S(2)}, u32[]{:S(2)}) collective-permute-start(f32[32,8,128]{2,1,0:T(8,128)S(1)} %get-tuple-element.40), channel_id=1, source_target_pairs={{0,16},{8,24},{16,32},{24,40},{32,48},{40,56},{48,0},{56,8},{1,17}... | collective-permute-start | bytes 393224 | tf_op jit(solution)/shard_map/ppermute | solution.py:150
  7.7 4.0 %collective-permute-start.2 = (f32[32,8,128]{2,1,0:T(8,128)S(1)}, f32[32,8,128]{2,1,0:T(8,128)S(1)}, u32[]{:S(2)}, u32[]{:S(2)}) collective-permute-start(f32[32,8,128]{2,1,0:T(8,128)S(1)} %get-tuple-element.41), channel_id=1, source_target_pairs={{0,24},{8,32},{16,40},{24,48},{32,56},{40,0},{48,8},{56,16},{1,25}... | collective-permute-start | bytes 393224 | tf_op jit(solution)/shard_map/ppermute | solution.py:150
  12.3 4.9 %collective-permute-start.4 = (f32[32,8,128]{2,1,0:T(8,128)S(1)}, f32[32,8,128]{2,1,0:T(8,128)S(1)}, u32[]{:S(2)}, u32[]{:S(2)}) collective-permute-start(f32[32,8,128]{2,1,0:T(8,128)S(1)} %get-tuple-element.43), channel_id=1, source_target_pairs={{0,40},{8,48},{16,56},{24,0},{32,8},{40,16},{48,24},{56,32},{1,41}... | collective-permute-start | bytes 393224 | tf_op jit(solution)/shard_map/ppermute | solution.py:150
  24.1 5.4 %collective-permute-done.2.refs_3_ = f32[32,8,128]{2,1,0:T(8,128)S(1)} collective-permute-done((f32[32,8,128]{2,1,0:T(8,128)S(1)}, f32[32,8,128]{2,1,0:T(8,128)S(1)}, u32[]{:S(2)}, u32[]{:S(2)}) %collective-permute-start.2) | collective-permute-done | bytes 131104 | tf_op jit(solution)/shard_map/ppermute | solution.py:150
  29.5 3.8 %collective-permute-done.4.refs_5_ = f32[32,8,128]{2,1,0:T(8,128)S(1)} collective-permute-done((f32[32,8,128]{2,1,0:T(8,128)S(1)}, f32[32,8,128]{2,1,0:T(8,128)S(1)}, u32[]{:S(2)}, u32[]{:S(2)}) %collective-permute-start.4) | collective-permute-done | bytes 131104 | tf_op jit(solution)/shard_map/ppermute | solution.py:150
  37.0 23.0 %all_to_all.20.refs_0_.refs_5_ = f32[32,8,8,128]{3,2,1,0:T(8,128)S(1)} all-to-all(f32[32,8,8,128]{3,2,1,0:T(8,128)S(1)} %shard_map.95), channel_id=1, replica_groups=mesh['x'=4,'zh'=2,'zl'=4,'y'=4,'c'=2] {'x','y','c'}, dimensions={0} | all-to-all | bytes 2097152 | tf_op jit(solution)/shard_map/all_to_all | solution.py:155
  60.0 5.8 %all-to-all-start.1 = ((f32[32,8,8,128]{3,2,1,0:T(8,128)}), f32[32,8,8,128]{3,2,1,0:T(8,128)}, u32[]{:S(2)}, u32[]{:S(2)}) async-start(f32[32,8,8,128]{3,2,1,0:T(8,128)} %copy-done.7), calls=%async_computation.1 | async-start | bytes 2097152 | tf_op jit(solution)/shard_map/all_to_all | solution.py:155
  69.9 11.5 %all-to-all-done.1.src = f32[32,8,8,128]{3,2,1,0:T(8,128)} async-done(((f32[32,8,8,128]{3,2,1,0:T(8,128)}), f32[32,8,8,128]{3,2,1,0:T(8,128)}, u32[]{:S(2)}, u32[]{:S(2)}) %all-to-all-start.1) | async-done | bytes 1048608 | tf_op jit(solution)/shard_map/all_to_all | solution.py:155
  81.5 5.7 %all-to-all-start.3 = ((f32[32,8,8,128]{3,2,1,0:T(8,128)}), f32[32,8,8,128]{3,2,1,0:T(8,128)}, u32[]{:S(2)}, u32[]{:S(2)}) async-start(f32[32,8,8,128]{3,2,1,0:T(8,128)} %copy-done.4), calls=%async_computation.3 | async-start | bytes 2097152 | tf_op jit(solution)/shard_map/all_to_all | solution.py:155
  88.5 3.1 %collective-permute-start.7 = (f32[32,8,128]{2,1,0:T(8,128)S(1)}, f32[32,8,128]{2,1,0:T(8,128)S(1)}, u32[]{:S(2)}, u32[]{:S(2)}) collective-permute-start(f32[32,8,128]{2,1,0:T(8,128)S(1)} %get-tuple-element.48), channel_id=1, source_target_pairs={{0,8},{8,16},{16,24},{24,32},{32,40},{40,48},{48,56},{56,0},{1,9},... | collective-permute-start | bytes 393224 | tf_op jit(solution)/shard_map/ppermute | solution.py:150
  93.4 4.7 %collective-permute-start.10 = (f32[32,8,128]{2,1,0:T(8,128)S(1)}, f32[32,8,128]{2,1,0:T(8,128)S(1)}, u32[]{:S(2)}, u32[]{:S(2)}) collective-permute-start(f32[32,8,128]{2,1,0:T(8,128)S(1)} %get-tuple-element.51), channel_id=1, source_target_pairs={{0,32},{8,40},{16,48},{24,56},{32,0},{40,8},{48,16},{56,24},{1,33}... | collective-permute-start | bytes 393224 | tf_op jit(solution)/shard_map/ppermute | solution.py:150
  102.0 6.6 %collective-permute-done.8.refs_3_.refs_7_ = f32[32,8,128]{2,1,0:T(8,128)S(1)} collective-permute-done((f32[32,8,128]{2,1,0:T(8,128)S(1)}, f32[32,8,128]{2,1,0:T(8,128)S(1)}, u32[]{:S(2)}, u32[]{:S(2)}) %collective-permute-start.8) | collective-permute-done | bytes 131104 | tf_op jit(solution)/shard_map/ppermute | solution.py:150
  108.6 5.0 %collective-permute-done.10.refs_5_.refs_9_ = f32[32,8,128]{2,1,0:T(8,128)S(1)} collective-permute-done((f32[32,8,128]{2,1,0:T(8,128)S(1)}, f32[32,8,128]{2,1,0:T(8,128)S(1)}, u32[]{:S(2)}, u32[]{:S(2)}) %collective-permute-start.10) | collective-permute-done | bytes 131104 | tf_op jit(solution)/shard_map/ppermute | solution.py:150
  113.9 5.3 %collective-permute-done.12.refs_7_.refs_11_ = f32[32,8,128]{2,1,0:T(8,128)S(1)} collective-permute-done((f32[32,8,128]{2,1,0:T(8,128)S(1)}, f32[32,8,128]{2,1,0:T(8,128)S(1)}, u32[]{:S(2)}, u32[]{:S(2)}) %collective-permute-start.12) | collective-permute-done | bytes 131104 | tf_op jit(solution)/shard_map/ppermute | solution.py:150
  132.6 4.2 %collective-permute-start.18 = (f32[32,8,128]{2,1,0:T(8,128)S(1)}, f32[32,8,128]{2,1,0:T(8,128)S(1)}, u32[]{:S(2)}, u32[]{:S(2)}) collective-permute-start(f32[32,8,128]{2,1,0:T(8,128)S(1)} %get-tuple-element.62), channel_id=1, source_target_pairs={{0,40},{8,48},{16,56},{24,0},{32,8},{40,16},{48,24},{56,32},{1,41}... | collective-permute-start | bytes 393224 | tf_op jit(solution)/shard_map/ppermute | solution.py:150
  136.8 3.0 %collective-permute-start.19 = (f32[32,8,128]{2,1,0:T(8,128)S(1)}, f32[32,8,128]{2,1,0:T(8,128)S(1)}, u32[]{:S(2)}, u32[]{:S(2)}) collective-permute-start(f32[32,8,128]{2,1,0:T(8,128)S(1)} %get-tuple-element.63), channel_id=1, source_target_pairs={{0,48},{8,56},{16,0},{24,8},{32,16},{40,24},{48,32},{56,40},{1,49}... | collective-permute-start | bytes 393224 | tf_op jit(solution)/shard_map/ppermute | solution.py:150
  141.9 6.1 %collective-permute-done.16.refs_3_ = f32[32,8,128]{2,1,0:T(8,128)S(1)} collective-permute-done((f32[32,8,128]{2,1,0:T(8,128)S(1)}, f32[32,8,128]{2,1,0:T(8,128)S(1)}, u32[]{:S(2)}, u32[]{:S(2)}) %collective-permute-start.16) | collective-permute-done | bytes 131104 | tf_op jit(solution)/shard_map/ppermute | solution.py:150
  148.0 3.0 %collective-permute-done.17.refs_4_ = f32[32,8,128]{2,1,0:T(8,128)S(1)} collective-permute-done((f32[32,8,128]{2,1,0:T(8,128)S(1)}, f32[32,8,128]{2,1,0:T(8,128)S(1)}, u32[]{:S(2)}, u32[]{:S(2)}) %collective-permute-start.17) | collective-permute-done | bytes 131104 | tf_op jit(solution)/shard_map/ppermute | solution.py:150
  152.5 3.5 %collective-permute-done.19.refs_6_ = f32[32,8,128]{2,1,0:T(8,128)S(1)} collective-permute-done((f32[32,8,128]{2,1,0:T(8,128)S(1)}, f32[32,8,128]{2,1,0:T(8,128)S(1)}, u32[]{:S(2)}, u32[]{:S(2)}) %collective-permute-start.19) | collective-permute-done | bytes 131104 | tf_op jit(solution)/shard_map/ppermute | solution.py:150
  158.6 7.5 %all-to-all-start.2 = ((f32[32,8,8,128]{3,2,1,0:T(8,128)}), f32[32,8,8,128]{3,2,1,0:T(8,128)}, u32[]{:S(2)}, u32[]{:S(2)}) async-start(f32[32,8,8,128]{3,2,1,0:T(8,128)} %copy-done.5), calls=%async_computation.2 | async-start | bytes 2097152 | tf_op jit(solution)/shard_map/all_to_all | solution.py:155
  173.4 4.3 %collective-permute-start.24 = (f32[32,8,128]{2,1,0:T(8,128)}, f32[32,8,128]{2,1,0:T(8,128)}, u32[]{:S(2)}, u32[]{:S(2)}) collective-permute-start(f32[32,8,128]{2,1,0:T(8,128)} %get-tuple-element.69), channel_id=1, source_target_pairs={{0,32},{8,40},{16,48},{24,56},{32,0},{40,8},{48,16},{56,24},{1,33}... | collective-permute-start | bytes 393224 | tf_op jit(solution)/shard_map/ppermute | solution.py:150
  182.7 5.8 %collective-permute-done.22.refs_2_ = f32[32,8,128]{2,1,0:T(8,128)S(1)} collective-permute-done((f32[32,8,128]{2,1,0:T(8,128)S(1)}, f32[32,8,128]{2,1,0:T(8,128)S(1)}, u32[]{:S(2)}, u32[]{:S(2)}) %collective-permute-start.22) | collective-permute-done | bytes 131104 | tf_op jit(solution)/shard_map/ppermute | solution.py:150
  195.3 4.3 %shard_map.97 = (f32[8,4,8,2,8,128]{5,4,3,2,1,0:T(8,128)}, f32[8,4,8,2,8,128]{5,4,3,2,1,0:T(8,128)}) custom-call(s32[1]{0:T(128)} %bitcast.z_ref.refs_0_, s32[8]{0:T(128)S(1)} %copy-done.25, s32[256]{0:T(256)S(1)} %copy-done.24, s32[8]{0:T(128)S(1)} %copy-done.26, f32[32,8,8,128]{3,2,1,0:T(8,128)S(1)} %all_to_all.20.refs_0_.refs_5_, ...), custom_call_target="tpu_custom_call" | custom-call | flops 10485760 | bytes 10485760 | tf_op jit(solution)/shard_map/pallas_call | solution.py:31
  204.3 2.9 %shard_map.102 = f32[256,2,8,128]{3,2,1,0:T(8,128)} custom-call(s32[1]{0:T(128)} %bitcast.z_ref.refs_0_, f32[32,8,8,128]{3,2,1,0:T(8,128)} %all-to-all-done.2.b_ref, f32[32,8,128]{2,1,0:T(8,128)S(1)} %copy-done.19, f32[32,8,128]{2,1,0:T(8,128)S(1)} %copy-done.21, f32[32,8,128]{2,1,0:T(8,128)S(1)} %copy-done.23, ...), custom_call_target="tpu_custom_call" | custom-call | flops 4194304 | bytes 4194304 | tf_op jit(solution)/shard_map/pallas_call | solution.py:31
  (104 shorter events, 69.4 us)
Async XLA Ops:
  4.4 16.9 %collective-permute-start.1 = (f32[32,8,128]{2,1,0:T(8,128)S(1)}, f32[32,8,128]{2,1,0:T(8,128)S(1)}, u32[]{:S(2)}, u32[]{:S(2)}) collective-permute-start(f32[32,8,128]{2,1,0:T(8,128)S(1)} %get-tuple-element.40), channel_id=1, source_target_pairs={{0,16},{8,24},{16,32},{24,40},{32,48},{40,56},{48,0},{56,8},{1,17}... | collective-permute-start | bytes 393224 | tf_op jit(solution)/shard_map/ppermute | solution.py:150
  7.7 21.8 %collective-permute-start.2 = (f32[32,8,128]{2,1,0:T(8,128)S(1)}, f32[32,8,128]{2,1,0:T(8,128)S(1)}, u32[]{:S(2)}, u32[]{:S(2)}) collective-permute-start(f32[32,8,128]{2,1,0:T(8,128)S(1)} %get-tuple-element.41), channel_id=1, source_target_pairs={{0,24},{8,32},{16,40},{24,48},{32,56},{40,0},{48,8},{56,16},{1,25}... | collective-permute-start | bytes 393224 | tf_op jit(solution)/shard_map/ppermute | solution.py:150
  11.7 17.8 %collective-permute-start.3 = (f32[32,8,128]{2,1,0:T(8,128)S(1)}, f32[32,8,128]{2,1,0:T(8,128)S(1)}, u32[]{:S(2)}, u32[]{:S(2)}) collective-permute-start(f32[32,8,128]{2,1,0:T(8,128)S(1)} %get-tuple-element.42), channel_id=1, source_target_pairs={{0,32},{8,40},{16,48},{24,56},{32,0},{40,8},{48,16},{56,24},{1,33}... | collective-permute-start | bytes 393224 | tf_op jit(solution)/shard_map/ppermute | solution.py:150
  12.3 21.0 %collective-permute-start.4 = (f32[32,8,128]{2,1,0:T(8,128)S(1)}, f32[32,8,128]{2,1,0:T(8,128)S(1)}, u32[]{:S(2)}, u32[]{:S(2)}) collective-permute-start(f32[32,8,128]{2,1,0:T(8,128)S(1)} %get-tuple-element.43), channel_id=1, source_target_pairs={{0,40},{8,48},{16,56},{24,0},{32,8},{40,16},{48,24},{56,32},{1,41}... | collective-permute-start | bytes 393224 | tf_op jit(solution)/shard_map/ppermute | solution.py:150
  17.2 18.4 %collective-permute-start.5 = (f32[32,8,128]{2,1,0:T(8,128)S(1)}, f32[32,8,128]{2,1,0:T(8,128)S(1)}, u32[]{:S(2)}, u32[]{:S(2)}) collective-permute-start(f32[32,8,128]{2,1,0:T(8,128)S(1)} %get-tuple-element.44), channel_id=1, source_target_pairs={{0,48},{8,56},{16,0},{24,8},{32,16},{40,24},{48,32},{56,40},{1,49}... | collective-permute-start | bytes 393224 | tf_op jit(solution)/shard_map/ppermute | solution.py:150
  21.3 15.5 %collective-permute-start.6 = (f32[32,8,128]{2,1,0:T(8,128)S(1)}, f32[32,8,128]{2,1,0:T(8,128)S(1)}, u32[]{:S(2)}, u32[]{:S(2)}) collective-permute-start(f32[32,8,128]{2,1,0:T(8,128)S(1)} %get-tuple-element.45), channel_id=1, source_target_pairs={{0,56},{8,0},{16,8},{24,16},{32,24},{40,32},{48,40},{56,48},{1,57}... | collective-permute-start | bytes 393224 | tf_op jit(solution)/shard_map/ppermute | solution.py:150
  60.0 21.5 %all-to-all-start.1 = ((f32[32,8,8,128]{3,2,1,0:T(8,128)}), f32[32,8,8,128]{3,2,1,0:T(8,128)}, u32[]{:S(2)}, u32[]{:S(2)}) async-start(f32[32,8,8,128]{3,2,1,0:T(8,128)} %copy-done.7), calls=%async_computation.1 | async-start | bytes 2097152 | tf_op jit(solution)/shard_map/all_to_all | solution.py:155
  81.5 77.1 %all-to-all-start.3 = ((f32[32,8,8,128]{3,2,1,0:T(8,128)}), f32[32,8,8,128]{3,2,1,0:T(8,128)}, u32[]{:S(2)}, u32[]{:S(2)}) async-start(f32[32,8,8,128]{3,2,1,0:T(8,128)} %copy-done.4), calls=%async_computation.3 | async-start | bytes 2097152 | tf_op jit(solution)/shard_map/all_to_all | solution.py:155
  91.7 16.9 %collective-permute-start.8 = (f32[32,8,128]{2,1,0:T(8,128)S(1)}, f32[32,8,128]{2,1,0:T(8,128)S(1)}, u32[]{:S(2)}, u32[]{:S(2)}) collective-permute-start(f32[32,8,128]{2,1,0:T(8,128)S(1)} %get-tuple-element.49), channel_id=1, source_target_pairs={{0,16},{8,24},{16,32},{24,40},{32,48},{40,56},{48,0},{56,8},{1,17}... | collective-permute-start | bytes 393224 | tf_op jit(solution)/shard_map/ppermute | solution.py:150
  92.8 15.8 %collective-permute-start.9 = (f32[32,8,128]{2,1,0:T(8,128)S(1)}, f32[32,8,128]{2,1,0:T(8,128)S(1)}, u32[]{:S(2)}, u32[]{:S(2)}) collective-permute-start(f32[32,8,128]{2,1,0:T(8,128)S(1)} %get-tuple-element.50), channel_id=1, source_target_pairs={{0,24},{8,32},{16,40},{24,48},{32,56},{40,0},{48,8},{56,16},{1,25}... | collective-permute-start | bytes 393224 | tf_op jit(solution)/shard_map/ppermute | solution.py:150
  93.4 20.1 %collective-permute-start.10 = (f32[32,8,128]{2,1,0:T(8,128)S(1)}, f32[32,8,128]{2,1,0:T(8,128)S(1)}, u32[]{:S(2)}, u32[]{:S(2)}) collective-permute-start(f32[32,8,128]{2,1,0:T(8,128)S(1)} %get-tuple-element.51), channel_id=1, source_target_pairs={{0,32},{8,40},{16,48},{24,56},{32,0},{40,8},{48,16},{56,24},{1,33}... | collective-permute-start | bytes 393224 | tf_op jit(solution)/shard_map/ppermute | solution.py:150
  98.1 15.8 %collective-permute-start.11 = (f32[32,8,128]{2,1,0:T(8,128)S(1)}, f32[32,8,128]{2,1,0:T(8,128)S(1)}, u32[]{:S(2)}, u32[]{:S(2)}) collective-permute-start(f32[32,8,128]{2,1,0:T(8,128)S(1)} %get-tuple-element.52), channel_id=1, source_target_pairs={{0,40},{8,48},{16,56},{24,0},{32,8},{40,16},{48,24},{56,32},{1,41}... | collective-permute-start | bytes 393224 | tf_op jit(solution)/shard_map/ppermute | solution.py:150
  100.1 19.1 %collective-permute-start.12 = (f32[32,8,128]{2,1,0:T(8,128)S(1)}, f32[32,8,128]{2,1,0:T(8,128)S(1)}, u32[]{:S(2)}, u32[]{:S(2)}) collective-permute-start(f32[32,8,128]{2,1,0:T(8,128)S(1)} %get-tuple-element.53), channel_id=1, source_target_pairs={{0,48},{8,56},{16,0},{24,8},{32,16},{40,24},{48,32},{56,40},{1,49}... | collective-permute-start | bytes 393224 | tf_op jit(solution)/shard_map/ppermute | solution.py:150
  128.3 19.7 %collective-permute-start.16 = (f32[32,8,128]{2,1,0:T(8,128)S(1)}, f32[32,8,128]{2,1,0:T(8,128)S(1)}, u32[]{:S(2)}, u32[]{:S(2)}) collective-permute-start(f32[32,8,128]{2,1,0:T(8,128)S(1)} %get-tuple-element.60), channel_id=1, source_target_pairs={{0,24},{8,32},{16,40},{24,48},{32,56},{40,0},{48,8},{56,16},{1,25}... | collective-permute-start | bytes 393224 | tf_op jit(solution)/shard_map/ppermute | solution.py:150
  131.2 19.8 %collective-permute-start.17 = (f32[32,8,128]{2,1,0:T(8,128)S(1)}, f32[32,8,128]{2,1,0:T(8,128)S(1)}, u32[]{:S(2)}, u32[]{:S(2)}) collective-permute-start(f32[32,8,128]{2,1,0:T(8,128)S(1)} %get-tuple-element.61), channel_id=1, source_target_pairs={{0,32},{8,40},{16,48},{24,56},{32,0},{40,8},{48,16},{56,24},{1,33}... | collective-permute-start | bytes 393224 | tf_op jit(solution)/shard_map/ppermute | solution.py:150
  132.6 19.9 %collective-permute-start.18 = (f32[32,8,128]{2,1,0:T(8,128)S(1)}, f32[32,8,128]{2,1,0:T(8,128)S(1)}, u32[]{:S(2)}, u32[]{:S(2)}) collective-permute-start(f32[32,8,128]{2,1,0:T(8,128)S(1)} %get-tuple-element.62), channel_id=1, source_target_pairs={{0,40},{8,48},{16,56},{24,0},{32,8},{40,16},{48,24},{56,32},{1,41}... | collective-permute-start | bytes 393224 | tf_op jit(solution)/shard_map/ppermute | solution.py:150
  136.8 19.3 %collective-permute-start.19 = (f32[32,8,128]{2,1,0:T(8,128)S(1)}, f32[32,8,128]{2,1,0:T(8,128)S(1)}, u32[]{:S(2)}, u32[]{:S(2)}) collective-permute-start(f32[32,8,128]{2,1,0:T(8,128)S(1)} %get-tuple-element.63), channel_id=1, source_target_pairs={{0,48},{8,56},{16,0},{24,8},{32,16},{40,24},{48,32},{56,40},{1,49}... | collective-permute-start | bytes 393224 | tf_op jit(solution)/shard_map/ppermute | solution.py:150
  140.8 16.7 %collective-permute-start.20 = (f32[32,8,128]{2,1,0:T(8,128)S(1)}, f32[32,8,128]{2,1,0:T(8,128)S(1)}, u32[]{:S(2)}, u32[]{:S(2)}) collective-permute-start(f32[32,8,128]{2,1,0:T(8,128)S(1)} %get-tuple-element.64), channel_id=1, source_target_pairs={{0,56},{8,0},{16,8},{24,16},{32,24},{40,32},{48,40},{56,48},{1,57}... | collective-permute-start | bytes 393224 | tf_op jit(solution)/shard_map/ppermute | solution.py:150
  158.6 41.0 %all-to-all-start.2 = ((f32[32,8,8,128]{3,2,1,0:T(8,128)}), f32[32,8,8,128]{3,2,1,0:T(8,128)}, u32[]{:S(2)}, u32[]{:S(2)}) async-start(f32[32,8,8,128]{3,2,1,0:T(8,128)} %copy-done.5), calls=%async_computation.2 | async-start | bytes 2097152 | tf_op jit(solution)/shard_map/all_to_all | solution.py:155
  171.2 17.3 %collective-permute-start.22 = (f32[32,8,128]{2,1,0:T(8,128)S(1)}, f32[32,8,128]{2,1,0:T(8,128)S(1)}, u32[]{:S(2)}, u32[]{:S(2)}) collective-permute-start(f32[32,8,128]{2,1,0:T(8,128)S(1)} %get-tuple-element.67), channel_id=1, source_target_pairs={{0,16},{8,24},{16,32},{24,40},{32,48},{40,56},{48,0},{56,8},{1,17}... | collective-permute-start | bytes 393224 | tf_op jit(solution)/shard_map/ppermute | solution.py:150
  172.4 27.2 %collective-permute-start.23 = (f32[32,8,128]{2,1,0:T(8,128)}, f32[32,8,128]{2,1,0:T(8,128)}, u32[]{:S(2)}, u32[]{:S(2)}) collective-permute-start(f32[32,8,128]{2,1,0:T(8,128)} %get-tuple-element.68), channel_id=1, source_target_pairs={{0,24},{8,32},{16,40},{24,48},{32,56},{40,0},{48,8},{56,16},{1,25}... | collective-permute-start | bytes 393224 | tf_op jit(solution)/shard_map/ppermute | solution.py:150
  173.4 26.2 %collective-permute-start.24 = (f32[32,8,128]{2,1,0:T(8,128)}, f32[32,8,128]{2,1,0:T(8,128)}, u32[]{:S(2)}, u32[]{:S(2)}) collective-permute-start(f32[32,8,128]{2,1,0:T(8,128)} %get-tuple-element.69), channel_id=1, source_target_pairs={{0,32},{8,40},{16,48},{24,56},{32,0},{40,8},{48,16},{56,24},{1,33}... | collective-permute-start | bytes 393224 | tf_op jit(solution)/shard_map/ppermute | solution.py:150
  177.7 21.9 %collective-permute-start.25 = (f32[32,8,128]{2,1,0:T(8,128)}, f32[32,8,128]{2,1,0:T(8,128)}, u32[]{:S(2)}, u32[]{:S(2)}) collective-permute-start(f32[32,8,128]{2,1,0:T(8,128)} %get-tuple-element.70), channel_id=1, source_target_pairs={{0,40},{8,48},{16,56},{24,0},{32,8},{40,16},{48,24},{56,32},{1,41}... | collective-permute-start | bytes 393224 | tf_op jit(solution)/shard_map/ppermute | solution.py:150
  181.0 18.6 %collective-permute-start.26 = (f32[32,8,128]{2,1,0:T(8,128)}, f32[32,8,128]{2,1,0:T(8,128)}, u32[]{:S(2)}, u32[]{:S(2)}) collective-permute-start(f32[32,8,128]{2,1,0:T(8,128)} %get-tuple-element.71), channel_id=1, source_target_pairs={{0,48},{8,56},{16,0},{24,8},{32,16},{40,24},{48,32},{56,40},{1,49}... | collective-permute-start | bytes 393224 | tf_op jit(solution)/shard_map/ppermute | solution.py:150
  (35 other events, 358.0 us)

commit v2 on v0

v2 whole, which is shorter than its diff:
```python
import math

import jax
import jax.numpy as jnp
from jax import lax
from jax.experimental import pallas as pl
from jax.experimental.pallas import tpu as pltpu
from jax.sharding import Mesh
from jax.sharding import PartitionSpec as P

XZ = ("x", "zh", "zl")
YC = ("y", "c")
NY, NC = 4, 2
NYC = NY * NC
SHIFTS = (4, 5, 2, 6, 3, 7, 1)
TILE = (8, 128)
F32 = jnp.float32
MIB = 1 << 20


def tiles(value):
    lead, rows, cols = value.shape[:-2], value.shape[-2], value.shape[-1]
    value = value.reshape(*lead, rows // 8, 8, cols // 128, 128)
    return jnp.swapaxes(value, -3, -2)


def call(body, ins, outs, scalars, limit=16 * MIB):
    smem = pl.BlockSpec(memory_space=pltpu.SMEM)
    vmem = pl.BlockSpec(memory_space=pltpu.VMEM)
    moved = 4 * (sum(a.size for a in ins[scalars:]) + sum(math.prod(s) for s in outs))
    return pl.pallas_call(
        body,
        out_shape=[jax.ShapeDtypeStruct(s, F32) for s in outs],
        in_specs=[smem] * scalars + [vmem] * (len(ins) - scalars),
        out_specs=[vmem] * len(outs),
        cost_estimate=pl.CostEstimate(flops=moved, bytes_accessed=moved, transcendentals=0),
        compiler_params=pltpu.CompilerParams(vmem_limit_bytes=limit),
    )(*ins)


def ahead(me, d):
    return ((((me >> 1) + d // NC) & (NY - 1)) << 1) | ((me & 1) ^ (d % NC))


def behind(me, d):
    return ((((me >> 1) + NY - d // NC) & (NY - 1)) << 1) | ((me & 1) ^ (d % NC))


def base_kernel(me_ref, m_ref, v_ref, *outs):
    for d in range(NYC):
        at = ahead(me_ref[0], d)
        outs[d][...] = m_ref[:, :, at] - (0.7 * 0.81) * v_ref[:, :, at]


def mix_kernel(me_ref, old_ref, new_ref, pm_ref, steps_ref, r_ref, *refs):
    me = me_ref[0]
    bases, averages, out = refs[:NYC], refs[NYC : 2 * NYC], refs[2 * NYC]
    islands = steps_ref.shape[0]
    old = [pm_ref[old_ref[j]] for j in range(islands)]
    new = [pm_ref[new_ref[j]] for j in range(islands)]
    weights = []
    for j in range(islands):
        total = jnp.int32(0)
        for i in range(islands):
            total += jnp.where(old[i] == old[j], steps_ref[i], 0)
        splat = lambda s: jnp.full(TILE, s, jnp.int32).astype(F32)
        weights.append(splat(steps_ref[j]) / splat(jnp.maximum(total, 1)))
    for d in range(NYC):
        rows = ahead(me, d)
        e = ((NY - d // NC) % NY) * NC + d % NC
        averages[d][...] = jnp.zeros(averages[d].shape, F32)
        for j in range(islands):
            averages[d][old[j]] += weights[j] * r_ref[j, :, rows]
        for j in range(islands):
            out[j, :, rows] = bases[e][new[j]] - (0.7 * 1.9) * averages[d][new[j]]


def owner_kernel(me_ref, m_ref, v_ref, *refs):
    averages, (nm_ref, nv_ref) = refs[:NYC], refs[NYC:]
    for d in range(NYC):
        at = behind(me_ref[0], d)
        avg = averages[d][...]
        mom = 0.9 * v_ref[:, :, at] + avg
        nv_ref[:, :, at] = mom
        nm_ref[:, :, at] = m_ref[:, :, at] - 0.7 * (avg + 0.9 * mom)


def along_yc(pieces):
    got = [pieces[0]] + [None] * (NYC - 1)
    for d in SHIFTS:
        got[d] = lax.ppermute(pieces[d], YC, [(i, ahead(i, d)) for i in range(NYC)])
    return got


def across_xz(value):
    return lax.all_to_all(value, XZ, split_axis=0, concat_axis=0, tiled=True)


def shards(master, momentum, deltas, old_path, new_path, path_module, island_steps):
    modules = master.shape[0]
    me = lax.axis_index(YC).astype(jnp.int32).reshape(1)
    owner = (modules, 4, NYC, 2, *TILE)
    piece = (modules, 4, 2, *TILE)
    m = tiles(master).reshape(owner)
    v = tiles(momentum).reshape(owner)

    got = across_xz(deltas[0].reshape(32, 64, 256))
    base = along_yc(call(base_kernel, [me, m, v], [piece] * NYC, 1))
    isles = (8, 4, NYC, 2, *TILE)
    *avg, out = call(
        mix_kernel,
        [me, old_path, new_path, path_module, island_steps, tiles(got).reshape(isles), *base],
        [piece] * NYC + [isles],
        5,
    )
    out = jnp.swapaxes(out.reshape(32, NYC, 2, *TILE), 2, 3).reshape(32, 64, 256)
    new_module = across_xz(out).reshape(deltas.shape)
    nm, nv = call(owner_kernel, [me, m, v, *along_yc(avg)], [owner] * 2, 1)

    def whole(value):
        return jnp.swapaxes(value.reshape(modules, 64, *TILE), 1, 2).reshape(master.shape)

    return whole(nm), whole(nv), new_module


def solution(mesh):
    fine = Mesh(mesh.devices.reshape(4, 2, 4, 4, 2), ("x", "zh", "zl", "y", "c"))
    owners = P(None, ("x", "zh", "zl", "y", "c"), None)
    island = P(("x", "zh"), None, ("zl", "y", "c"))
    return jax.shard_map(
        shards,
        mesh=fine,
        in_specs=(owners, owners, island, P(), P(), P(), P()),
        out_specs=(owners, owners, island),
        check_vma=False,
    )
```

time: 146 us -> 134 us (0.918)
  waiting for transfers between devices: 102 us -> 76.1 us
  starting transfers between devices: 20.7 us -> 32.7 us
  local copies, waits for them, and re-layouts: 12.3 us -> 19.1 us
  matrix products: 5.66 us -> 0 us
  Pallas kernels: 0 us -> 5.24 us
  other arithmetic: 3.38 us -> 0 us
    all_to_all x2, waiting for transfers between devices: 102 us -> 33.5 us  [across_xz(): return lax.all_to_all(value, XZ, split_axis=0, concat_axis=0, tiled=True)]
    ppermute x0 -> x14, waiting for transfers between devices: none -> 42.5 us  [along_yc(): got[d] = lax.ppermute(pieces[d], YC, [(i, ahead(i, d)) for i in range(NYC)])]
    ppermute x0 -> x14, starting transfers between devices: none -> 14.7 us  [along_yc(): got[d] = lax.ppermute(pieces[d], YC, [(i, ahead(i, d)) for i in range(NYC)])]
    unnamed x17 -> x55, local copies, waits for them, and re-layouts: 7.7 us -> 19.1 us
    dot_general x1 -> x0, matrix products: 5.66 us -> none  [shards(): jnp.einsum('kj,jrc->krc', mixing, received, precision=lax.Precision.HIGHEST)]
    pallas_call x0 -> x3, Pallas kernels: none -> 5.24 us  [call(): pl.pallas_call(body, out_shape=[jax.ShapeDtypeStruct(s, F32) for s in out...]
    gather x3 -> x0, local copies, waits for them, and re-layouts: 3.38 us -> none  [the longest x1 2.09 us: shards(): picked = jnp.take(new_master, new_index, axis=0)]
    select_n x4 -> x0, other arithmetic: 3.23 us -> none  [the longest x2 3.23 us: shards(): picked = jnp.take(new_master, new_index, axis=0)]
  transfers between devices with their start and end apart: 2 -> 16, of which waited for: 2 -> 12; matrix products, arithmetic and copies ran while one was open for 4% -> 0% of each run, Pallas kernels for 0% -> 2%
where the time goes in v2:
time: 134 us
  waiting for transfers between devices  76.1 us (57%)
  starting transfers between devices  32.7 us (24%)
  local copies, waits for them, and re-layouts  19.1 us (14%)
  Pallas kernels  5.24 us (4%)
    ppermute x14, waiting for transfers between devices, along_yc(): got[d] = lax.ppermute(pieces[d], YC, [(i, ahead(i, d)) for i in range(NYC)])  42.5 us
    all_to_all x2, waiting for transfers between devices, across_xz(): return lax.all_to_all(value, XZ, split_axis=0, concat_axis=0, tiled=True)  33.5 us
    unnamed x55, local copies, waits for them, and re-layouts  19.1 us
    all_to_all x2, starting transfers between devices, across_xz(): return lax.all_to_all(value, XZ, split_axis=0, concat_axis=0, tiled=True)  18 us
    ppermute x14, starting transfers between devices, along_yc(): got[d] = lax.ppermute(pieces[d], YC, [(i, ahead(i, d)) for i in range(NYC)])  14.7 us
    pallas_call x3, Pallas kernels, call(): pl.pallas_call(body, out_shape=[jax.ShapeDtypeStruct(s, F32) for s in out...  5.24 us
  transfers between devices with their start and end apart: 16, of which 12 were waited for; matrix products, arithmetic and copies ran while one was open for 0% of the time, Pallas kernels for 2%

profile of v2, /device:TPU:8, one launch (start us, length us, event | category | flops | bytes accessed | tf_op | source)
XLA Modules:
  0.0 133.9 jit_solution(3088788610049862687)
XLA Ops:
  0.6 11.6 %all-to-all-start = ((f32[32,64,256]{2,1,0:T(8,128)}), f32[32,64,256]{2,1,0:T(8,128)}, u32[]{:S(2)}, u32[]{:S(2)}) async-start(f32[32,64,256]{2,1,0:T(8,128)} %bitcast.38), calls=%async_computation | async-start | bytes 4194304 | tf_op jit(solution)/shard_map/all_to_all | solution.py:96
  12.3 1.6 %copy-done.1 = f32[8,8,8192]{2,1,0:T(8,128)S(1)} copy-done((f32[8,8,8192]{2,1,0:T(8,128)S(1)}, f32[8,8,8192]{2,1,0:T(8,128)}, u32[]{:S(2)}) %copy-start.1) | copy-done | bytes 2097176
  14.3 1.7 %collective-permute-start.1 = (f32[8,4,2,8,128]{4,3,2,1,0:T(8,128)S(1)}, f32[8,4,2,8,128]{4,3,2,1,0:T(8,128)S(1)}, u32[]{:S(2)}, u32[]{:S(2)}) collective-permute-start(f32[8,4,2,8,128]{4,3,2,1,0:T(8,128)S(1)} %get-tuple-element.24), channel_id=1, source_target_pairs={{0,2},{1,3},{2,4},{3,5},{4,6},{5,7},{6,0},{7,1},{8,10},{9,11},{10,... | collective-permute-start | bytes 786440 | tf_op jit(solution)/shard_map/ppermute | solution.py:91
  18.2 2.0 %collective-permute-start.4 = (f32[8,4,2,8,128]{4,3,2,1,0:T(8,128)S(1)}, f32[8,4,2,8,128]{4,3,2,1,0:T(8,128)S(1)}, u32[]{:S(2)}, u32[]{:S(2)}) collective-permute-start(f32[8,4,2,8,128]{4,3,2,1,0:T(8,128)S(1)} %get-tuple-element.27), channel_id=1, source_target_pairs={{0,5},{1,4},{2,7},{3,6},{4,1},{5,0},{6,3},{7,2},{8,13},{9,12},{10,... | collective-permute-start | bytes 786440 | tf_op jit(solution)/shard_map/ppermute | solution.py:91
  20.9 2.5 %collective-permute-done.1.refs_2_ = f32[8,4,2,8,128]{4,3,2,1,0:T(8,128)S(1)} collective-permute-done((f32[8,4,2,8,128]{4,3,2,1,0:T(8,128)S(1)}, f32[8,4,2,8,128]{4,3,2,1,0:T(8,128)S(1)}, u32[]{:S(2)}, u32[]{:S(2)}) %collective-permute-start.1) | collective-permute-done | bytes 262176 | tf_op jit(solution)/shard_map/ppermute | solution.py:91
  24.1 4.0 %collective-permute-done.2.refs_3_ = f32[8,4,2,8,128]{4,3,2,1,0:T(8,128)S(1)} collective-permute-done((f32[8,4,2,8,128]{4,3,2,1,0:T(8,128)S(1)}, f32[8,4,2,8,128]{4,3,2,1,0:T(8,128)S(1)}, u32[]{:S(2)}, u32[]{:S(2)}) %collective-permute-start.2) | collective-permute-done | bytes 262176 | tf_op jit(solution)/shard_map/ppermute | solution.py:91
  28.8 3.3 %collective-permute-done.4.refs_5_ = f32[8,4,2,8,128]{4,3,2,1,0:T(8,128)S(1)} collective-permute-done((f32[8,4,2,8,128]{4,3,2,1,0:T(8,128)S(1)}, f32[8,4,2,8,128]{4,3,2,1,0:T(8,128)S(1)}, u32[]{:S(2)}, u32[]{:S(2)}) %collective-permute-start.4) | collective-permute-done | bytes 262176 | tf_op jit(solution)/shard_map/ppermute | solution.py:91
  32.9 5.4 %collective-permute-done.5.refs_6_ = f32[8,4,2,8,128]{4,3,2,1,0:T(8,128)S(1)} collective-permute-done((f32[8,4,2,8,128]{4,3,2,1,0:T(8,128)S(1)}, f32[8,4,2,8,128]{4,3,2,1,0:T(8,128)S(1)}, u32[]{:S(2)}, u32[]{:S(2)}) %collective-permute-start.5) | collective-permute-done | bytes 262176 | tf_op jit(solution)/shard_map/ppermute | solution.py:91
  39.0 4.8 %collective-permute-done.6.refs_7_ = f32[8,4,2,8,128]{4,3,2,1,0:T(8,128)S(1)} collective-permute-done((f32[8,4,2,8,128]{4,3,2,1,0:T(8,128)S(1)}, f32[8,4,2,8,128]{4,3,2,1,0:T(8,128)S(1)}, u32[]{:S(2)}, u32[]{:S(2)}) %collective-permute-start.6) | collective-permute-done | bytes 262176 | tf_op jit(solution)/shard_map/ppermute | solution.py:91
  44.6 17.7 %all-to-all-done = f32[32,64,256]{2,1,0:T(8,128)} async-done(((f32[32,64,256]{2,1,0:T(8,128)}), f32[32,64,256]{2,1,0:T(8,128)}, u32[]{:S(2)}, u32[]{:S(2)}) %all-to-all-start) | async-done | bytes 2097184 | tf_op jit(solution)/shard_map/all_to_all | solution.py:96
  66.1 2.3 %shard_map.95 = (f32[8,4,2,8,128]{4,3,2,1,0:T(8,128)S(1)}, f32[8,4,2,8,128]{4,3,2,1,0:T(8,128)S(1)}, f32[8,4,2,8,128]{4,3,2,1,0:T(8,128)S(1)}, f32[8,4,2,8,128]{...) custom-call(s32[1]{0:T(128)} %bitcast.me_ref, ...), custom_call_target="tpu_custom_call" | custom-call | flops 8388608 | bytes 8388608 | tf_op jit(solution)/shard_map/pallas_call | solution.py:31
  68.4 1.3 copy-done.3
  74.7 6.4 %all-to-all-start.1 = ((f32[32,64,256]{2,1,0:T(8,128)}), f32[32,64,256]{2,1,0:T(8,128)}, u32[]{:S(2)}, u32[]{:S(2)}) async-start(f32[32,64,256]{2,1,0:T(8,128)} %bitcast.37), calls=%async_computation.1 | async-start | bytes 4194304 | tf_op jit(solution)/shard_map/all_to_all | solution.py:96
  81.2 1.7 %collective-permute-start.8 = (f32[8,4,2,8,128]{4,3,2,1,0:T(8,128)}, f32[8,4,2,8,128]{4,3,2,1,0:T(8,128)S(1)}, u32[]{:S(2)}, u32[]{:S(2)}) collective-permute-start(f32[8,4,2,8,128]{4,3,2,1,0:T(8,128)} %copy-done.25), channel_id=1, source_target_pairs={{0,2},{1,3},{2,4},{3,5},{4,6},{5,7},{6,0},{7,1},{8,10},{9,11},{10,... | collective-permute-start | bytes 786440 | tf_op jit(solution)/shard_map/ppermute | solution.py:91
  85.2 2.0 %collective-permute-start.11 = (f32[8,4,2,8,128]{4,3,2,1,0:T(8,128)S(1)}, f32[8,4,2,8,128]{4,3,2,1,0:T(8,128)S(1)}, u32[]{:S(2)}, u32[]{:S(2)}) collective-permute-start(f32[8,4,2,8,128]{4,3,2,1,0:T(8,128)S(1)} %copy-done.21), channel_id=1, source_target_pairs={{0,5},{1,4},{2,7},{3,6},{4,1},{5,0},{6,3},{7,2},{8,13},{9,12},{10,... | collective-permute-start | bytes 786440 | tf_op jit(solution)/shard_map/ppermute | solution.py:91
  87.9 2.7 %collective-permute-done.8.refs_2_ = f32[8,4,2,8,128]{4,3,2,1,0:T(8,128)S(1)} collective-permute-done((f32[8,4,2,8,128]{4,3,2,1,0:T(8,128)}, f32[8,4,2,8,128]{4,3,2,1,0:T(8,128)S(1)}, u32[]{:S(2)}, u32[]{:S(2)}) %collective-permute-start.8) | collective-permute-done | bytes 262176 | tf_op jit(solution)/shard_map/ppermute | solution.py:91
  91.1 4.2 %collective-permute-done.9.refs_3_ = f32[8,4,2,8,128]{4,3,2,1,0:T(8,128)S(1)} collective-permute-done((f32[8,4,2,8,128]{4,3,2,1,0:T(8,128)}, f32[8,4,2,8,128]{4,3,2,1,0:T(8,128)S(1)}, u32[]{:S(2)}, u32[]{:S(2)}) %collective-permute-start.9) | collective-permute-done | bytes 262176 | tf_op jit(solution)/shard_map/ppermute | solution.py:91
  95.4 3.7 %collective-permute-done.11.refs_5_ = f32[8,4,2,8,128]{4,3,2,1,0:T(8,128)S(1)} collective-permute-done((f32[8,4,2,8,128]{4,3,2,1,0:T(8,128)S(1)}, f32[8,4,2,8,128]{4,3,2,1,0:T(8,128)S(1)}, u32[]{:S(2)}, u32[]{:S(2)}) %collective-permute-start.11) | collective-permute-done | bytes 262176 | tf_op jit(solution)/shard_map/ppermute | solution.py:91
  99.1 6.1 %collective-permute-done.12.refs_6_ = f32[8,4,2,8,128]{4,3,2,1,0:T(8,128)S(1)} collective-permute-done((f32[8,4,2,8,128]{4,3,2,1,0:T(8,128)S(1)}, f32[8,4,2,8,128]{4,3,2,1,0:T(8,128)S(1)}, u32[]{:S(2)}, u32[]{:S(2)}) %collective-permute-start.12) | collective-permute-done | bytes 262176 | tf_op jit(solution)/shard_map/ppermute | solution.py:91
  105.3 5.5 %collective-permute-done.13.refs_7_ = f32[8,4,2,8,128]{4,3,2,1,0:T(8,128)S(1)} collective-permute-done((f32[8,4,2,8,128]{4,3,2,1,0:T(8,128)S(1)}, f32[8,4,2,8,128]{4,3,2,1,0:T(8,128)S(1)}, u32[]{:S(2)}, u32[]{:S(2)}) %collective-permute-start.13) | collective-permute-done | bytes 262176 | tf_op jit(solution)/shard_map/ppermute | solution.py:91
  110.8 1.6 %copy-done.2 = f32[8,8,8192]{2,1,0:T(8,128)S(1)} copy-done((f32[8,8,8192]{2,1,0:T(8,128)S(1)}, f32[8,8,8192]{2,1,0:T(8,128)}, u32[]{:S(2)}) %copy-start.2) | copy-done | bytes 2097176
  112.4 2.6 %shard_map.96 = (f32[8,4,8,2,8,128]{5,4,3,2,1,0:T(8,128)}, f32[8,4,8,2,8,128]{5,4,3,2,1,0:T(8,128)}) custom-call(s32[1]{0:T(128)} %bitcast.me_ref, f32[8,4,8,2,8,128]{5,4,3,2,1,0:T(8,128)S(1)} %bitcast.34, f32[8,4,8,2,8,128]{5,4,3,2,1,0:T(8,128)S(1)} %bitcast.36, f32[8,4,2,8,128]{4,3,2,1,0:T(8,128)S(1)} %get-tuple-element.30.refs_0_, ...), custom_call_target="tpu_custom_call" | custom-call | flops 10485760 | bytes 10485760 | tf_op jit(solution)/shard_map/pallas_call | solution.py:31
  115.0 15.8 %all-to-all-done.1 = f32[32,64,256]{2,1,0:T(8,128)} async-done(((f32[32,64,256]{2,1,0:T(8,128)}), f32[32,64,256]{2,1,0:T(8,128)}, u32[]{:S(2)}, u32[]{:S(2)}) %all-to-all-start.1) | async-done | bytes 2097184 | tf_op jit(solution)/shard_map/all_to_all | solution.py:96
  130.8 3.0 %copy.11 = f32[1,2048,256]{2,1,0:T(8,128)} copy(f32[1,2048,256]{2,1,0:T(8,128)} %bitcast.24) | data formatting | bytes 4194304
  (66 shorter events, 19.4 us)
Async XLA Ops:
  0.6 11.6 %copy-start = (f32[8,8,8192]{2,1,0:T(8,128)S(1)}, f32[8,8,8192]{2,1,0:T(8,128)}, u32[]{:S(2)}) copy-start(f32[8,8,8192]{2,1,0:T(8,128)} %param.7) | copy-start | bytes 6291460
  0.6 61.6 %all-to-all-start = ((f32[32,64,256]{2,1,0:T(8,128)}), f32[32,64,256]{2,1,0:T(8,128)}, u32[]{:S(2)}, u32[]{:S(2)}) async-start(f32[32,64,256]{2,1,0:T(8,128)} %bitcast.38), calls=%async_computation | async-start | bytes 4194304 | tf_op jit(solution)/shard_map/all_to_all | solution.py:96
  13.8 48.4 %copy-start.12 = (s32[256]{0:T(256)S(1)}, s32[256]{0:T(256)}, u32[]{:S(2)}) copy-start(s32[256]{0:T(256)} %pm_ref.1) | copy-start | bytes 3076
  13.9 48.4 %copy-start.13 = (s32[8]{0:T(128)S(1)}, s32[8]{0:T(128)}, u32[]{:S(2)}) copy-start(s32[8]{0:T(128)} %old_ref.1) | copy-start | bytes 100
  13.9 48.4 %copy-start.14 = (s32[8]{0:T(128)S(1)}, s32[8]{0:T(128)}, u32[]{:S(2)}) copy-start(s32[8]{0:T(128)} %new_ref.1) | copy-start | bytes 100
  13.9 48.4 %copy-start.15 = (s32[8]{0:T(128)S(1)}, s32[8]{0:T(128)}, u32[]{:S(2)}) copy-start(s32[8]{0:T(128)} %steps_ref.1) | copy-start | bytes 100
  14.2 6.0 %collective-permute-start = (f32[8,4,2,8,128]{4,3,2,1,0:T(8,128)S(1)}, f32[8,4,2,8,128]{4,3,2,1,0:T(8,128)S(1)}, u32[]{:S(2)}, u32[]{:S(2)}) collective-permute-start(f32[8,4,2,8,128]{4,3,2,1,0:T(8,128)S(1)} %get-tuple-element.23), channel_id=1, source_target_pairs={{0,1},{1,0},{2,3},{3,2},{4,5},{5,4},{6,7},{7,6},{8,9},{9,8},{10,11... | collective-permute-start | bytes 786440 | tf_op jit(solution)/shard_map/ppermute | solution.py:91
  14.3 9.2 %collective-permute-start.1 = (f32[8,4,2,8,128]{4,3,2,1,0:T(8,128)S(1)}, f32[8,4,2,8,128]{4,3,2,1,0:T(8,128)S(1)}, u32[]{:S(2)}, u32[]{:S(2)}) collective-permute-start(f32[8,4,2,8,128]{4,3,2,1,0:T(8,128)S(1)} %get-tuple-element.24), channel_id=1, source_target_pairs={{0,2},{1,3},{2,4},{3,5},{4,6},{5,7},{6,0},{7,1},{8,10},{9,11},{10,... | collective-permute-start | bytes 786440 | tf_op jit(solution)/shard_map/ppermute | solution.py:91
  15.9 12.2 %collective-permute-start.2 = (f32[8,4,2,8,128]{4,3,2,1,0:T(8,128)S(1)}, f32[8,4,2,8,128]{4,3,2,1,0:T(8,128)S(1)}, u32[]{:S(2)}, u32[]{:S(2)}) collective-permute-start(f32[8,4,2,8,128]{4,3,2,1,0:T(8,128)S(1)} %get-tuple-element.25), channel_id=1, source_target_pairs={{0,3},{1,2},{2,5},{3,4},{4,7},{5,6},{6,1},{7,0},{8,11},{9,10},{10,... | collective-permute-start | bytes 786440 | tf_op jit(solution)/shard_map/ppermute | solution.py:91
  17.0 11.2 %collective-permute-start.3 = (f32[8,4,2,8,128]{4,3,2,1,0:T(8,128)S(1)}, f32[8,4,2,8,128]{4,3,2,1,0:T(8,128)S(1)}, u32[]{:S(2)}, u32[]{:S(2)}) collective-permute-start(f32[8,4,2,8,128]{4,3,2,1,0:T(8,128)S(1)} %get-tuple-element.26), channel_id=1, source_target_pairs={{0,4},{1,5},{2,6},{3,7},{4,0},{5,1},{6,2},{7,3},{8,12},{9,13},{10,... | collective-permute-start | bytes 786440 | tf_op jit(solution)/shard_map/ppermute | solution.py:91
  18.2 14.0 %collective-permute-start.4 = (f32[8,4,2,8,128]{4,3,2,1,0:T(8,128)S(1)}, f32[8,4,2,8,128]{4,3,2,1,0:T(8,128)S(1)}, u32[]{:S(2)}, u32[]{:S(2)}) collective-permute-start(f32[8,4,2,8,128]{4,3,2,1,0:T(8,128)S(1)} %get-tuple-element.27), channel_id=1, source_target_pairs={{0,5},{1,4},{2,7},{3,6},{4,1},{5,0},{6,3},{7,2},{8,13},{9,12},{10,... | collective-permute-start | bytes 786440 | tf_op jit(solution)/shard_map/ppermute | solution.py:91
  20.2 18.1 %collective-permute-start.5 = (f32[8,4,2,8,128]{4,3,2,1,0:T(8,128)S(1)}, f32[8,4,2,8,128]{4,3,2,1,0:T(8,128)S(1)}, u32[]{:S(2)}, u32[]{:S(2)}) collective-permute-start(f32[8,4,2,8,128]{4,3,2,1,0:T(8,128)S(1)} %get-tuple-element.28), channel_id=1, source_target_pairs={{0,6},{1,7},{2,0},{3,1},{4,2},{5,3},{6,4},{7,5},{8,14},{9,15},{10,... | collective-permute-start | bytes 786440 | tf_op jit(solution)/shard_map/ppermute | solution.py:91
  23.5 20.4 %collective-permute-start.6 = (f32[8,4,2,8,128]{4,3,2,1,0:T(8,128)S(1)}, f32[8,4,2,8,128]{4,3,2,1,0:T(8,128)S(1)}, u32[]{:S(2)}, u32[]{:S(2)}) collective-permute-start(f32[8,4,2,8,128]{4,3,2,1,0:T(8,128)S(1)} %get-tuple-element.29), channel_id=1, source_target_pairs={{0,7},{1,6},{2,1},{3,0},{4,3},{5,2},{6,5},{7,4},{8,15},{9,14},{10,... | collective-permute-start | bytes 786440 | tf_op jit(solution)/shard_map/ppermute | solution.py:91
  74.7 10.5 %copy-start.21 = (f32[8,4,2,8,128]{4,3,2,1,0:T(8,128)S(1)}, f32[8,4,2,8,128]{4,3,2,1,0:T(8,128)}, u32[]{:S(2)}) copy-start(f32[8,4,2,8,128]{4,3,2,1,0:T(8,128)} %copy-done.20) | copy-start | bytes 786436
  74.7 12.4 %copy-start.19 = (f32[8,4,2,8,128]{4,3,2,1,0:T(8,128)S(1)}, f32[8,4,2,8,128]{4,3,2,1,0:T(8,128)}, u32[]{:S(2)}) copy-start(f32[8,4,2,8,128]{4,3,2,1,0:T(8,128)} %copy-done.18) | copy-start | bytes 786436
  74.7 15.9 %copy-start.17 = (f32[8,4,2,8,128]{4,3,2,1,0:T(8,128)S(1)}, f32[8,4,2,8,128]{4,3,2,1,0:T(8,128)}, u32[]{:S(2)}) copy-start(f32[8,4,2,8,128]{4,3,2,1,0:T(8,128)} %copy-done.16) | copy-start | bytes 786436
  74.7 56.2 %all-to-all-start.1 = ((f32[32,64,256]{2,1,0:T(8,128)}), f32[32,64,256]{2,1,0:T(8,128)}, u32[]{:S(2)}, u32[]{:S(2)}) async-start(f32[32,64,256]{2,1,0:T(8,128)} %bitcast.37), calls=%async_computation.1 | async-start | bytes 4194304 | tf_op jit(solution)/shard_map/all_to_all | solution.py:96
  81.1 6.0 %collective-permute-start.7 = (f32[8,4,2,8,128]{4,3,2,1,0:T(8,128)}, f32[8,4,2,8,128]{4,3,2,1,0:T(8,128)S(1)}, u32[]{:S(2)}, u32[]{:S(2)}) collective-permute-start(f32[8,4,2,8,128]{4,3,2,1,0:T(8,128)} %copy-done.26), channel_id=1, source_target_pairs={{0,1},{1,0},{2,3},{3,2},{4,5},{5,4},{6,7},{7,6},{8,9},{9,8},{10,11... | collective-permute-start | bytes 786440 | tf_op jit(solution)/shard_map/ppermute | solution.py:91
  81.2 9.4 %collective-permute-start.8 = (f32[8,4,2,8,128]{4,3,2,1,0:T(8,128)}, f32[8,4,2,8,128]{4,3,2,1,0:T(8,128)S(1)}, u32[]{:S(2)}, u32[]{:S(2)}) collective-permute-start(f32[8,4,2,8,128]{4,3,2,1,0:T(8,128)} %copy-done.25), channel_id=1, source_target_pairs={{0,2},{1,3},{2,4},{3,5},{4,6},{5,7},{6,0},{7,1},{8,10},{9,11},{10,... | collective-permute-start | bytes 786440 | tf_op jit(solution)/shard_map/ppermute | solution.py:91
  82.9 12.5 %collective-permute-start.9 = (f32[8,4,2,8,128]{4,3,2,1,0:T(8,128)}, f32[8,4,2,8,128]{4,3,2,1,0:T(8,128)S(1)}, u32[]{:S(2)}, u32[]{:S(2)}) collective-permute-start(f32[8,4,2,8,128]{4,3,2,1,0:T(8,128)} %copy-done.24), channel_id=1, source_target_pairs={{0,3},{1,2},{2,5},{3,4},{4,7},{5,6},{6,1},{7,0},{8,11},{9,10},{10,... | collective-permute-start | bytes 786440 | tf_op jit(solution)/shard_map/ppermute | solution.py:91
  83.9 11.5 %collective-permute-start.10 = (f32[8,4,2,8,128]{4,3,2,1,0:T(8,128)S(1)}, f32[8,4,2,8,128]{4,3,2,1,0:T(8,128)S(1)}, u32[]{:S(2)}, u32[]{:S(2)}) collective-permute-start(f32[8,4,2,8,128]{4,3,2,1,0:T(8,128)S(1)} %copy-done.23), channel_id=1, source_target_pairs={{0,4},{1,5},{2,6},{3,7},{4,0},{5,1},{6,2},{7,3},{8,12},{9,13},{10,... | collective-permute-start | bytes 786440 | tf_op jit(solution)/shard_map/ppermute | solution.py:91
  85.2 14.0 %collective-permute-start.11 = (f32[8,4,2,8,128]{4,3,2,1,0:T(8,128)S(1)}, f32[8,4,2,8,128]{4,3,2,1,0:T(8,128)S(1)}, u32[]{:S(2)}, u32[]{:S(2)}) collective-permute-start(f32[8,4,2,8,128]{4,3,2,1,0:T(8,128)S(1)} %copy-done.21), channel_id=1, source_target_pairs={{0,5},{1,4},{2,7},{3,6},{4,1},{5,0},{6,3},{7,2},{8,13},{9,12},{10,... | collective-permute-start | bytes 786440 | tf_op jit(solution)/shard_map/ppermute | solution.py:91
  87.1 18.1 %collective-permute-start.12 = (f32[8,4,2,8,128]{4,3,2,1,0:T(8,128)S(1)}, f32[8,4,2,8,128]{4,3,2,1,0:T(8,128)S(1)}, u32[]{:S(2)}, u32[]{:S(2)}) collective-permute-start(f32[8,4,2,8,128]{4,3,2,1,0:T(8,128)S(1)} %copy-done.19), channel_id=1, source_target_pairs={{0,6},{1,7},{2,0},{3,1},{4,2},{5,3},{6,4},{7,5},{8,14},{9,15},{10,... | collective-permute-start | bytes 786440 | tf_op jit(solution)/shard_map/ppermute | solution.py:91
  90.6 20.2 %collective-permute-start.13 = (f32[8,4,2,8,128]{4,3,2,1,0:T(8,128)S(1)}, f32[8,4,2,8,128]{4,3,2,1,0:T(8,128)S(1)}, u32[]{:S(2)}, u32[]{:S(2)}) collective-permute-start(f32[8,4,2,8,128]{4,3,2,1,0:T(8,128)S(1)} %copy-done.17), channel_id=1, source_target_pairs={{0,7},{1,6},{2,1},{3,0},{4,3},{5,2},{6,5},{7,4},{8,15},{9,14},{10,... | collective-permute-start | bytes 786440 | tf_op jit(solution)/shard_map/ppermute | solution.py:91
  (19 other events, 25.3 us)

commit v3 on v2

--- a/solution.py
+++ b/solution.py
@@ -24,20 +24,27 @@
     return jnp.swapaxes(value, -3, -2)
 
 
-def call(body, ins, outs, scalars, limit=16 * MIB):
+def call(body, ins, outs, scalars, scratch, sems, limit=64 * MIB - MIB // 4):
     smem = pl.BlockSpec(memory_space=pltpu.SMEM)
-    vmem = pl.BlockSpec(memory_space=pltpu.VMEM)
+    hbm = pl.BlockSpec(memory_space=pltpu.HBM)
     moved = 4 * (sum(a.size for a in ins[scalars:]) + sum(math.prod(s) for s in outs))
     return pl.pallas_call(
         body,
         out_shape=[jax.ShapeDtypeStruct(s, F32) for s in outs],
-        in_specs=[smem] * scalars + [vmem] * (len(ins) - scalars),
-        out_specs=[vmem] * len(outs),
+        in_specs=[smem] * scalars + [hbm] * (len(ins) - scalars),
+        out_specs=[hbm] * len(outs),
+        scratch_shapes=[pltpu.VMEM(s, F32) for s in scratch] + [pltpu.SemaphoreType.DMA((sems, NYC))],
         cost_estimate=pl.CostEstimate(flops=moved, bytes_accessed=moved, transcendentals=0),
         compiler_params=pltpu.CompilerParams(vmem_limit_bytes=limit),
     )(*ins)
 
 
+def started(copies):
+    for copy in copies:
+        copy.start()
+    return copies
+
+
 def ahead(me, d):
     return ((((me >> 1) + d // NC) & (NY - 1)) << 1) | ((me & 1) ^ (d % NC))
 
@@ -46,15 +53,36 @@
     return ((((me >> 1) + NY - d // NC) & (NY - 1)) << 1) | ((me & 1) ^ (d % NC))
 
 
-def base_kernel(me_ref, m_ref, v_ref, *outs):
-    for d in range(NYC):
-        at = ahead(me_ref[0], d)
-        outs[d][...] = m_ref[:, :, at] - (0.7 * 0.81) * v_ref[:, :, at]
+def base_kernel(me_ref, m_ref, v_ref, *refs):
+    outs, (m_buf, v_buf, sem) = refs[:NYC], refs[NYC:]
+    copy = pltpu.make_async_copy
+    at = [ahead(me_ref[0], d) for d in range(NYC)]
+    ms = [copy(m_ref.at[:, :, at[d]], m_buf.at[d], sem.at[0, d]) for d in range(NYC)]
+    vs = [copy(v_ref.at[:, :, at[d]], v_buf.at[d], sem.at[1, d]) for d in range(NYC)]
+    order = (*SHIFTS, 0)
+    for d in order:
+        started([ms[d], vs[d]])
+    back = []
+    for d in order:
+        ms[d].wait()
+        vs[d].wait()
+        m_buf[d] -= (0.7 * 0.81) * v_buf[d]
+        back += started([copy(m_buf.at[d], outs[d], sem.at[2, d])])
+    for done in back:
+        done.wait()
 
 
 def mix_kernel(me_ref, old_ref, new_ref, pm_ref, steps_ref, r_ref, *refs):
     me = me_ref[0]
     bases, averages, out = refs[:NYC], refs[NYC : 2 * NYC], refs[2 * NYC]
+    r_buf, b_buf, a_buf, o_buf, sem = refs[2 * NYC + 1 :]
+    copy = pltpu.make_async_copy
+    rows = [ahead(me, d) for d in range(NYC)]
+    opposite = [((NY - d // NC) % NY) * NC + d % NC for d in range(NYC)]
+    rs = [copy(r_ref.at[:, :, rows[d]], r_buf.at[d], sem.at[0, d]) for d in range(NYC)]
+    bs = [copy(bases[opposite[d]], b_buf.at[d], sem.at[1, d]) for d in range(NYC)]
+    for d in range(NYC):
+        started([rs[d], bs[d]])
     islands = steps_ref.shape[0]
     old = [pm_ref[old_ref[j]] for j in range(islands)]
     new = [pm_ref[new_ref[j]] for j in range(islands)]
@@ -65,24 +93,67 @@
             total += jnp.where(old[i] == old[j], steps_ref[i], 0)
         splat = lambda s: jnp.full(TILE, s, jnp.int32).astype(F32)
         weights.append(splat(steps_ref[j]) / splat(jnp.maximum(total, 1)))
-    for d in range(NYC):
-        rows = ahead(me, d)
-        e = ((NY - d // NC) % NY) * NC + d % NC
-        averages[d][...] = jnp.zeros(averages[d].shape, F32)
+    back = []
+    for d in range(NYC):
+        a_buf[d] = jnp.zeros(a_buf.shape[1:], F32)
+        rs[d].wait()
         for j in range(islands):
-            averages[d][old[j]] += weights[j] * r_ref[j, :, rows]
+            a_buf[d, old[j]] += weights[j] * r_buf[d, j]
+        bs[d].wait()
         for j in range(islands):
-            out[j, :, rows] = bases[e][new[j]] - (0.7 * 1.9) * averages[d][new[j]]
+            o_buf[d, j] = b_buf[d, new[j]] - (0.7 * 1.9) * a_buf[d, new[j]]
+        back += started(
+            [
+                copy(o_buf.at[d], out.at[:, :, rows[d]], sem.at[2, d]),
+                copy(a_buf.at[d], averages[d], sem.at[3, d]),
+            ]
+        )
+    for done in back:
+        done.wait()
 
 
 def owner_kernel(me_ref, m_ref, v_ref, *refs):
-    averages, (nm_ref, nv_ref) = refs[:NYC], refs[NYC:]
-    for d in range(NYC):
-        at = behind(me_ref[0], d)
-        avg = averages[d][...]
-        mom = 0.9 * v_ref[:, :, at] + avg
-        nv_ref[:, :, at] = mom
-        nm_ref[:, :, at] = m_ref[:, :, at] - 0.7 * (avg + 0.9 * mom)
+    averages, (nm_ref, nv_ref), (m_buf, v_buf, a_buf, sem) = refs[:NYC], refs[NYC : NYC + 2], refs[NYC + 2 :]
+    copy = pltpu.make_async_copy
+    at = [behind(me_ref[0], d) for d in range(NYC)]
+    ins = []
+    for d in range(NYC):
+        ins.append(
+            started(
+                [
+                    copy(m_ref.at[:, :, at[d]], m_buf.at[d], sem.at[0, d]),
+                    copy(v_ref.at[:, :, at[d]], v_buf.at[d], sem.at[1, d]),
+                    copy(averages[d], a_buf.at[d], sem.at[2, d]),
+                ]
+            )
+        )
+    back = []
+    for d in range(NYC):
+        for done in ins[d]:
+            done.wait()
+        avg = a_buf[d]
+        mom = 0.9 * v_buf[d] + avg
+        v_buf[d] = mom
+        m_buf[d] -= 0.7 * (avg + 0.9 * mom)
+        back += started(
+            [
+                copy(m_buf.at[d], nm_ref.at[:, :, at[d]], sem.at[3, d]),
+                copy(v_buf.at[d], nv_ref.at[:, :, at[d]], sem.at[4, d]),
+            ]
+        )
+    for done in back:
+        done.wait()
+
+
+def place_kernel(src, out, sem):
+    step = src.shape[0] // NYC
+    for done in started(
+        [
+            pltpu.make_async_copy(src.at[pl.ds(d * step, step)], out.at[pl.ds(d * step, step)], sem.at[0, d])
+            for d in range(NYC)
+        ]
+    ):
+        done.wait()
 
 
 def along_yc(pieces):
@@ -105,17 +176,22 @@
     v = tiles(momentum).reshape(owner)
 
     got = across_xz(deltas[0].reshape(32, 64, 256))
-    base = along_yc(call(base_kernel, [me, m, v], [piece] * NYC, 1))
+    slots = (NYC, *piece)
+    base = along_yc(call(base_kernel, [me, m, v], [piece] * NYC, 1, [slots] * 2, 3))
     isles = (8, 4, NYC, 2, *TILE)
     *avg, out = call(
         mix_kernel,
         [me, old_path, new_path, path_module, island_steps, tiles(got).reshape(isles), *base],
         [piece] * NYC + [isles],
         5,
+        [slots] * 4,
+        4,
     )
     out = jnp.swapaxes(out.reshape(32, NYC, 2, *TILE), 2, 3).reshape(32, 64, 256)
-    new_module = across_xz(out).reshape(deltas.shape)
-    nm, nv = call(owner_kernel, [me, m, v, *along_yc(avg)], [owner] * 2, 1)
+    landed = across_xz(out)
+    nm, nv = call(owner_kernel, [me, m, v, *along_yc(avg)], [owner] * 2, 1, [slots] * 3, 5)
+    [new_module] = call(place_kernel, [landed], [landed.shape], 0, [], 1)
+    new_module = new_module.reshape(deltas.shape)
 
     def whole(value):
         return jnp.swapaxes(value.reshape(modules, 64, *TILE), 1, 2).reshape(master.shape)

time: 134 us -> 188 us (1.40)
  Pallas kernels: 5.24 us -> 77.5 us
  local copies, waits for them, and re-layouts: 19.1 us -> 0.03 us
    pallas_call x3 -> x4, Pallas kernels: 5.24 us -> 77.5 us  [call(): pl.pallas_call(body, out_shape=[jax.ShapeDtypeStruct(s, F32) for s in out...]
    unnamed x55 -> x14, local copies, waits for them, and re-layouts: 19.1 us -> 0.03 us
    ppermute x14, waiting for transfers between devices: 42.5 us -> 45.2 us  [along_yc(): got[d] = lax.ppermute(pieces[d], YC, [(i, ahead(i, d)) for i in range(NYC)])]
    all_to_all x2, waiting for transfers between devices: 33.5 us -> 31.6 us  [across_xz(): return lax.all_to_all(value, XZ, split_axis=0, concat_axis=0, tiled=True)]
  transfers between devices with their start and end apart: 16 -> 16, of which waited for: 12 -> 12; matrix products, arithmetic and copies ran while one was open for 0% -> 0% of each run, Pallas kernels for 2% -> 4%
where the time goes in v3:
time: 188 us; the launch traced here: 187 us
  Pallas kernels  77.5 us (41%)
  waiting for transfers between devices  76.8 us (41%)
  starting transfers between devices  32.4 us (17%)
    pallas_call x4, Pallas kernels, call(): pl.pallas_call(body, out_shape=[jax.ShapeDtypeStruct(s, F32) for s in out...  77.5 us
    ppermute x14, waiting for transfers between devices, along_yc(): got[d] = lax.ppermute(pieces[d], YC, [(i, ahead(i, d)) for i in range(NYC)])  45.2 us
    all_to_all x2, waiting for transfers between devices, across_xz(): return lax.all_to_all(value, XZ, split_axis=0, concat_axis=0, tiled=True)  31.6 us
    all_to_all x2, starting transfers between devices, across_xz(): return lax.all_to_all(value, XZ, split_axis=0, concat_axis=0, tiled=True)  17.9 us
    ppermute x14, starting transfers between devices, along_yc(): got[d] = lax.ppermute(pieces[d], YC, [(i, ahead(i, d)) for i in range(NYC)])  14.5 us
  transfers between devices with their start and end apart: 16, of which 12 were waited for; matrix products, arithmetic and copies ran while one was open for 0% of the time, Pallas kernels for 4%

profile of v3, /device:TPU:8, one launch (start us, length us, event | category | flops | bytes accessed | tf_op | source)
XLA Modules:
  0.0 187.5 jit_solution(1329491986594982908)
XLA Ops:
  0.6 11.5 %all-to-all-start = ((f32[32,64,256]{2,1,0:T(8,128)}), f32[32,64,256]{2,1,0:T(8,128)}, u32[]{:S(2)}, u32[]{:S(2)}) async-start(f32[32,64,256]{2,1,0:T(8,128)} %bitcast.37), calls=%async_computation | async-start | bytes 4194304 | tf_op jit(solution)/shard_map/all_to_all | solution.py:167
  12.1 3.4 %shard_map.94 = (f32[8,4,2,8,128]{4,3,2,1,0:T(8,128)}, f32[8,4,2,8,128]{4,3,2,1,0:T(8,128)}, f32[8,4,2,8,128]{4,3,2,1,0:T(8,128)}, f32[8,4,2,8,128]{4,3,2,1,0:T(...) custom-call(s32[1]{0:T(128)} %bitcast.me_ref, ...), custom_call_target="tpu_custom_call" | custom-call | flops 6291456 | bytes 6291456 | tf_op jit(solution)/shard_map/pallas_call | solution.py:31
  15.6 1.7 collective-permute-start.1
  18.3 1.2 collective-permute-start.3
  19.6 2.0 %collective-permute-start.4 = (f32[8,4,2,8,128]{4,3,2,1,0:T(8,128)}, f32[8,4,2,8,128]{4,3,2,1,0:T(8,128)}, u32[]{:S(2)}, u32[]{:S(2)}) collective-permute-start(f32[8,4,2,8,128]{4,3,2,1,0:T(8,128)} %get-tuple-element.27), channel_id=1, source_target_pairs={{0,5},{1,4},{2,7},{3,6},{4,1},{5,0},{6,3},{7,2},{8,13},{9,12},{10,... | collective-permute-start | bytes 786440 | tf_op jit(solution)/shard_map/ppermute | solution.py:162
  22.3 2.9 %collective-permute-done.1.refs_2_ = f32[8,4,2,8,128]{4,3,2,1,0:T(8,128)} collective-permute-done((f32[8,4,2,8,128]{4,3,2,1,0:T(8,128)}, f32[8,4,2,8,128]{4,3,2,1,0:T(8,128)}, u32[]{:S(2)}, u32[]{:S(2)}) %collective-permute-start.1) | collective-permute-done | bytes 262176 | tf_op jit(solution)/shard_map/ppermute | solution.py:162
  25.7 4.1 %collective-permute-done.2.refs_3_ = f32[8,4,2,8,128]{4,3,2,1,0:T(8,128)} collective-permute-done((f32[8,4,2,8,128]{4,3,2,1,0:T(8,128)}, f32[8,4,2,8,128]{4,3,2,1,0:T(8,128)}, u32[]{:S(2)}, u32[]{:S(2)}) %collective-permute-start.2) | collective-permute-done | bytes 262176 | tf_op jit(solution)/shard_map/ppermute | solution.py:162
  29.8 4.0 %collective-permute-done.4.refs_5_ = f32[8,4,2,8,128]{4,3,2,1,0:T(8,128)} collective-permute-done((f32[8,4,2,8,128]{4,3,2,1,0:T(8,128)}, f32[8,4,2,8,128]{4,3,2,1,0:T(8,128)}, u32[]{:S(2)}, u32[]{:S(2)}) %collective-permute-start.4) | collective-permute-done | bytes 262176 | tf_op jit(solution)/shard_map/ppermute | solution.py:162
  33.9 6.1 %collective-permute-done.5.refs_6_ = f32[8,4,2,8,128]{4,3,2,1,0:T(8,128)} collective-permute-done((f32[8,4,2,8,128]{4,3,2,1,0:T(8,128)}, f32[8,4,2,8,128]{4,3,2,1,0:T(8,128)}, u32[]{:S(2)}, u32[]{:S(2)}) %collective-permute-start.5) | collective-permute-done | bytes 262176 | tf_op jit(solution)/shard_map/ppermute | solution.py:162
  40.0 5.5 %collective-permute-done.6.refs_7_ = f32[8,4,2,8,128]{4,3,2,1,0:T(8,128)} collective-permute-done((f32[8,4,2,8,128]{4,3,2,1,0:T(8,128)}, f32[8,4,2,8,128]{4,3,2,1,0:T(8,128)}, u32[]{:S(2)}, u32[]{:S(2)}) %collective-permute-start.6) | collective-permute-done | bytes 262176 | tf_op jit(solution)/shard_map/ppermute | solution.py:162
  45.5 16.6 %all-to-all-done = f32[32,64,256]{2,1,0:T(8,128)} async-done(((f32[32,64,256]{2,1,0:T(8,128)}), f32[32,64,256]{2,1,0:T(8,128)}, u32[]{:S(2)}, u32[]{:S(2)}) %all-to-all-start) | async-done | bytes 2097184 | tf_op jit(solution)/shard_map/all_to_all | solution.py:167
  62.1 4.4 %shard_map.95 = (f32[8,4,2,8,128]{4,3,2,1,0:T(8,128)}, f32[8,4,2,8,128]{4,3,2,1,0:T(8,128)}, f32[8,4,2,8,128]{4,3,2,1,0:T(8,128)}, f32[8,4,2,8,128]{4,3,2,1,0:T(...) custom-call(s32[1]{0:T(128)} %bitcast.me_ref, ...), custom_call_target="tpu_custom_call" | custom-call | flops 8388608 | bytes 8388608 | tf_op jit(solution)/shard_map/pallas_call | solution.py:31
  66.6 6.4 %all-to-all-start.1 = ((f32[32,64,256]{2,1,0:T(8,128)}), f32[32,64,256]{2,1,0:T(8,128)}, u32[]{:S(2)}, u32[]{:S(2)}) async-start(f32[32,64,256]{2,1,0:T(8,128)} %bitcast.38), calls=%async_computation.1 | async-start | bytes 4194304 | tf_op jit(solution)/shard_map/all_to_all | solution.py:167
  73.2 1.7 collective-permute-start.8
  75.9 1.2 collective-permute-start.10
  77.1 2.0 %collective-permute-start.11 = (f32[8,4,2,8,128]{4,3,2,1,0:T(8,128)S(1)}, f32[8,4,2,8,128]{4,3,2,1,0:T(8,128)}, u32[]{:S(2)}, u32[]{:S(2)}) collective-permute-start(f32[8,4,2,8,128]{4,3,2,1,0:T(8,128)S(1)} %copy-done.2), channel_id=1, source_target_pairs={{0,5},{1,4},{2,7},{3,6},{4,1},{5,0},{6,3},{7,2},{8,13},{9,12},{10,... | collective-permute-start | bytes 786440 | tf_op jit(solution)/shard_map/ppermute | solution.py:162
  79.8 2.6 %collective-permute-done.8.refs_2_ = f32[8,4,2,8,128]{4,3,2,1,0:T(8,128)} collective-permute-done((f32[8,4,2,8,128]{4,3,2,1,0:T(8,128)S(1)}, f32[8,4,2,8,128]{4,3,2,1,0:T(8,128)}, u32[]{:S(2)}, u32[]{:S(2)}) %collective-permute-start.8) | collective-permute-done | bytes 262176 | tf_op jit(solution)/shard_map/ppermute | solution.py:162
  83.0 4.1 %collective-permute-done.9.refs_3_ = f32[8,4,2,8,128]{4,3,2,1,0:T(8,128)} collective-permute-done((f32[8,4,2,8,128]{4,3,2,1,0:T(8,128)S(1)}, f32[8,4,2,8,128]{4,3,2,1,0:T(8,128)}, u32[]{:S(2)}, u32[]{:S(2)}) %collective-permute-start.9) | collective-permute-done | bytes 262176 | tf_op jit(solution)/shard_map/ppermute | solution.py:162
  87.1 4.1 %collective-permute-done.11.refs_5_ = f32[8,4,2,8,128]{4,3,2,1,0:T(8,128)} collective-permute-done((f32[8,4,2,8,128]{4,3,2,1,0:T(8,128)S(1)}, f32[8,4,2,8,128]{4,3,2,1,0:T(8,128)}, u32[]{:S(2)}, u32[]{:S(2)}) %collective-permute-start.11) | collective-permute-done | bytes 262176 | tf_op jit(solution)/shard_map/ppermute | solution.py:162
  91.2 6.1 %collective-permute-done.12.refs_6_ = f32[8,4,2,8,128]{4,3,2,1,0:T(8,128)} collective-permute-done((f32[8,4,2,8,128]{4,3,2,1,0:T(8,128)S(1)}, f32[8,4,2,8,128]{4,3,2,1,0:T(8,128)}, u32[]{:S(2)}, u32[]{:S(2)}) %collective-permute-start.12) | collective-permute-done | bytes 262176 | tf_op jit(solution)/shard_map/ppermute | solution.py:162
  97.3 5.5 %collective-permute-done.13.refs_7_ = f32[8,4,2,8,128]{4,3,2,1,0:T(8,128)} collective-permute-done((f32[8,4,2,8,128]{4,3,2,1,0:T(8,128)S(1)}, f32[8,4,2,8,128]{4,3,2,1,0:T(8,128)}, u32[]{:S(2)}, u32[]{:S(2)}) %collective-permute-start.13) | collective-permute-done | bytes 262176 | tf_op jit(solution)/shard_map/ppermute | solution.py:162
  102.9 4.9 %shard_map.96 = (f32[8,4,8,2,8,128]{5,4,3,2,1,0:T(8,128)}, f32[8,4,8,2,8,128]{5,4,3,2,1,0:T(8,128)}) custom-call(s32[1]{0:T(128)} %bitcast.me_ref, f32[8,4,8,2,8,128]{5,4,3,2,1,0:T(8,128)} %bitcast.34, f32[8,4,8,2,8,128]{5,4,3,2,1,0:T(8,128)} %bitcast.36, f32[8,4,2,8,128]{4,3,2,1,0:T(8,128)} %get-tuple-element.30.refs_0_, ...), custom_call_target="tpu_custom_call" | custom-call | flops 10485760 | bytes 10485760 | tf_op jit(solution)/shard_map/pallas_call | solution.py:31
  107.8 15.0 %all-to-all-done.1.src = f32[32,64,256]{2,1,0:T(8,128)} async-done(((f32[32,64,256]{2,1,0:T(8,128)}), f32[32,64,256]{2,1,0:T(8,128)}, u32[]{:S(2)}, u32[]{:S(2)}) %all-to-all-start.1) | async-done | bytes 2097184 | tf_op jit(solution)/shard_map/all_to_all | solution.py:167
  122.8 64.7 %shard_map.97 = f32[32,64,256]{2,1,0:T(8,128)} custom-call(f32[32,64,256]{2,1,0:T(8,128)} %all-to-all-done.1.src), custom_call_target="tpu_custom_call" | custom-call | flops 4194304 | bytes 4194304 | tf_op jit(solution)/shard_map/pallas_call | solution.py:31
  (26 shorter events, 4.8 us)
Async XLA Ops:
  0.6 61.5 %all-to-all-start = ((f32[32,64,256]{2,1,0:T(8,128)}), f32[32,64,256]{2,1,0:T(8,128)}, u32[]{:S(2)}, u32[]{:S(2)}) async-start(f32[32,64,256]{2,1,0:T(8,128)} %bitcast.37), calls=%async_computation | async-start | bytes 4194304 | tf_op jit(solution)/shard_map/all_to_all | solution.py:167
  15.5 6.0 %collective-permute-start = (f32[8,4,2,8,128]{4,3,2,1,0:T(8,128)}, f32[8,4,2,8,128]{4,3,2,1,0:T(8,128)}, u32[]{:S(2)}, u32[]{:S(2)}) collective-permute-start(f32[8,4,2,8,128]{4,3,2,1,0:T(8,128)} %get-tuple-element.23), channel_id=1, source_target_pairs={{0,1},{1,0},{2,3},{3,2},{4,5},{5,4},{6,7},{7,6},{8,9},{9,8},{10,11... | collective-permute-start | bytes 786440 | tf_op jit(solution)/shard_map/ppermute | solution.py:162
  15.6 9.5 %collective-permute-start.1 = (f32[8,4,2,8,128]{4,3,2,1,0:T(8,128)}, f32[8,4,2,8,128]{4,3,2,1,0:T(8,128)}, u32[]{:S(2)}, u32[]{:S(2)}) collective-permute-start(f32[8,4,2,8,128]{4,3,2,1,0:T(8,128)} %get-tuple-element.24), channel_id=1, source_target_pairs={{0,2},{1,3},{2,4},{3,5},{4,6},{5,7},{6,0},{7,1},{8,10},{9,11},{10,... | collective-permute-start | bytes 786440 | tf_op jit(solution)/shard_map/ppermute | solution.py:162
  17.3 12.5 %collective-permute-start.2 = (f32[8,4,2,8,128]{4,3,2,1,0:T(8,128)}, f32[8,4,2,8,128]{4,3,2,1,0:T(8,128)}, u32[]{:S(2)}, u32[]{:S(2)}) collective-permute-start(f32[8,4,2,8,128]{4,3,2,1,0:T(8,128)} %get-tuple-element.25), channel_id=1, source_target_pairs={{0,3},{1,2},{2,5},{3,4},{4,7},{5,6},{6,1},{7,0},{8,11},{9,10},{10,... | collective-permute-start | bytes 786440 | tf_op jit(solution)/shard_map/ppermute | solution.py:162
  18.3 11.5 %collective-permute-start.3 = (f32[8,4,2,8,128]{4,3,2,1,0:T(8,128)}, f32[8,4,2,8,128]{4,3,2,1,0:T(8,128)}, u32[]{:S(2)}, u32[]{:S(2)}) collective-permute-start(f32[8,4,2,8,128]{4,3,2,1,0:T(8,128)} %get-tuple-element.26), channel_id=1, source_target_pairs={{0,4},{1,5},{2,6},{3,7},{4,0},{5,1},{6,2},{7,3},{8,12},{9,13},{10,... | collective-permute-start | bytes 786440 | tf_op jit(solution)/shard_map/ppermute | solution.py:162
  19.6 14.3 %collective-permute-start.4 = (f32[8,4,2,8,128]{4,3,2,1,0:T(8,128)}, f32[8,4,2,8,128]{4,3,2,1,0:T(8,128)}, u32[]{:S(2)}, u32[]{:S(2)}) collective-permute-start(f32[8,4,2,8,128]{4,3,2,1,0:T(8,128)} %get-tuple-element.27), channel_id=1, source_target_pairs={{0,5},{1,4},{2,7},{3,6},{4,1},{5,0},{6,3},{7,2},{8,13},{9,12},{10,... | collective-permute-start | bytes 786440 | tf_op jit(solution)/shard_map/ppermute | solution.py:162
  21.5 18.5 %collective-permute-start.5 = (f32[8,4,2,8,128]{4,3,2,1,0:T(8,128)}, f32[8,4,2,8,128]{4,3,2,1,0:T(8,128)}, u32[]{:S(2)}, u32[]{:S(2)}) collective-permute-start(f32[8,4,2,8,128]{4,3,2,1,0:T(8,128)} %get-tuple-element.28), channel_id=1, source_target_pairs={{0,6},{1,7},{2,0},{3,1},{4,2},{5,3},{6,4},{7,5},{8,14},{9,15},{10,... | collective-permute-start | bytes 786440 | tf_op jit(solution)/shard_map/ppermute | solution.py:162
  25.1 20.4 %collective-permute-start.6 = (f32[8,4,2,8,128]{4,3,2,1,0:T(8,128)}, f32[8,4,2,8,128]{4,3,2,1,0:T(8,128)}, u32[]{:S(2)}, u32[]{:S(2)}) collective-permute-start(f32[8,4,2,8,128]{4,3,2,1,0:T(8,128)} %get-tuple-element.29), channel_id=1, source_target_pairs={{0,7},{1,6},{2,1},{3,0},{4,3},{5,2},{6,5},{7,4},{8,15},{9,14},{10,... | collective-permute-start | bytes 786440 | tf_op jit(solution)/shard_map/ppermute | solution.py:162
  66.6 6.5 %copy-start.6 = (f32[8,4,2,8,128]{4,3,2,1,0:T(8,128)S(1)}, f32[8,4,2,8,128]{4,3,2,1,0:T(8,128)}, u32[]{:S(2)}) copy-start(f32[8,4,2,8,128]{4,3,2,1,0:T(8,128)} %get-tuple-element.31) | copy-start | bytes 786436
  66.6 6.6 %copy-start.5 = (f32[8,4,2,8,128]{4,3,2,1,0:T(8,128)S(1)}, f32[8,4,2,8,128]{4,3,2,1,0:T(8,128)}, u32[]{:S(2)}) copy-start(f32[8,4,2,8,128]{4,3,2,1,0:T(8,128)} %get-tuple-element.32) | copy-start | bytes 786436
  66.6 8.2 %copy-start.4 = (f32[8,4,2,8,128]{4,3,2,1,0:T(8,128)S(1)}, f32[8,4,2,8,128]{4,3,2,1,0:T(8,128)}, u32[]{:S(2)}) copy-start(f32[8,4,2,8,128]{4,3,2,1,0:T(8,128)} %get-tuple-element.33) | copy-start | bytes 786436
  66.6 9.3 %copy-start.3 = (f32[8,4,2,8,128]{4,3,2,1,0:T(8,128)S(1)}, f32[8,4,2,8,128]{4,3,2,1,0:T(8,128)}, u32[]{:S(2)}) copy-start(f32[8,4,2,8,128]{4,3,2,1,0:T(8,128)} %get-tuple-element.34) | copy-start | bytes 786436
  66.6 10.5 %copy-start.2 = (f32[8,4,2,8,128]{4,3,2,1,0:T(8,128)S(1)}, f32[8,4,2,8,128]{4,3,2,1,0:T(8,128)}, u32[]{:S(2)}) copy-start(f32[8,4,2,8,128]{4,3,2,1,0:T(8,128)} %get-tuple-element.35) | copy-start | bytes 786436
  66.6 12.5 %copy-start.1 = (f32[8,4,2,8,128]{4,3,2,1,0:T(8,128)S(1)}, f32[8,4,2,8,128]{4,3,2,1,0:T(8,128)}, u32[]{:S(2)}) copy-start(f32[8,4,2,8,128]{4,3,2,1,0:T(8,128)} %get-tuple-element.36) | copy-start | bytes 786436
  66.6 15.8 %copy-start = (f32[8,4,2,8,128]{4,3,2,1,0:T(8,128)S(1)}, f32[8,4,2,8,128]{4,3,2,1,0:T(8,128)}, u32[]{:S(2)}) copy-start(f32[8,4,2,8,128]{4,3,2,1,0:T(8,128)} %get-tuple-element.37) | copy-start | bytes 786436
  66.6 56.2 %all-to-all-start.1 = ((f32[32,64,256]{2,1,0:T(8,128)}), f32[32,64,256]{2,1,0:T(8,128)}, u32[]{:S(2)}, u32[]{:S(2)}) async-start(f32[32,64,256]{2,1,0:T(8,128)} %bitcast.38), calls=%async_computation.1 | async-start | bytes 4194304 | tf_op jit(solution)/shard_map/all_to_all | solution.py:167
  73.1 6.0 %collective-permute-start.7 = (f32[8,4,2,8,128]{4,3,2,1,0:T(8,128)S(1)}, f32[8,4,2,8,128]{4,3,2,1,0:T(8,128)}, u32[]{:S(2)}, u32[]{:S(2)}) collective-permute-start(f32[8,4,2,8,128]{4,3,2,1,0:T(8,128)S(1)} %copy-done.6), channel_id=1, source_target_pairs={{0,1},{1,0},{2,3},{3,2},{4,5},{5,4},{6,7},{7,6},{8,9},{9,8},{10,11... | collective-permute-start | bytes 786440 | tf_op jit(solution)/shard_map/ppermute | solution.py:162
  73.2 9.3 %collective-permute-start.8 = (f32[8,4,2,8,128]{4,3,2,1,0:T(8,128)S(1)}, f32[8,4,2,8,128]{4,3,2,1,0:T(8,128)}, u32[]{:S(2)}, u32[]{:S(2)}) collective-permute-start(f32[8,4,2,8,128]{4,3,2,1,0:T(8,128)S(1)} %copy-done.5), channel_id=1, source_target_pairs={{0,2},{1,3},{2,4},{3,5},{4,6},{5,7},{6,0},{7,1},{8,10},{9,11},{10,... | collective-permute-start | bytes 786440 | tf_op jit(solution)/shard_map/ppermute | solution.py:162
  74.8 12.3 %collective-permute-start.9 = (f32[8,4,2,8,128]{4,3,2,1,0:T(8,128)S(1)}, f32[8,4,2,8,128]{4,3,2,1,0:T(8,128)}, u32[]{:S(2)}, u32[]{:S(2)}) collective-permute-start(f32[8,4,2,8,128]{4,3,2,1,0:T(8,128)S(1)} %copy-done.4), channel_id=1, source_target_pairs={{0,3},{1,2},{2,5},{3,4},{4,7},{5,6},{6,1},{7,0},{8,11},{9,10},{10,... | collective-permute-start | bytes 786440 | tf_op jit(solution)/shard_map/ppermute | solution.py:162
  75.9 11.3 %collective-permute-start.10 = (f32[8,4,2,8,128]{4,3,2,1,0:T(8,128)S(1)}, f32[8,4,2,8,128]{4,3,2,1,0:T(8,128)}, u32[]{:S(2)}, u32[]{:S(2)}) collective-permute-start(f32[8,4,2,8,128]{4,3,2,1,0:T(8,128)S(1)} %copy-done.3), channel_id=1, source_target_pairs={{0,4},{1,5},{2,6},{3,7},{4,0},{5,1},{6,2},{7,3},{8,12},{9,13},{10,... | collective-permute-start | bytes 786440 | tf_op jit(solution)/shard_map/ppermute | solution.py:162
  77.1 14.1 %collective-permute-start.11 = (f32[8,4,2,8,128]{4,3,2,1,0:T(8,128)S(1)}, f32[8,4,2,8,128]{4,3,2,1,0:T(8,128)}, u32[]{:S(2)}, u32[]{:S(2)}) collective-permute-start(f32[8,4,2,8,128]{4,3,2,1,0:T(8,128)S(1)} %copy-done.2), channel_id=1, source_target_pairs={{0,5},{1,4},{2,7},{3,6},{4,1},{5,0},{6,3},{7,2},{8,13},{9,12},{10,... | collective-permute-start | bytes 786440 | tf_op jit(solution)/shard_map/ppermute | solution.py:162
  79.1 18.2 %collective-permute-start.12 = (f32[8,4,2,8,128]{4,3,2,1,0:T(8,128)S(1)}, f32[8,4,2,8,128]{4,3,2,1,0:T(8,128)}, u32[]{:S(2)}, u32[]{:S(2)}) collective-permute-start(f32[8,4,2,8,128]{4,3,2,1,0:T(8,128)S(1)} %copy-done.1), channel_id=1, source_target_pairs={{0,6},{1,7},{2,0},{3,1},{4,2},{5,3},{6,4},{7,5},{8,14},{9,15},{10,... | collective-permute-start | bytes 786440 | tf_op jit(solution)/shard_map/ppermute | solution.py:162
  82.5 20.4 %collective-permute-start.13 = (f32[8,4,2,8,128]{4,3,2,1,0:T(8,128)S(1)}, f32[8,4,2,8,128]{4,3,2,1,0:T(8,128)}, u32[]{:S(2)}, u32[]{:S(2)}) collective-permute-start(f32[8,4,2,8,128]{4,3,2,1,0:T(8,128)S(1)} %copy-done), channel_id=1, source_target_pairs={{0,7},{1,6},{2,1},{3,0},{4,3},{5,2},{6,5},{7,4},{8,15},{9,14},{10,... | collective-permute-start | bytes 786440 | tf_op jit(solution)/shard_map/ppermute | solution.py:162

commit v4 on v3

--- a/solution.py
+++ b/solution.py
@@ -9,8 +9,9 @@
 from jax.sharding import PartitionSpec as P
 
 XZ = ("x", "zh", "zl")
+ZX = ("zh", "zl", "x")
 YC = ("y", "c")
-NY, NC = 4, 2
+NY, NC, NZ = 4, 2, 8
 NYC = NY * NC
 SHIFTS = (4, 5, 2, 6, 3, 7, 1)
 TILE = (8, 128)
@@ -24,15 +25,16 @@
     return jnp.swapaxes(value, -3, -2)
 
 
-def call(body, ins, outs, scalars, scratch, sems, limit=64 * MIB - MIB // 4):
+def call(body, ins, outs, scalars, scratch, sems, limit=64 * MIB - MIB // 4, near=()):
     smem = pl.BlockSpec(memory_space=pltpu.SMEM)
     hbm = pl.BlockSpec(memory_space=pltpu.HBM)
+    vmem = pl.BlockSpec(memory_space=pltpu.VMEM)
     moved = 4 * (sum(a.size for a in ins[scalars:]) + sum(math.prod(s) for s in outs))
     return pl.pallas_call(
         body,
         out_shape=[jax.ShapeDtypeStruct(s, F32) for s in outs],
         in_specs=[smem] * scalars + [hbm] * (len(ins) - scalars),
-        out_specs=[hbm] * len(outs),
+        out_specs=[vmem if i in near else hbm for i in range(len(outs))],
         scratch_shapes=[pltpu.VMEM(s, F32) for s in scratch] + [pltpu.SemaphoreType.DMA((sems, NYC))],
         cost_estimate=pl.CostEstimate(flops=moved, bytes_accessed=moved, transcendentals=0),
         compiler_params=pltpu.CompilerParams(vmem_limit_bytes=limit),
@@ -75,7 +77,7 @@
 def mix_kernel(me_ref, old_ref, new_ref, pm_ref, steps_ref, r_ref, *refs):
     me = me_ref[0]
     bases, averages, out = refs[:NYC], refs[NYC : 2 * NYC], refs[2 * NYC]
-    r_buf, b_buf, a_buf, o_buf, sem = refs[2 * NYC + 1 :]
+    r_buf, b_buf, a_buf, sem = refs[2 * NYC + 1 :]
     copy = pltpu.make_async_copy
     rows = [ahead(me, d) for d in range(NYC)]
     opposite = [((NY - d // NC) % NY) * NC + d % NC for d in range(NYC)]
@@ -101,13 +103,8 @@
             a_buf[d, old[j]] += weights[j] * r_buf[d, j]
         bs[d].wait()
         for j in range(islands):
-            o_buf[d, j] = b_buf[d, new[j]] - (0.7 * 1.9) * a_buf[d, new[j]]
-        back += started(
-            [
-                copy(o_buf.at[d], out.at[:, :, rows[d]], sem.at[2, d]),
-                copy(a_buf.at[d], averages[d], sem.at[3, d]),
-            ]
-        )
+            out[j % 2, :, j // 2, rows[d]] = b_buf[d, new[j]] - (0.7 * 1.9) * a_buf[d, new[j]]
+        back += started([copy(a_buf.at[d], averages[d], sem.at[2, d])])
     for done in back:
         done.wait()
 
@@ -145,14 +142,14 @@
         done.wait()
 
 
-def place_kernel(src, out, sem):
-    step = src.shape[0] // NYC
-    for done in started(
-        [
-            pltpu.make_async_copy(src.at[pl.ds(d * step, step)], out.at[pl.ds(d * step, step)], sem.at[0, d])
-            for d in range(NYC)
-        ]
-    ):
+def place_kernel(src, out, buf, sem):
+    copy = pltpu.make_async_copy
+    ins = started([copy(src.at[z], buf.at[:, z], sem.at[0, z]) for z in range(NZ)])
+    back = []
+    for z in range(NZ):
+        ins[z].wait()
+        back += started([copy(buf.at[:, z], out.at[:, z], sem.at[1, z])])
+    for done in back:
         done.wait()
 
 
@@ -163,8 +160,8 @@
     return got
 
 
-def across_xz(value):
-    return lax.all_to_all(value, XZ, split_axis=0, concat_axis=0, tiled=True)
+def across(axes, value):
+    return lax.all_to_all(value, axes, split_axis=0, concat_axis=0, tiled=True)
 
 
 def shards(master, momentum, deltas, old_path, new_path, path_module, island_steps):
@@ -175,22 +172,26 @@
     m = tiles(master).reshape(owner)
     v = tiles(momentum).reshape(owner)
 
-    got = across_xz(deltas[0].reshape(32, 64, 256))
+    got = across(XZ, deltas[0].reshape(32, 64, 256))
     slots = (NYC, *piece)
     base = along_yc(call(base_kernel, [me, m, v], [piece] * NYC, 1, [slots] * 2, 3))
-    isles = (8, 4, NYC, 2, *TILE)
+    isles, sent = (8, 4, NYC, 2, *TILE), (2, 4, 4, NYC, 2, *TILE)
     *avg, out = call(
         mix_kernel,
         [me, old_path, new_path, path_module, island_steps, tiles(got).reshape(isles), *base],
-        [piece] * NYC + [isles],
+        [piece] * NYC + [sent],
         5,
-        [slots] * 4,
-        4,
+        [slots] * 3,
+        3,
+        limit=64 * MIB - MIB // 4,
+        near=(NYC,),
     )
     out = jnp.swapaxes(out.reshape(32, NYC, 2, *TILE), 2, 3).reshape(32, 64, 256)
-    landed = across_xz(out)
+    landed = across(ZX, out)
     nm, nv = call(owner_kernel, [me, m, v, *along_yc(avg)], [owner] * 2, 1, [slots] * 3, 5)
-    [new_module] = call(place_kernel, [landed], [landed.shape], 0, [], 1)
+    landed = landed.reshape(NZ, 4, 64, 256)
+    placed = (4, NZ, 64, 256)
+    [new_module] = call(place_kernel, [landed], [placed], 0, [placed], 2)
     new_module = new_module.reshape(deltas.shape)
 
     def whole(value):

time: 188 us -> 127 us (0.68)
  Pallas kernels: 77.5 us -> 16.2 us
    pallas_call x4, Pallas kernels: 77.5 us -> 16.2 us  [call(): pl.pallas_call(body, out_shape=[jax.ShapeDtypeStruct(s, F32) for s in out...]
  transfers between devices with their start and end apart: 16 -> 16, of which waited for: 12 -> 12; matrix products, arithmetic and copies ran while one was open for 0% -> 0% of each run, Pallas kernels for 4% -> 7%
where the time goes in v4:
time: 127 us; the launch traced here: 126 us
  waiting for transfers between devices  76.9 us (61%)
  starting transfers between devices  32.4 us (26%)
  Pallas kernels  16.2 us (13%)
    ppermute x14, waiting for transfers between devices, along_yc(): got[d] = lax.ppermute(pieces[d], YC, [(i, ahead(i, d)) for i in range(NYC)])  45.2 us
    all_to_all x2, waiting for transfers between devices, across(): return lax.all_to_all(value, axes, split_axis=0, concat_axis=0, tiled=True)  31.7 us
    all_to_all x2, starting transfers between devices, across(): return lax.all_to_all(value, axes, split_axis=0, concat_axis=0, tiled=True)  17.9 us
    pallas_call x4, Pallas kernels, call(): pl.pallas_call(body, out_shape=[jax.ShapeDtypeStruct(s, F32) for s in out...  16.2 us
    ppermute x14, starting transfers between devices, along_yc(): got[d] = lax.ppermute(pieces[d], YC, [(i, ahead(i, d)) for i in range(NYC)])  14.5 us
  transfers between devices with their start and end apart: 16, of which 12 were waited for; matrix products, arithmetic and copies ran while one was open for 0% of the time, Pallas kernels for 7%

profile of v4, /device:TPU:8, one launch (start us, length us, event | category | flops | bytes accessed | tf_op | source)
XLA Modules:
  0.0 126.3 jit_solution(14291787089372160478)
XLA Ops:
  0.6 11.5 %all-to-all-start = ((f32[32,64,256]{2,1,0:T(8,128)}), f32[32,64,256]{2,1,0:T(8,128)}, u32[]{:S(2)}, u32[]{:S(2)}) async-start(f32[32,64,256]{2,1,0:T(8,128)} %bitcast.38), calls=%async_computation | async-start | bytes 4194304 | tf_op jit(solution)/shard_map/all_to_all | solution.py:164
  12.1 3.4 %shard_map.94 = (f32[8,4,2,8,128]{4,3,2,1,0:T(8,128)}, f32[8,4,2,8,128]{4,3,2,1,0:T(8,128)}, f32[8,4,2,8,128]{4,3,2,1,0:T(8,128)}, f32[8,4,2,8,128]{4,3,2,1,0:T(...) custom-call(s32[1]{0:T(128)} %bitcast.me_ref, ...), custom_call_target="tpu_custom_call" | custom-call | flops 6291456 | bytes 6291456 | tf_op jit(solution)/shard_map/pallas_call | solution.py:33
  15.6 1.7 %collective-permute-start.1 = (f32[8,4,2,8,128]{4,3,2,1,0:T(8,128)}, f32[8,4,2,8,128]{4,3,2,1,0:T(8,128)}, u32[]{:S(2)}, u32[]{:S(2)}) collective-permute-start(f32[8,4,2,8,128]{4,3,2,1,0:T(8,128)} %get-tuple-element.24), channel_id=1, source_target_pairs={{0,2},{1,3},{2,4},{3,5},{4,6},{5,7},{6,0},{7,1},{8,10},{9,11},{10,... | collective-permute-start | bytes 786440 | tf_op jit(solution)/shard_map/ppermute | solution.py:159
  18.3 1.2 collective-permute-start.3
  19.6 2.0 %collective-permute-start.4 = (f32[8,4,2,8,128]{4,3,2,1,0:T(8,128)}, f32[8,4,2,8,128]{4,3,2,1,0:T(8,128)}, u32[]{:S(2)}, u32[]{:S(2)}) collective-permute-start(f32[8,4,2,8,128]{4,3,2,1,0:T(8,128)} %get-tuple-element.27), channel_id=1, source_target_pairs={{0,5},{1,4},{2,7},{3,6},{4,1},{5,0},{6,3},{7,2},{8,13},{9,12},{10,... | collective-permute-start | bytes 786440 | tf_op jit(solution)/shard_map/ppermute | solution.py:159
  22.3 2.9 %collective-permute-done.1.refs_2_ = f32[8,4,2,8,128]{4,3,2,1,0:T(8,128)} collective-permute-done((f32[8,4,2,8,128]{4,3,2,1,0:T(8,128)}, f32[8,4,2,8,128]{4,3,2,1,0:T(8,128)}, u32[]{:S(2)}, u32[]{:S(2)}) %collective-permute-start.1) | collective-permute-done | bytes 262176 | tf_op jit(solution)/shard_map/ppermute | solution.py:159
  25.7 4.1 %collective-permute-done.2.refs_3_ = f32[8,4,2,8,128]{4,3,2,1,0:T(8,128)} collective-permute-done((f32[8,4,2,8,128]{4,3,2,1,0:T(8,128)}, f32[8,4,2,8,128]{4,3,2,1,0:T(8,128)}, u32[]{:S(2)}, u32[]{:S(2)}) %collective-permute-start.2) | collective-permute-done | bytes 262176 | tf_op jit(solution)/shard_map/ppermute | solution.py:159
  29.8 4.0 %collective-permute-done.4.refs_5_ = f32[8,4,2,8,128]{4,3,2,1,0:T(8,128)} collective-permute-done((f32[8,4,2,8,128]{4,3,2,1,0:T(8,128)}, f32[8,4,2,8,128]{4,3,2,1,0:T(8,128)}, u32[]{:S(2)}, u32[]{:S(2)}) %collective-permute-start.4) | collective-permute-done | bytes 262176 | tf_op jit(solution)/shard_map/ppermute | solution.py:159
  33.9 6.1 %collective-permute-done.5.refs_6_ = f32[8,4,2,8,128]{4,3,2,1,0:T(8,128)} collective-permute-done((f32[8,4,2,8,128]{4,3,2,1,0:T(8,128)}, f32[8,4,2,8,128]{4,3,2,1,0:T(8,128)}, u32[]{:S(2)}, u32[]{:S(2)}) %collective-permute-start.5) | collective-permute-done | bytes 262176 | tf_op jit(solution)/shard_map/ppermute | solution.py:159
  40.0 5.5 %collective-permute-done.6.refs_7_ = f32[8,4,2,8,128]{4,3,2,1,0:T(8,128)} collective-permute-done((f32[8,4,2,8,128]{4,3,2,1,0:T(8,128)}, f32[8,4,2,8,128]{4,3,2,1,0:T(8,128)}, u32[]{:S(2)}, u32[]{:S(2)}) %collective-permute-start.6) | collective-permute-done | bytes 262176 | tf_op jit(solution)/shard_map/ppermute | solution.py:159
  45.5 16.6 %all-to-all-done = f32[32,64,256]{2,1,0:T(8,128)} async-done(((f32[32,64,256]{2,1,0:T(8,128)}), f32[32,64,256]{2,1,0:T(8,128)}, u32[]{:S(2)}, u32[]{:S(2)}) %all-to-all-start) | async-done | bytes 2097184 | tf_op jit(solution)/shard_map/all_to_all | solution.py:164
  62.1 5.5 %shard_map.95 = (f32[8,4,2,8,128]{4,3,2,1,0:T(8,128)}, f32[8,4,2,8,128]{4,3,2,1,0:T(8,128)}, f32[8,4,2,8,128]{4,3,2,1,0:T(8,128)}, f32[8,4,2,8,128]{4,3,2,1,0:T(...) custom-call(s32[1]{0:T(128)} %bitcast.me_ref, ...), custom_call_target="tpu_custom_call" | custom-call | flops 8388608 | bytes 8388608 | tf_op jit(solution)/shard_map/pallas_call | solution.py:33
  67.6 6.4 %all-to-all-start.1 = ((f32[32,64,256]{2,1,0:T(8,128)}), f32[32,64,256]{2,1,0:T(8,128)}, u32[]{:S(2)}, u32[]{:S(2)}) async-start(f32[32,64,256]{2,1,0:T(8,128)} %bitcast.39), calls=%async_computation.1 | async-start | bytes 4194304 | tf_op jit(solution)/shard_map/all_to_all | solution.py:164
  74.2 1.7 %collective-permute-start.8 = (f32[8,4,2,8,128]{4,3,2,1,0:T(8,128)S(1)}, f32[8,4,2,8,128]{4,3,2,1,0:T(8,128)}, u32[]{:S(2)}, u32[]{:S(2)}) collective-permute-start(f32[8,4,2,8,128]{4,3,2,1,0:T(8,128)S(1)} %copy-done.5), channel_id=1, source_target_pairs={{0,2},{1,3},{2,4},{3,5},{4,6},{5,7},{6,0},{7,1},{8,10},{9,11},{10,... | collective-permute-start | bytes 786440 | tf_op jit(solution)/shard_map/ppermute | solution.py:159
  76.9 1.2 collective-permute-start.10
  78.1 2.0 %collective-permute-start.11 = (f32[8,4,2,8,128]{4,3,2,1,0:T(8,128)S(1)}, f32[8,4,2,8,128]{4,3,2,1,0:T(8,128)}, u32[]{:S(2)}, u32[]{:S(2)}) collective-permute-start(f32[8,4,2,8,128]{4,3,2,1,0:T(8,128)S(1)} %copy-done.2), channel_id=1, source_target_pairs={{0,5},{1,4},{2,7},{3,6},{4,1},{5,0},{6,3},{7,2},{8,13},{9,12},{10,... | collective-permute-start | bytes 786440 | tf_op jit(solution)/shard_map/ppermute | solution.py:159
  80.8 2.6 %collective-permute-done.8.refs_2_ = f32[8,4,2,8,128]{4,3,2,1,0:T(8,128)} collective-permute-done((f32[8,4,2,8,128]{4,3,2,1,0:T(8,128)S(1)}, f32[8,4,2,8,128]{4,3,2,1,0:T(8,128)}, u32[]{:S(2)}, u32[]{:S(2)}) %collective-permute-start.8) | collective-permute-done | bytes 262176 | tf_op jit(solution)/shard_map/ppermute | solution.py:159
  84.0 4.1 %collective-permute-done.9.refs_3_ = f32[8,4,2,8,128]{4,3,2,1,0:T(8,128)} collective-permute-done((f32[8,4,2,8,128]{4,3,2,1,0:T(8,128)S(1)}, f32[8,4,2,8,128]{4,3,2,1,0:T(8,128)}, u32[]{:S(2)}, u32[]{:S(2)}) %collective-permute-start.9) | collective-permute-done | bytes 262176 | tf_op jit(solution)/shard_map/ppermute | solution.py:159
  88.1 4.1 %collective-permute-done.11.refs_5_ = f32[8,4,2,8,128]{4,3,2,1,0:T(8,128)} collective-permute-done((f32[8,4,2,8,128]{4,3,2,1,0:T(8,128)S(1)}, f32[8,4,2,8,128]{4,3,2,1,0:T(8,128)}, u32[]{:S(2)}, u32[]{:S(2)}) %collective-permute-start.11) | collective-permute-done | bytes 262176 | tf_op jit(solution)/shard_map/ppermute | solution.py:159
  92.2 6.1 %collective-permute-done.12.refs_6_ = f32[8,4,2,8,128]{4,3,2,1,0:T(8,128)} collective-permute-done((f32[8,4,2,8,128]{4,3,2,1,0:T(8,128)S(1)}, f32[8,4,2,8,128]{4,3,2,1,0:T(8,128)}, u32[]{:S(2)}, u32[]{:S(2)}) %collective-permute-start.12) | collective-permute-done | bytes 262176 | tf_op jit(solution)/shard_map/ppermute | solution.py:159
  98.3 5.5 %collective-permute-done.13.refs_7_ = f32[8,4,2,8,128]{4,3,2,1,0:T(8,128)} collective-permute-done((f32[8,4,2,8,128]{4,3,2,1,0:T(8,128)S(1)}, f32[8,4,2,8,128]{4,3,2,1,0:T(8,128)}, u32[]{:S(2)}, u32[]{:S(2)}) %collective-permute-start.13) | collective-permute-done | bytes 262176 | tf_op jit(solution)/shard_map/ppermute | solution.py:159
  103.9 4.9 %shard_map.96 = (f32[8,4,8,2,8,128]{5,4,3,2,1,0:T(8,128)}, f32[8,4,8,2,8,128]{5,4,3,2,1,0:T(8,128)}) custom-call(s32[1]{0:T(128)} %bitcast.me_ref, f32[8,4,8,2,8,128]{5,4,3,2,1,0:T(8,128)} %bitcast.35, f32[8,4,8,2,8,128]{5,4,3,2,1,0:T(8,128)} %bitcast.37, f32[8,4,2,8,128]{4,3,2,1,0:T(8,128)} %get-tuple-element.30.refs_0_, ...), custom_call_target="tpu_custom_call" | custom-call | flops 10485760 | bytes 10485760 | tf_op jit(solution)/shard_map/pallas_call | solution.py:33
  108.8 15.1 %all-to-all-done.1 = f32[32,64,256]{2,1,0:T(8,128)} async-done(((f32[32,64,256]{2,1,0:T(8,128)}), f32[32,64,256]{2,1,0:T(8,128)}, u32[]{:S(2)}, u32[]{:S(2)}) %all-to-all-start.1) | async-done | bytes 2097184 | tf_op jit(solution)/shard_map/all_to_all | solution.py:164
  123.9 2.4 %shard_map.97 = f32[4,8,64,256]{3,2,1,0:T(8,128)} custom-call(f32[8,4,64,256]{3,2,1,0:T(8,128)} %bitcast.24.src), custom_call_target="tpu_custom_call" | custom-call | flops 4194304 | bytes 4194304 | tf_op jit(solution)/shard_map/pallas_call | solution.py:33
  (26 shorter events, 4.8 us)
Async XLA Ops:
  0.6 61.5 %all-to-all-start = ((f32[32,64,256]{2,1,0:T(8,128)}), f32[32,64,256]{2,1,0:T(8,128)}, u32[]{:S(2)}, u32[]{:S(2)}) async-start(f32[32,64,256]{2,1,0:T(8,128)} %bitcast.38), calls=%async_computation | async-start | bytes 4194304 | tf_op jit(solution)/shard_map/all_to_all | solution.py:164
  15.5 6.0 %collective-permute-start = (f32[8,4,2,8,128]{4,3,2,1,0:T(8,128)}, f32[8,4,2,8,128]{4,3,2,1,0:T(8,128)}, u32[]{:S(2)}, u32[]{:S(2)}) collective-permute-start(f32[8,4,2,8,128]{4,3,2,1,0:T(8,128)} %get-tuple-element.23), channel_id=1, source_target_pairs={{0,1},{1,0},{2,3},{3,2},{4,5},{5,4},{6,7},{7,6},{8,9},{9,8},{10,11... | collective-permute-start | bytes 786440 | tf_op jit(solution)/shard_map/ppermute | solution.py:159
  15.6 9.5 %collective-permute-start.1 = (f32[8,4,2,8,128]{4,3,2,1,0:T(8,128)}, f32[8,4,2,8,128]{4,3,2,1,0:T(8,128)}, u32[]{:S(2)}, u32[]{:S(2)}) collective-permute-start(f32[8,4,2,8,128]{4,3,2,1,0:T(8,128)} %get-tuple-element.24), channel_id=1, source_target_pairs={{0,2},{1,3},{2,4},{3,5},{4,6},{5,7},{6,0},{7,1},{8,10},{9,11},{10,... | collective-permute-start | bytes 786440 | tf_op jit(solution)/shard_map/ppermute | solution.py:159
  17.3 12.5 %collective-permute-start.2 = (f32[8,4,2,8,128]{4,3,2,1,0:T(8,128)}, f32[8,4,2,8,128]{4,3,2,1,0:T(8,128)}, u32[]{:S(2)}, u32[]{:S(2)}) collective-permute-start(f32[8,4,2,8,128]{4,3,2,1,0:T(8,128)} %get-tuple-element.25), channel_id=1, source_target_pairs={{0,3},{1,2},{2,5},{3,4},{4,7},{5,6},{6,1},{7,0},{8,11},{9,10},{10,... | collective-permute-start | bytes 786440 | tf_op jit(solution)/shard_map/ppermute | solution.py:159
  18.3 11.5 %collective-permute-start.3 = (f32[8,4,2,8,128]{4,3,2,1,0:T(8,128)}, f32[8,4,2,8,128]{4,3,2,1,0:T(8,128)}, u32[]{:S(2)}, u32[]{:S(2)}) collective-permute-start(f32[8,4,2,8,128]{4,3,2,1,0:T(8,128)} %get-tuple-element.26), channel_id=1, source_target_pairs={{0,4},{1,5},{2,6},{3,7},{4,0},{5,1},{6,2},{7,3},{8,12},{9,13},{10,... | collective-permute-start | bytes 786440 | tf_op jit(solution)/shard_map/ppermute | solution.py:159
  19.6 14.3 %collective-permute-start.4 = (f32[8,4,2,8,128]{4,3,2,1,0:T(8,128)}, f32[8,4,2,8,128]{4,3,2,1,0:T(8,128)}, u32[]{:S(2)}, u32[]{:S(2)}) collective-permute-start(f32[8,4,2,8,128]{4,3,2,1,0:T(8,128)} %get-tuple-element.27), channel_id=1, source_target_pairs={{0,5},{1,4},{2,7},{3,6},{4,1},{5,0},{6,3},{7,2},{8,13},{9,12},{10,... | collective-permute-start | bytes 786440 | tf_op jit(solution)/shard_map/ppermute | solution.py:159
  21.5 18.5 %collective-permute-start.5 = (f32[8,4,2,8,128]{4,3,2,1,0:T(8,128)}, f32[8,4,2,8,128]{4,3,2,1,0:T(8,128)}, u32[]{:S(2)}, u32[]{:S(2)}) collective-permute-start(f32[8,4,2,8,128]{4,3,2,1,0:T(8,128)} %get-tuple-element.28), channel_id=1, source_target_pairs={{0,6},{1,7},{2,0},{3,1},{4,2},{5,3},{6,4},{7,5},{8,14},{9,15},{10,... | collective-permute-start | bytes 786440 | tf_op jit(solution)/shard_map/ppermute | solution.py:159
  25.1 20.4 %collective-permute-start.6 = (f32[8,4,2,8,128]{4,3,2,1,0:T(8,128)}, f32[8,4,2,8,128]{4,3,2,1,0:T(8,128)}, u32[]{:S(2)}, u32[]{:S(2)}) collective-permute-start(f32[8,4,2,8,128]{4,3,2,1,0:T(8,128)} %get-tuple-element.29), channel_id=1, source_target_pairs={{0,7},{1,6},{2,1},{3,0},{4,3},{5,2},{6,5},{7,4},{8,15},{9,14},{10,... | collective-permute-start | bytes 786440 | tf_op jit(solution)/shard_map/ppermute | solution.py:159
  67.6 6.5 %copy-start.6 = (f32[8,4,2,8,128]{4,3,2,1,0:T(8,128)S(1)}, f32[8,4,2,8,128]{4,3,2,1,0:T(8,128)}, u32[]{:S(2)}) copy-start(f32[8,4,2,8,128]{4,3,2,1,0:T(8,128)} %get-tuple-element.31) | copy-start | bytes 786436
  67.6 6.6 %copy-start.5 = (f32[8,4,2,8,128]{4,3,2,1,0:T(8,128)S(1)}, f32[8,4,2,8,128]{4,3,2,1,0:T(8,128)}, u32[]{:S(2)}) copy-start(f32[8,4,2,8,128]{4,3,2,1,0:T(8,128)} %get-tuple-element.32) | copy-start | bytes 786436
  67.6 8.2 %copy-start.4 = (f32[8,4,2,8,128]{4,3,2,1,0:T(8,128)S(1)}, f32[8,4,2,8,128]{4,3,2,1,0:T(8,128)}, u32[]{:S(2)}) copy-start(f32[8,4,2,8,128]{4,3,2,1,0:T(8,128)} %get-tuple-element.33) | copy-start | bytes 786436
  67.6 9.3 %copy-start.3 = (f32[8,4,2,8,128]{4,3,2,1,0:T(8,128)S(1)}, f32[8,4,2,8,128]{4,3,2,1,0:T(8,128)}, u32[]{:S(2)}) copy-start(f32[8,4,2,8,128]{4,3,2,1,0:T(8,128)} %get-tuple-element.34) | copy-start | bytes 786436
  67.6 10.5 %copy-start.2 = (f32[8,4,2,8,128]{4,3,2,1,0:T(8,128)S(1)}, f32[8,4,2,8,128]{4,3,2,1,0:T(8,128)}, u32[]{:S(2)}) copy-start(f32[8,4,2,8,128]{4,3,2,1,0:T(8,128)} %get-tuple-element.35) | copy-start | bytes 786436
  67.6 12.5 %copy-start.1 = (f32[8,4,2,8,128]{4,3,2,1,0:T(8,128)S(1)}, f32[8,4,2,8,128]{4,3,2,1,0:T(8,128)}, u32[]{:S(2)}) copy-start(f32[8,4,2,8,128]{4,3,2,1,0:T(8,128)} %get-tuple-element.36) | copy-start | bytes 786436
  67.6 15.8 %copy-start = (f32[8,4,2,8,128]{4,3,2,1,0:T(8,128)S(1)}, f32[8,4,2,8,128]{4,3,2,1,0:T(8,128)}, u32[]{:S(2)}) copy-start(f32[8,4,2,8,128]{4,3,2,1,0:T(8,128)} %get-tuple-element.37) | copy-start | bytes 786436
  67.6 56.3 %all-to-all-start.1 = ((f32[32,64,256]{2,1,0:T(8,128)}), f32[32,64,256]{2,1,0:T(8,128)}, u32[]{:S(2)}, u32[]{:S(2)}) async-start(f32[32,64,256]{2,1,0:T(8,128)} %bitcast.39), calls=%async_computation.1 | async-start | bytes 4194304 | tf_op jit(solution)/shard_map/all_to_all | solution.py:164
  74.1 6.0 %collective-permute-start.7 = (f32[8,4,2,8,128]{4,3,2,1,0:T(8,128)S(1)}, f32[8,4,2,8,128]{4,3,2,1,0:T(8,128)}, u32[]{:S(2)}, u32[]{:S(2)}) collective-permute-start(f32[8,4,2,8,128]{4,3,2,1,0:T(8,128)S(1)} %copy-done.6), channel_id=1, source_target_pairs={{0,1},{1,0},{2,3},{3,2},{4,5},{5,4},{6,7},{7,6},{8,9},{9,8},{10,11... | collective-permute-start | bytes 786440 | tf_op jit(solution)/shard_map/ppermute | solution.py:159
  74.2 9.3 %collective-permute-start.8 = (f32[8,4,2,8,128]{4,3,2,1,0:T(8,128)S(1)}, f32[8,4,2,8,128]{4,3,2,1,0:T(8,128)}, u32[]{:S(2)}, u32[]{:S(2)}) collective-permute-start(f32[8,4,2,8,128]{4,3,2,1,0:T(8,128)S(1)} %copy-done.5), channel_id=1, source_target_pairs={{0,2},{1,3},{2,4},{3,5},{4,6},{5,7},{6,0},{7,1},{8,10},{9,11},{10,... | collective-permute-start | bytes 786440 | tf_op jit(solution)/shard_map/ppermute | solution.py:159
  75.8 12.3 %collective-permute-start.9 = (f32[8,4,2,8,128]{4,3,2,1,0:T(8,128)S(1)}, f32[8,4,2,8,128]{4,3,2,1,0:T(8,128)}, u32[]{:S(2)}, u32[]{:S(2)}) collective-permute-start(f32[8,4,2,8,128]{4,3,2,1,0:T(8,128)S(1)} %copy-done.4), channel_id=1, source_target_pairs={{0,3},{1,2},{2,5},{3,4},{4,7},{5,6},{6,1},{7,0},{8,11},{9,10},{10,... | collective-permute-start | bytes 786440 | tf_op jit(solution)/shard_map/ppermute | solution.py:159
  76.9 11.3 %collective-permute-start.10 = (f32[8,4,2,8,128]{4,3,2,1,0:T(8,128)S(1)}, f32[8,4,2,8,128]{4,3,2,1,0:T(8,128)}, u32[]{:S(2)}, u32[]{:S(2)}) collective-permute-start(f32[8,4,2,8,128]{4,3,2,1,0:T(8,128)S(1)} %copy-done.3), channel_id=1, source_target_pairs={{0,4},{1,5},{2,6},{3,7},{4,0},{5,1},{6,2},{7,3},{8,12},{9,13},{10,... | collective-permute-start | bytes 786440 | tf_op jit(solution)/shard_map/ppermute | solution.py:159
  78.1 14.1 %collective-permute-start.11 = (f32[8,4,2,8,128]{4,3,2,1,0:T(8,128)S(1)}, f32[8,4,2,8,128]{4,3,2,1,0:T(8,128)}, u32[]{:S(2)}, u32[]{:S(2)}) collective-permute-start(f32[8,4,2,8,128]{4,3,2,1,0:T(8,128)S(1)} %copy-done.2), channel_id=1, source_target_pairs={{0,5},{1,4},{2,7},{3,6},{4,1},{5,0},{6,3},{7,2},{8,13},{9,12},{10,... | collective-permute-start | bytes 786440 | tf_op jit(solution)/shard_map/ppermute | solution.py:159
  80.1 18.2 %collective-permute-start.12 = (f32[8,4,2,8,128]{4,3,2,1,0:T(8,128)S(1)}, f32[8,4,2,8,128]{4,3,2,1,0:T(8,128)}, u32[]{:S(2)}, u32[]{:S(2)}) collective-permute-start(f32[8,4,2,8,128]{4,3,2,1,0:T(8,128)S(1)} %copy-done.1), channel_id=1, source_target_pairs={{0,6},{1,7},{2,0},{3,1},{4,2},{5,3},{6,4},{7,5},{8,14},{9,15},{10,... | collective-permute-start | bytes 786440 | tf_op jit(solution)/shard_map/ppermute | solution.py:159
  83.5 20.4 %collective-permute-start.13 = (f32[8,4,2,8,128]{4,3,2,1,0:T(8,128)S(1)}, f32[8,4,2,8,128]{4,3,2,1,0:T(8,128)}, u32[]{:S(2)}, u32[]{:S(2)}) collective-permute-start(f32[8,4,2,8,128]{4,3,2,1,0:T(8,128)S(1)} %copy-done), channel_id=1, source_target_pairs={{0,7},{1,6},{2,1},{3,0},{4,3},{5,2},{6,5},{7,4},{8,15},{9,14},{10,... | collective-permute-start | bytes 786440 | tf_op jit(solution)/shard_map/ppermute | solution.py:159

commit v5 on v3

--- a/solution.py
+++ b/solution.py
@@ -16,6 +16,7 @@
 TILE = (8, 128)
 F32 = jnp.float32
 MIB = 1 << 20
+WHOLE = 64 * MIB - MIB // 4
 
 
 def tiles(value):
@@ -24,9 +25,8 @@
     return jnp.swapaxes(value, -3, -2)
 
 
-def call(body, ins, outs, scalars, scratch, sems, limit=64 * MIB - MIB // 4):
-    smem = pl.BlockSpec(memory_space=pltpu.SMEM)
-    hbm = pl.BlockSpec(memory_space=pltpu.HBM)
+def call(body, ins, outs, scalars, scratch, sems, limit):
+    smem, hbm = (pl.BlockSpec(memory_space=m) for m in (pltpu.SMEM, pltpu.HBM))
     moved = 4 * (sum(a.size for a in ins[scalars:]) + sum(math.prod(s) for s in outs))
     return pl.pallas_call(
         body,
@@ -75,12 +75,12 @@
 def mix_kernel(me_ref, old_ref, new_ref, pm_ref, steps_ref, r_ref, *refs):
     me = me_ref[0]
     bases, averages, out = refs[:NYC], refs[NYC : 2 * NYC], refs[2 * NYC]
-    r_buf, b_buf, a_buf, o_buf, sem = refs[2 * NYC + 1 :]
+    r_buf, b_buf, o_buf, a_buf, sem = refs[2 * NYC + 1 :]
     copy = pltpu.make_async_copy
     rows = [ahead(me, d) for d in range(NYC)]
     opposite = [((NY - d // NC) % NY) * NC + d % NC for d in range(NYC)]
     rs = [copy(r_ref.at[:, :, rows[d]], r_buf.at[d], sem.at[0, d]) for d in range(NYC)]
-    bs = [copy(bases[opposite[d]], b_buf.at[d], sem.at[1, d]) for d in range(NYC)]
+    bs = [copy(bases[opposite[d]], b_buf.at[d], sem.at[3, d]) for d in range(NYC)]
     for d in range(NYC):
         started([rs[d], bs[d]])
     islands = steps_ref.shape[0]
@@ -95,19 +95,17 @@
         weights.append(splat(steps_ref[j]) / splat(jnp.maximum(total, 1)))
     back = []
     for d in range(NYC):
-        a_buf[d] = jnp.zeros(a_buf.shape[1:], F32)
+        avg = a_buf.at[d]
+        avg[...] = jnp.zeros(avg.shape, F32)
         rs[d].wait()
         for j in range(islands):
-            a_buf[d, old[j]] += weights[j] * r_buf[d, j]
+            avg[old[j]] += weights[j] * r_buf[d, j]
         bs[d].wait()
         for j in range(islands):
-            o_buf[d, j] = b_buf[d, new[j]] - (0.7 * 1.9) * a_buf[d, new[j]]
-        back += started(
-            [
-                copy(o_buf.at[d], out.at[:, :, rows[d]], sem.at[2, d]),
-                copy(a_buf.at[d], averages[d], sem.at[3, d]),
-            ]
-        )
+            o_buf[d, j] = b_buf[d, new[j]] - (0.7 * 1.9) * avg[new[j]]
+        back += started([copy(o_buf.at[d], out.at[:, :, rows[d]], sem.at[1, d])])
+    for d in range(NYC):
+        back += started([copy(a_buf.at[d], averages[d], sem.at[2, d])])
     for done in back:
         done.wait()
 
@@ -145,17 +143,6 @@
         done.wait()
 
 
-def place_kernel(src, out, sem):
-    step = src.shape[0] // NYC
-    for done in started(
-        [
-            pltpu.make_async_copy(src.at[pl.ds(d * step, step)], out.at[pl.ds(d * step, step)], sem.at[0, d])
-            for d in range(NYC)
-        ]
-    ):
-        done.wait()
-
-
 def along_yc(pieces):
     got = [pieces[0]] + [None] * (NYC - 1)
     for d in SHIFTS:
@@ -163,7 +150,7 @@
     return got
 
 
-def across_xz(value):
+def across(value):
     return lax.all_to_all(value, XZ, split_axis=0, concat_axis=0, tiled=True)
 
 
@@ -175,9 +162,9 @@
     m = tiles(master).reshape(owner)
     v = tiles(momentum).reshape(owner)
 
-    got = across_xz(deltas[0].reshape(32, 64, 256))
+    got = across(deltas[0].reshape(32, 64, 256))
     slots = (NYC, *piece)
-    base = along_yc(call(base_kernel, [me, m, v], [piece] * NYC, 1, [slots] * 2, 3))
+    base = along_yc(call(base_kernel, [me, m, v], [piece] * NYC, 1, [slots] * 2, 3, WHOLE))
     isles = (8, 4, NYC, 2, *TILE)
     *avg, out = call(
         mix_kernel,
@@ -186,12 +173,12 @@
         5,
         [slots] * 4,
         4,
+        WHOLE,
     )
     out = jnp.swapaxes(out.reshape(32, NYC, 2, *TILE), 2, 3).reshape(32, 64, 256)
-    landed = across_xz(out)
-    nm, nv = call(owner_kernel, [me, m, v, *along_yc(avg)], [owner] * 2, 1, [slots] * 3, 5)
-    [new_module] = call(place_kernel, [landed], [landed.shape], 0, [], 1)
-    new_module = new_module.reshape(deltas.shape)
+    landed = across(out)
+    nm, nv = call(owner_kernel, [me, m, v, *along_yc(avg)], [owner] * 2, 1, [slots] * 3, 5, 61 * MIB)
+    new_module = landed.reshape(deltas.shape)
 
     def whole(value):
         return jnp.swapaxes(value.reshape(modules, 64, *TILE), 1, 2).reshape(master.shape)

time: 188 us -> 125 us (0.66)
  Pallas kernels: 77.5 us -> 13.2 us
    pallas_call x4 -> x3, Pallas kernels: 77.5 us -> 13.2 us  [call(): pl.pallas_call(body, out_shape=[jax.ShapeDtypeStruct(s, F32) for s in out...]
  transfers between devices with their start and end apart: 16 -> 16, of which waited for: 12 -> 12; matrix products, arithmetic and copies ran while one was open for 0% -> 0% of each run, Pallas kernels for 4% -> 7%
where the time goes in v5:
time: 125 us; the launch traced here: 124 us
  waiting for transfers between devices  76.8 us (61%)
  starting transfers between devices  32.3 us (26%)
  Pallas kernels  13.2 us (11%)
  local copies, waits for them, and re-layouts  1.33 us (1%)
    ppermute x14, waiting for transfers between devices, along_yc(): got[d] = lax.ppermute(pieces[d], YC, [(i, ahead(i, d)) for i in range(NYC)])  45.4 us
    all_to_all x2, waiting for transfers between devices, across(): return lax.all_to_all(value, XZ, split_axis=0, concat_axis=0, tiled=True)  31.4 us
    all_to_all x2, starting transfers between devices, across(): return lax.all_to_all(value, XZ, split_axis=0, concat_axis=0, tiled=True)  17.7 us
    ppermute x14, starting transfers between devices, along_yc(): got[d] = lax.ppermute(pieces[d], YC, [(i, ahead(i, d)) for i in range(NYC)])  14.6 us
    pallas_call x3, Pallas kernels, call(): pl.pallas_call(body, out_shape=[jax.ShapeDtypeStruct(s, F32) for s in out...  13.2 us
  transfers between devices with their start and end apart: 16, of which 12 were waited for; matrix products, arithmetic and copies ran while one was open for 0% of the time, Pallas kernels for 7%

profile of v5, /device:TPU:8, one launch (start us, length us, event | category | flops | bytes accessed | tf_op | source)
XLA Modules:
  0.0 124.4 jit_solution(9429077605243045723)
XLA Ops:
  0.6 11.5 %all-to-all-start = ((f32[32,64,256]{2,1,0:T(8,128)}), f32[32,64,256]{2,1,0:T(8,128)}, u32[]{:S(2)}, u32[]{:S(2)}) async-start(f32[32,64,256]{2,1,0:T(8,128)} %bitcast.38), calls=%async_computation | async-start | bytes 4194304 | tf_op jit(solution)/shard_map/all_to_all | solution.py:154
  12.1 3.4 %shard_map.94 = (f32[8,4,2,8,128]{4,3,2,1,0:T(8,128)}, f32[8,4,2,8,128]{4,3,2,1,0:T(8,128)}, f32[8,4,2,8,128]{4,3,2,1,0:T(8,128)}, f32[8,4,2,8,128]{4,3,2,1,0:T(...) custom-call(s32[1]{0:T(128)} %bitcast.me_ref, ...), custom_call_target="tpu_custom_call" | custom-call | flops 6291456 | bytes 6291456 | tf_op jit(solution)/shard_map/pallas_call | solution.py:31
  15.6 1.7 %collective-permute-start.1 = (f32[8,4,2,8,128]{4,3,2,1,0:T(8,128)}, f32[8,4,2,8,128]{4,3,2,1,0:T(8,128)}, u32[]{:S(2)}, u32[]{:S(2)}) collective-permute-start(f32[8,4,2,8,128]{4,3,2,1,0:T(8,128)} %get-tuple-element.24), channel_id=1, source_target_pairs={{0,2},{1,3},{2,4},{3,5},{4,6},{5,7},{6,0},{7,1},{8,10},{9,11},{10,... | collective-permute-start | bytes 786440 | tf_op jit(solution)/shard_map/ppermute | solution.py:149
  18.3 1.2 %collective-permute-start.3 = (f32[8,4,2,8,128]{4,3,2,1,0:T(8,128)}, f32[8,4,2,8,128]{4,3,2,1,0:T(8,128)}, u32[]{:S(2)}, u32[]{:S(2)}) collective-permute-start(f32[8,4,2,8,128]{4,3,2,1,0:T(8,128)} %get-tuple-element.26), channel_id=1, source_target_pairs={{0,4},{1,5},{2,6},{3,7},{4,0},{5,1},{6,2},{7,3},{8,12},{9,13},{10,... | collective-permute-start | bytes 786440 | tf_op jit(solution)/shard_map/ppermute | solution.py:149
  19.6 2.0 %collective-permute-start.4 = (f32[8,4,2,8,128]{4,3,2,1,0:T(8,128)}, f32[8,4,2,8,128]{4,3,2,1,0:T(8,128)}, u32[]{:S(2)}, u32[]{:S(2)}) collective-permute-start(f32[8,4,2,8,128]{4,3,2,1,0:T(8,128)} %get-tuple-element.27), channel_id=1, source_target_pairs={{0,5},{1,4},{2,7},{3,6},{4,1},{5,0},{6,3},{7,2},{8,13},{9,12},{10,... | collective-permute-start | bytes 786440 | tf_op jit(solution)/shard_map/ppermute | solution.py:149
  22.3 2.9 %collective-permute-done.1.refs_2_ = f32[8,4,2,8,128]{4,3,2,1,0:T(8,128)} collective-permute-done((f32[8,4,2,8,128]{4,3,2,1,0:T(8,128)}, f32[8,4,2,8,128]{4,3,2,1,0:T(8,128)}, u32[]{:S(2)}, u32[]{:S(2)}) %collective-permute-start.1) | collective-permute-done | bytes 262176 | tf_op jit(solution)/shard_map/ppermute | solution.py:149
  25.7 4.1 %collective-permute-done.2.refs_3_ = f32[8,4,2,8,128]{4,3,2,1,0:T(8,128)} collective-permute-done((f32[8,4,2,8,128]{4,3,2,1,0:T(8,128)}, f32[8,4,2,8,128]{4,3,2,1,0:T(8,128)}, u32[]{:S(2)}, u32[]{:S(2)}) %collective-permute-start.2) | collective-permute-done | bytes 262176 | tf_op jit(solution)/shard_map/ppermute | solution.py:149
  29.8 4.0 %collective-permute-done.4.refs_5_ = f32[8,4,2,8,128]{4,3,2,1,0:T(8,128)} collective-permute-done((f32[8,4,2,8,128]{4,3,2,1,0:T(8,128)}, f32[8,4,2,8,128]{4,3,2,1,0:T(8,128)}, u32[]{:S(2)}, u32[]{:S(2)}) %collective-permute-start.4) | collective-permute-done | bytes 262176 | tf_op jit(solution)/shard_map/ppermute | solution.py:149
  33.9 6.1 %collective-permute-done.5.refs_6_ = f32[8,4,2,8,128]{4,3,2,1,0:T(8,128)} collective-permute-done((f32[8,4,2,8,128]{4,3,2,1,0:T(8,128)}, f32[8,4,2,8,128]{4,3,2,1,0:T(8,128)}, u32[]{:S(2)}, u32[]{:S(2)}) %collective-permute-start.5) | collective-permute-done | bytes 262176 | tf_op jit(solution)/shard_map/ppermute | solution.py:149
  40.0 5.5 %collective-permute-done.6.refs_7_ = f32[8,4,2,8,128]{4,3,2,1,0:T(8,128)} collective-permute-done((f32[8,4,2,8,128]{4,3,2,1,0:T(8,128)}, f32[8,4,2,8,128]{4,3,2,1,0:T(8,128)}, u32[]{:S(2)}, u32[]{:S(2)}) %collective-permute-start.6) | collective-permute-done | bytes 262176 | tf_op jit(solution)/shard_map/ppermute | solution.py:149
  45.5 16.6 %all-to-all-done = f32[32,64,256]{2,1,0:T(8,128)} async-done(((f32[32,64,256]{2,1,0:T(8,128)}), f32[32,64,256]{2,1,0:T(8,128)}, u32[]{:S(2)}, u32[]{:S(2)}) %all-to-all-start) | async-done | bytes 2097184 | tf_op jit(solution)/shard_map/all_to_all | solution.py:154
  62.1 4.9 %shard_map.95 = (f32[8,4,2,8,128]{4,3,2,1,0:T(8,128)}, f32[8,4,2,8,128]{4,3,2,1,0:T(8,128)}, f32[8,4,2,8,128]{4,3,2,1,0:T(8,128)}, f32[8,4,2,8,128]{4,3,2,1,0:T(...) custom-call(s32[1]{0:T(128)} %bitcast.me_ref, ...), custom_call_target="tpu_custom_call" | custom-call | flops 8388608 | bytes 8388608 | tf_op jit(solution)/shard_map/pallas_call | solution.py:31
  67.0 6.3 %all-to-all-start.1 = ((f32[32,64,256]{2,1,0:T(8,128)}), f32[32,64,256]{2,1,0:T(8,128)S(1)}, u32[]{:S(2)}, u32[]{:S(2)}) async-start(f32[32,64,256]{2,1,0:T(8,128)} %bitcast.39), calls=%async_computation.1 | async-start | bytes 4194304 | tf_op jit(solution)/shard_map/all_to_all | solution.py:154
  73.4 1.7 %collective-permute-start.8 = (f32[8,4,2,8,128]{4,3,2,1,0:T(8,128)}, f32[8,4,2,8,128]{4,3,2,1,0:T(8,128)S(1)}, u32[]{:S(2)}, u32[]{:S(2)}) collective-permute-start(f32[8,4,2,8,128]{4,3,2,1,0:T(8,128)} %get-tuple-element.32), channel_id=1, source_target_pairs={{0,2},{1,3},{2,4},{3,5},{4,6},{5,7},{6,0},{7,1},{8,10},{9,11},{10,... | collective-permute-start | bytes 786440 | tf_op jit(solution)/shard_map/ppermute | solution.py:149
  76.1 1.2 %collective-permute-start.10 = (f32[8,4,2,8,128]{4,3,2,1,0:T(8,128)}, f32[8,4,2,8,128]{4,3,2,1,0:T(8,128)}, u32[]{:S(2)}, u32[]{:S(2)}) collective-permute-start(f32[8,4,2,8,128]{4,3,2,1,0:T(8,128)} %get-tuple-element.34), channel_id=1, source_target_pairs={{0,4},{1,5},{2,6},{3,7},{4,0},{5,1},{6,2},{7,3},{8,12},{9,13},{10,... | collective-permute-start | bytes 786440 | tf_op jit(solution)/shard_map/ppermute | solution.py:149
  77.3 2.0 %collective-permute-start.11 = (f32[8,4,2,8,128]{4,3,2,1,0:T(8,128)}, f32[8,4,2,8,128]{4,3,2,1,0:T(8,128)}, u32[]{:S(2)}, u32[]{:S(2)}) collective-permute-start(f32[8,4,2,8,128]{4,3,2,1,0:T(8,128)} %get-tuple-element.35), channel_id=1, source_target_pairs={{0,5},{1,4},{2,7},{3,6},{4,1},{5,0},{6,3},{7,2},{8,13},{9,12},{10,... | collective-permute-start | bytes 786440 | tf_op jit(solution)/shard_map/ppermute | solution.py:149
  80.0 2.7 %collective-permute-done.8.refs_2_ = f32[8,4,2,8,128]{4,3,2,1,0:T(8,128)S(1)} collective-permute-done((f32[8,4,2,8,128]{4,3,2,1,0:T(8,128)}, f32[8,4,2,8,128]{4,3,2,1,0:T(8,128)S(1)}, u32[]{:S(2)}, u32[]{:S(2)}) %collective-permute-start.8) | collective-permute-done | bytes 262176 | tf_op jit(solution)/shard_map/ppermute | solution.py:149
  83.3 4.2 %collective-permute-done.9.refs_3_ = f32[8,4,2,8,128]{4,3,2,1,0:T(8,128)S(1)} collective-permute-done((f32[8,4,2,8,128]{4,3,2,1,0:T(8,128)}, f32[8,4,2,8,128]{4,3,2,1,0:T(8,128)S(1)}, u32[]{:S(2)}, u32[]{:S(2)}) %collective-permute-start.9) | collective-permute-done | bytes 262176 | tf_op jit(solution)/shard_map/ppermute | solution.py:149
  87.6 4.0 %collective-permute-done.11.refs_5_ = f32[8,4,2,8,128]{4,3,2,1,0:T(8,128)} collective-permute-done((f32[8,4,2,8,128]{4,3,2,1,0:T(8,128)}, f32[8,4,2,8,128]{4,3,2,1,0:T(8,128)}, u32[]{:S(2)}, u32[]{:S(2)}) %collective-permute-start.11) | collective-permute-done | bytes 262176 | tf_op jit(solution)/shard_map/ppermute | solution.py:149
  91.6 6.1 %collective-permute-done.12.refs_6_ = f32[8,4,2,8,128]{4,3,2,1,0:T(8,128)} collective-permute-done((f32[8,4,2,8,128]{4,3,2,1,0:T(8,128)}, f32[8,4,2,8,128]{4,3,2,1,0:T(8,128)}, u32[]{:S(2)}, u32[]{:S(2)}) %collective-permute-start.12) | collective-permute-done | bytes 262176 | tf_op jit(solution)/shard_map/ppermute | solution.py:149
  97.7 5.5 %collective-permute-done.13.refs_7_ = f32[8,4,2,8,128]{4,3,2,1,0:T(8,128)} collective-permute-done((f32[8,4,2,8,128]{4,3,2,1,0:T(8,128)S(1)}, f32[8,4,2,8,128]{4,3,2,1,0:T(8,128)}, u32[]{:S(2)}, u32[]{:S(2)}) %collective-permute-start.13) | collective-permute-done | bytes 262176 | tf_op jit(solution)/shard_map/ppermute | solution.py:149
  103.3 5.0 %shard_map.96 = (f32[8,4,8,2,8,128]{5,4,3,2,1,0:T(8,128)}, f32[8,4,8,2,8,128]{5,4,3,2,1,0:T(8,128)}) custom-call(s32[1]{0:T(128)} %bitcast.me_ref, f32[8,4,8,2,8,128]{5,4,3,2,1,0:T(8,128)} %bitcast.34, f32[8,4,8,2,8,128]{5,4,3,2,1,0:T(8,128)} %bitcast.36, f32[8,4,2,8,128]{4,3,2,1,0:T(8,128)} %get-tuple-element.30.refs_0_, f32[8,4,2,8,128]{4,3,2,1,0:T(8,128)} %copy-done, ...), custom_call_target="tpu_custom_call" | custom-call | flops 10485760 | bytes 10485760 | tf_op jit(solution)/shard_map/pallas_call | solution.py:31
  108.2 14.8 %all-to-all-done.1 = f32[32,64,256]{2,1,0:T(8,128)S(1)} async-done(((f32[32,64,256]{2,1,0:T(8,128)}), f32[32,64,256]{2,1,0:T(8,128)S(1)}, u32[]{:S(2)}, u32[]{:S(2)}) %all-to-all-start.1) | async-done | bytes 2097184 | tf_op jit(solution)/shard_map/all_to_all | solution.py:154
  123.0 1.3 %copy.11 = f32[1,2048,256]{2,1,0:T(8,128)} copy(f32[1,2048,256]{2,1,0:T(8,128)S(1)} %bitcast.37) | data formatting | bytes 4194304
  (20 shorter events, 4.9 us)
Async XLA Ops:
  0.6 61.5 %all-to-all-start = ((f32[32,64,256]{2,1,0:T(8,128)}), f32[32,64,256]{2,1,0:T(8,128)}, u32[]{:S(2)}, u32[]{:S(2)}) async-start(f32[32,64,256]{2,1,0:T(8,128)} %bitcast.38), calls=%async_computation | async-start | bytes 4194304 | tf_op jit(solution)/shard_map/all_to_all | solution.py:154
  15.5 6.0 %collective-permute-start = (f32[8,4,2,8,128]{4,3,2,1,0:T(8,128)}, f32[8,4,2,8,128]{4,3,2,1,0:T(8,128)}, u32[]{:S(2)}, u32[]{:S(2)}) collective-permute-start(f32[8,4,2,8,128]{4,3,2,1,0:T(8,128)} %get-tuple-element.23), channel_id=1, source_target_pairs={{0,1},{1,0},{2,3},{3,2},{4,5},{5,4},{6,7},{7,6},{8,9},{9,8},{10,11... | collective-permute-start | bytes 786440 | tf_op jit(solution)/shard_map/ppermute | solution.py:149
  15.6 9.5 %collective-permute-start.1 = (f32[8,4,2,8,128]{4,3,2,1,0:T(8,128)}, f32[8,4,2,8,128]{4,3,2,1,0:T(8,128)}, u32[]{:S(2)}, u32[]{:S(2)}) collective-permute-start(f32[8,4,2,8,128]{4,3,2,1,0:T(8,128)} %get-tuple-element.24), channel_id=1, source_target_pairs={{0,2},{1,3},{2,4},{3,5},{4,6},{5,7},{6,0},{7,1},{8,10},{9,11},{10,... | collective-permute-start | bytes 786440 | tf_op jit(solution)/shard_map/ppermute | solution.py:149
  17.3 12.5 %collective-permute-start.2 = (f32[8,4,2,8,128]{4,3,2,1,0:T(8,128)}, f32[8,4,2,8,128]{4,3,2,1,0:T(8,128)}, u32[]{:S(2)}, u32[]{:S(2)}) collective-permute-start(f32[8,4,2,8,128]{4,3,2,1,0:T(8,128)} %get-tuple-element.25), channel_id=1, source_target_pairs={{0,3},{1,2},{2,5},{3,4},{4,7},{5,6},{6,1},{7,0},{8,11},{9,10},{10,... | collective-permute-start | bytes 786440 | tf_op jit(solution)/shard_map/ppermute | solution.py:149
  18.3 11.5 %collective-permute-start.3 = (f32[8,4,2,8,128]{4,3,2,1,0:T(8,128)}, f32[8,4,2,8,128]{4,3,2,1,0:T(8,128)}, u32[]{:S(2)}, u32[]{:S(2)}) collective-permute-start(f32[8,4,2,8,128]{4,3,2,1,0:T(8,128)} %get-tuple-element.26), channel_id=1, source_target_pairs={{0,4},{1,5},{2,6},{3,7},{4,0},{5,1},{6,2},{7,3},{8,12},{9,13},{10,... | collective-permute-start | bytes 786440 | tf_op jit(solution)/shard_map/ppermute | solution.py:149
  19.6 14.3 %collective-permute-start.4 = (f32[8,4,2,8,128]{4,3,2,1,0:T(8,128)}, f32[8,4,2,8,128]{4,3,2,1,0:T(8,128)}, u32[]{:S(2)}, u32[]{:S(2)}) collective-permute-start(f32[8,4,2,8,128]{4,3,2,1,0:T(8,128)} %get-tuple-element.27), channel_id=1, source_target_pairs={{0,5},{1,4},{2,7},{3,6},{4,1},{5,0},{6,3},{7,2},{8,13},{9,12},{10,... | collective-permute-start | bytes 786440 | tf_op jit(solution)/shard_map/ppermute | solution.py:149
  21.5 18.5 %collective-permute-start.5 = (f32[8,4,2,8,128]{4,3,2,1,0:T(8,128)}, f32[8,4,2,8,128]{4,3,2,1,0:T(8,128)}, u32[]{:S(2)}, u32[]{:S(2)}) collective-permute-start(f32[8,4,2,8,128]{4,3,2,1,0:T(8,128)} %get-tuple-element.28), channel_id=1, source_target_pairs={{0,6},{1,7},{2,0},{3,1},{4,2},{5,3},{6,4},{7,5},{8,14},{9,15},{10,... | collective-permute-start | bytes 786440 | tf_op jit(solution)/shard_map/ppermute | solution.py:149
  25.1 20.4 %collective-permute-start.6 = (f32[8,4,2,8,128]{4,3,2,1,0:T(8,128)}, f32[8,4,2,8,128]{4,3,2,1,0:T(8,128)}, u32[]{:S(2)}, u32[]{:S(2)}) collective-permute-start(f32[8,4,2,8,128]{4,3,2,1,0:T(8,128)} %get-tuple-element.29), channel_id=1, source_target_pairs={{0,7},{1,6},{2,1},{3,0},{4,3},{5,2},{6,5},{7,4},{8,15},{9,14},{10,... | collective-permute-start | bytes 786440 | tf_op jit(solution)/shard_map/ppermute | solution.py:149
  67.0 15.8 %copy-start.3 = (f32[8,4,2,8,128]{4,3,2,1,0:T(8,128)S(1)}, f32[8,4,2,8,128]{4,3,2,1,0:T(8,128)}, u32[]{:S(2)}) copy-start(f32[8,4,2,8,128]{4,3,2,1,0:T(8,128)} %get-tuple-element.37) | copy-start | bytes 786436
  67.0 56.0 %all-to-all-start.1 = ((f32[32,64,256]{2,1,0:T(8,128)}), f32[32,64,256]{2,1,0:T(8,128)S(1)}, u32[]{:S(2)}, u32[]{:S(2)}) async-start(f32[32,64,256]{2,1,0:T(8,128)} %bitcast.39), calls=%async_computation.1 | async-start | bytes 4194304 | tf_op jit(solution)/shard_map/all_to_all | solution.py:154
  73.3 6.0 %collective-permute-start.7 = (f32[8,4,2,8,128]{4,3,2,1,0:T(8,128)}, f32[8,4,2,8,128]{4,3,2,1,0:T(8,128)S(1)}, u32[]{:S(2)}, u32[]{:S(2)}) collective-permute-start(f32[8,4,2,8,128]{4,3,2,1,0:T(8,128)} %get-tuple-element.31), channel_id=1, source_target_pairs={{0,1},{1,0},{2,3},{3,2},{4,5},{5,4},{6,7},{7,6},{8,9},{9,8},{10,11... | collective-permute-start | bytes 786440 | tf_op jit(solution)/shard_map/ppermute | solution.py:149
  73.4 9.4 %collective-permute-start.8 = (f32[8,4,2,8,128]{4,3,2,1,0:T(8,128)}, f32[8,4,2,8,128]{4,3,2,1,0:T(8,128)S(1)}, u32[]{:S(2)}, u32[]{:S(2)}) collective-permute-start(f32[8,4,2,8,128]{4,3,2,1,0:T(8,128)} %get-tuple-element.32), channel_id=1, source_target_pairs={{0,2},{1,3},{2,4},{3,5},{4,6},{5,7},{6,0},{7,1},{8,10},{9,11},{10,... | collective-permute-start | bytes 786440 | tf_op jit(solution)/shard_map/ppermute | solution.py:149
  75.0 12.5 %collective-permute-start.9 = (f32[8,4,2,8,128]{4,3,2,1,0:T(8,128)}, f32[8,4,2,8,128]{4,3,2,1,0:T(8,128)S(1)}, u32[]{:S(2)}, u32[]{:S(2)}) collective-permute-start(f32[8,4,2,8,128]{4,3,2,1,0:T(8,128)} %get-tuple-element.33), channel_id=1, source_target_pairs={{0,3},{1,2},{2,5},{3,4},{4,7},{5,6},{6,1},{7,0},{8,11},{9,10},{10,... | collective-permute-start | bytes 786440 | tf_op jit(solution)/shard_map/ppermute | solution.py:149
  76.1 11.5 %collective-permute-start.10 = (f32[8,4,2,8,128]{4,3,2,1,0:T(8,128)}, f32[8,4,2,8,128]{4,3,2,1,0:T(8,128)}, u32[]{:S(2)}, u32[]{:S(2)}) collective-permute-start(f32[8,4,2,8,128]{4,3,2,1,0:T(8,128)} %get-tuple-element.34), channel_id=1, source_target_pairs={{0,4},{1,5},{2,6},{3,7},{4,0},{5,1},{6,2},{7,3},{8,12},{9,13},{10,... | collective-permute-start | bytes 786440 | tf_op jit(solution)/shard_map/ppermute | solution.py:149
  77.3 14.3 %collective-permute-start.11 = (f32[8,4,2,8,128]{4,3,2,1,0:T(8,128)}, f32[8,4,2,8,128]{4,3,2,1,0:T(8,128)}, u32[]{:S(2)}, u32[]{:S(2)}) collective-permute-start(f32[8,4,2,8,128]{4,3,2,1,0:T(8,128)} %get-tuple-element.35), channel_id=1, source_target_pairs={{0,5},{1,4},{2,7},{3,6},{4,1},{5,0},{6,3},{7,2},{8,13},{9,12},{10,... | collective-permute-start | bytes 786440 | tf_op jit(solution)/shard_map/ppermute | solution.py:149
  79.3 24.0 %copy-start = (f32[8,4,2,8,128]{4,3,2,1,0:T(8,128)}, f32[8,4,2,8,128]{4,3,2,1,0:T(8,128)S(1)}, u32[]{:S(2)}) copy-start(f32[8,4,2,8,128]{4,3,2,1,0:T(8,128)S(1)} %collective-permute-done.7.refs_1_) | copy-start | bytes 786436
  79.3 18.4 %collective-permute-start.12 = (f32[8,4,2,8,128]{4,3,2,1,0:T(8,128)}, f32[8,4,2,8,128]{4,3,2,1,0:T(8,128)}, u32[]{:S(2)}, u32[]{:S(2)}) collective-permute-start(f32[8,4,2,8,128]{4,3,2,1,0:T(8,128)} %get-tuple-element.36), channel_id=1, source_target_pairs={{0,6},{1,7},{2,0},{3,1},{4,2},{5,3},{6,4},{7,5},{8,14},{9,15},{10,... | collective-permute-start | bytes 786440 | tf_op jit(solution)/shard_map/ppermute | solution.py:149
  82.8 20.5 %copy-start.1 = (f32[8,4,2,8,128]{4,3,2,1,0:T(8,128)}, f32[8,4,2,8,128]{4,3,2,1,0:T(8,128)S(1)}, u32[]{:S(2)}) copy-start(f32[8,4,2,8,128]{4,3,2,1,0:T(8,128)S(1)} %collective-permute-done.8.refs_2_) | copy-start | bytes 786436
  82.8 20.5 %collective-permute-start.13 = (f32[8,4,2,8,128]{4,3,2,1,0:T(8,128)S(1)}, f32[8,4,2,8,128]{4,3,2,1,0:T(8,128)}, u32[]{:S(2)}, u32[]{:S(2)}) collective-permute-start(f32[8,4,2,8,128]{4,3,2,1,0:T(8,128)S(1)} %copy-done.3), channel_id=1, source_target_pairs={{0,7},{1,6},{2,1},{3,0},{4,3},{5,2},{6,5},{7,4},{8,15},{9,14},{10,... | collective-permute-start | bytes 786440 | tf_op jit(solution)/shard_map/ppermute | solution.py:149
  87.6 15.7 %copy-start.2 = (f32[8,4,2,8,128]{4,3,2,1,0:T(8,128)}, f32[8,4,2,8,128]{4,3,2,1,0:T(8,128)S(1)}, u32[]{:S(2)}) copy-start(f32[8,4,2,8,128]{4,3,2,1,0:T(8,128)S(1)} %collective-permute-done.9.refs_3_) | copy-start | bytes 786436

commit v6 on v5

--- a/solution.py
+++ b/solution.py
@@ -25,14 +25,14 @@
     return jnp.swapaxes(value, -3, -2)
 
 
-def call(body, ins, outs, scalars, scratch, sems, limit):
-    smem, hbm = (pl.BlockSpec(memory_space=m) for m in (pltpu.SMEM, pltpu.HBM))
+def call(body, ins, outs, scalars, scratch, sems, limit, near_in=(), near_out=()):
+    smem, vmem, hbm = (pl.BlockSpec(memory_space=m) for m in (pltpu.SMEM, pltpu.VMEM, pltpu.HBM))
     moved = 4 * (sum(a.size for a in ins[scalars:]) + sum(math.prod(s) for s in outs))
     return pl.pallas_call(
         body,
         out_shape=[jax.ShapeDtypeStruct(s, F32) for s in outs],
-        in_specs=[smem] * scalars + [hbm] * (len(ins) - scalars),
-        out_specs=[hbm] * len(outs),
+        in_specs=[smem] * scalars + [vmem if i in near_in else hbm for i in range(scalars, len(ins))],
+        out_specs=[vmem if i in near_out else hbm for i in range(len(outs))],
         scratch_shapes=[pltpu.VMEM(s, F32) for s in scratch] + [pltpu.SemaphoreType.DMA((sems, NYC))],
         cost_estimate=pl.CostEstimate(flops=moved, bytes_accessed=moved, transcendentals=0),
         compiler_params=pltpu.CompilerParams(vmem_limit_bytes=limit),
@@ -72,20 +72,9 @@
         done.wait()
 
 
-def mix_kernel(me_ref, old_ref, new_ref, pm_ref, steps_ref, r_ref, *refs):
-    me = me_ref[0]
-    bases, averages, out = refs[:NYC], refs[NYC : 2 * NYC], refs[2 * NYC]
-    r_buf, b_buf, o_buf, a_buf, sem = refs[2 * NYC + 1 :]
-    copy = pltpu.make_async_copy
-    rows = [ahead(me, d) for d in range(NYC)]
-    opposite = [((NY - d // NC) % NY) * NC + d % NC for d in range(NYC)]
-    rs = [copy(r_ref.at[:, :, rows[d]], r_buf.at[d], sem.at[0, d]) for d in range(NYC)]
-    bs = [copy(bases[opposite[d]], b_buf.at[d], sem.at[3, d]) for d in range(NYC)]
-    for d in range(NYC):
-        started([rs[d], bs[d]])
+def weigh(old_ref, pm_ref, steps_ref):
     islands = steps_ref.shape[0]
     old = [pm_ref[old_ref[j]] for j in range(islands)]
-    new = [pm_ref[new_ref[j]] for j in range(islands)]
     weights = []
     for j in range(islands):
         total = jnp.int32(0)
@@ -93,19 +82,51 @@
             total += jnp.where(old[i] == old[j], steps_ref[i], 0)
         splat = lambda s: jnp.full(TILE, s, jnp.int32).astype(F32)
         weights.append(splat(steps_ref[j]) / splat(jnp.maximum(total, 1)))
+    return list(zip(old, weights))
+
+
+def add_up(avg, deltas, weighted):
+    avg[...] = jnp.zeros(avg.shape, F32)
+    for j, (k, w) in enumerate(weighted):
+        avg[k] += w * deltas[j]
+
+
+def hold_kernel(src, out, sem):
+    out[...] = src[...]
+
+
+def pick_kernel(me_ref, old_ref, new_ref, pm_ref, steps_ref, r_ref, *refs):
+    me = me_ref[0]
+    bases, (out, r_buf, o_buf, avg, sem) = refs[:NYC], refs[NYC:]
+    copy = pltpu.make_async_copy
+    rows = [behind(me, d) for d in range(NYC)]
+    rs = started([copy(r_ref.at[:, :, rows[d]], r_buf.at[d], sem.at[0, d]) for d in range(NYC)])
+    weighted = weigh(old_ref, pm_ref, steps_ref)
     back = []
     for d in range(NYC):
-        avg = a_buf.at[d]
-        avg[...] = jnp.zeros(avg.shape, F32)
         rs[d].wait()
-        for j in range(islands):
-            avg[old[j]] += weights[j] * r_buf[d, j]
-        bs[d].wait()
-        for j in range(islands):
-            o_buf[d, j] = b_buf[d, new[j]] - (0.7 * 1.9) * avg[new[j]]
+        add_up(avg, r_buf.at[d], weighted)
+        for j in range(steps_ref.shape[0]):
+            k = pm_ref[new_ref[j]]
+            o_buf[d, j] = bases[d][k] - (0.7 * 1.9) * avg[k]
         back += started([copy(o_buf.at[d], out.at[:, :, rows[d]], sem.at[1, d])])
-    for d in range(NYC):
-        back += started([copy(a_buf.at[d], averages[d], sem.at[2, d])])
+    for done in back:
+        done.wait()
+
+
+def average_kernel(me_ref, old_ref, pm_ref, steps_ref, r_ref, *refs):
+    averages, (r_buf, a_buf, sem) = refs[:NYC], refs[NYC:]
+    copy = pltpu.make_async_copy
+    rows = [ahead(me_ref[0], d) for d in range(NYC)]
+    order = (*SHIFTS, 0)
+    rs = [copy(r_ref.at[:, :, rows[d]], r_buf.at[d], sem.at[0, d]) for d in range(NYC)]
+    started([rs[d] for d in order])
+    weighted = weigh(old_ref, pm_ref, steps_ref)
+    back = []
+    for d in order:
+        rs[d].wait()
+        add_up(a_buf.at[d], r_buf.at[d], weighted)
+        back += started([copy(a_buf.at[d], averages[d], sem.at[1, d])])
     for done in back:
         done.wait()
 
@@ -165,15 +186,27 @@
     got = across(deltas[0].reshape(32, 64, 256))
     slots = (NYC, *piece)
     base = along_yc(call(base_kernel, [me, m, v], [piece] * NYC, 1, [slots] * 2, 3, WHOLE))
+    base[0:1] = call(hold_kernel, base[0:1], [piece], 0, [], 1, 4 * MIB, (0,), (0,))
     isles = (8, 4, NYC, 2, *TILE)
-    *avg, out = call(
-        mix_kernel,
-        [me, old_path, new_path, path_module, island_steps, tiles(got).reshape(isles), *base],
-        [piece] * NYC + [isles],
+    mixed = tiles(got).reshape(isles)
+    [out] = call(
+        pick_kernel,
+        [me, old_path, new_path, path_module, island_steps, mixed, *base],
+        [isles],
         5,
-        [slots] * 4,
+        [slots, slots, piece],
+        2,
+        20 * MIB,
+        range(6, 6 + NYC),
+    )
+    avg = call(
+        average_kernel,
+        [me, old_path, path_module, island_steps, mixed],
+        [piece] * NYC,
         4,
-        WHOLE,
+        [slots] * 2,
+        2,
+        61 * MIB,
     )
     out = jnp.swapaxes(out.reshape(32, NYC, 2, *TILE), 2, 3).reshape(32, 64, 256)
     landed = across(out)

time: 125 us -> 123 us (0.984)
  waiting for transfers between devices: 76.8 us -> 72.4 us
  Pallas kernels: 13.2 us -> 14.7 us
    all_to_all x2, waiting for transfers between devices: 31.4 us -> 28.3 us  [across(): return lax.all_to_all(value, XZ, split_axis=0, concat_axis=0, tiled=True)]
    pallas_call x3 -> x5, Pallas kernels: 13.2 us -> 14.7 us  [call(): pl.pallas_call(body, out_shape=[jax.ShapeDtypeStruct(s, F32) for s in out...]
    ppermute x14, waiting for transfers between devices: 45.4 us -> 44.1 us  [along_yc(): got[d] = lax.ppermute(pieces[d], YC, [(i, ahead(i, d)) for i in range(NYC)])]
  transfers between devices with their start and end apart: 16 -> 16, of which waited for: 12 -> 12; matrix products, arithmetic and copies ran while one was open for 0% -> 0% of each run, Pallas kernels for 7% -> 9%
where the time goes in v6:
time: 123 us; the launch traced here: 122 us
  waiting for transfers between devices  72.4 us (59%)
  starting transfers between devices  32.3 us (26%)
  Pallas kernels  14.7 us (12%)
  local copies, waits for them, and re-layouts  2.3 us (2%)
    ppermute x14, waiting for transfers between devices, along_yc(): got[d] = lax.ppermute(pieces[d], YC, [(i, ahead(i, d)) for i in range(NYC)])  44.1 us
    all_to_all x2, waiting for transfers between devices, across(): return lax.all_to_all(value, XZ, split_axis=0, concat_axis=0, tiled=True)  28.3 us
    all_to_all x2, starting transfers between devices, across(): return lax.all_to_all(value, XZ, split_axis=0, concat_axis=0, tiled=True)  17.6 us
    pallas_call x5, Pallas kernels, call(): pl.pallas_call(body, out_shape=[jax.ShapeDtypeStruct(s, F32) for s in out...  14.7 us
    ppermute x14, starting transfers between devices, along_yc(): got[d] = lax.ppermute(pieces[d], YC, [(i, ahead(i, d)) for i in range(NYC)])  14.7 us
  transfers between devices with their start and end apart: 16, of which 12 were waited for; matrix products, arithmetic and copies ran while one was open for 0% of the time, Pallas kernels for 9%

profile of v6, /device:TPU:8, one launch (start us, length us, event | category | flops | bytes accessed | tf_op | source)
XLA Modules:
  0.0 122.4 jit_solution(14975377521354448508)
XLA Ops:
  0.6 11.5 %all-to-all-start = ((f32[32,64,256]{2,1,0:T(8,128)}), f32[32,64,256]{2,1,0:T(8,128)}, u32[]{:S(2)}, u32[]{:S(2)}) async-start(f32[32,64,256]{2,1,0:T(8,128)} %bitcast.38), calls=%async_computation | async-start | bytes 4194304 | tf_op jit(solution)/shard_map/all_to_all | solution.py:175
  12.1 3.4 %shard_map.96 = (f32[8,4,2,8,128]{4,3,2,1,0:T(8,128)}, f32[8,4,2,8,128]{4,3,2,1,0:T(8,128)}, f32[8,4,2,8,128]{4,3,2,1,0:T(8,128)}, f32[8,4,2,8,128]{4,3,2,1,0:T(...) custom-call(s32[1]{0:T(128)} %bitcast.me_ref, ...), custom_call_target="tpu_custom_call" | custom-call | flops 6291456 | bytes 6291456 | tf_op jit(solution)/shard_map/pallas_call | solution.py:31
  15.7 1.7 %collective-permute-start.8 = (f32[8,4,2,8,128]{4,3,2,1,0:T(8,128)}, f32[8,4,2,8,128]{4,3,2,1,0:T(8,128)S(1)}, u32[]{:S(2)}, u32[]{:S(2)}) collective-permute-start(f32[8,4,2,8,128]{4,3,2,1,0:T(8,128)} %get-tuple-element.33), channel_id=1, source_target_pairs={{0,2},{1,3},{2,4},{3,5},{4,6},{5,7},{6,0},{7,1},{8,10},{9,11},{10,... | collective-permute-start | bytes 786440 | tf_op jit(solution)/shard_map/ppermute | solution.py:170
  18.4 1.2 %collective-permute-start.10 = (f32[8,4,2,8,128]{4,3,2,1,0:T(8,128)}, f32[8,4,2,8,128]{4,3,2,1,0:T(8,128)S(1)}, u32[]{:S(2)}, u32[]{:S(2)}) collective-permute-start(f32[8,4,2,8,128]{4,3,2,1,0:T(8,128)} %get-tuple-element.35), channel_id=1, source_target_pairs={{0,4},{1,5},{2,6},{3,7},{4,0},{5,1},{6,2},{7,3},{8,12},{9,13},{10,... | collective-permute-start | bytes 786440 | tf_op jit(solution)/shard_map/ppermute | solution.py:170
  19.6 2.0 %collective-permute-start.11 = (f32[8,4,2,8,128]{4,3,2,1,0:T(8,128)}, f32[8,4,2,8,128]{4,3,2,1,0:T(8,128)S(1)}, u32[]{:S(2)}, u32[]{:S(2)}) collective-permute-start(f32[8,4,2,8,128]{4,3,2,1,0:T(8,128)} %get-tuple-element.36), channel_id=1, source_target_pairs={{0,5},{1,4},{2,7},{3,6},{4,1},{5,0},{6,3},{7,2},{8,13},{9,12},{10,... | collective-permute-start | bytes 786440 | tf_op jit(solution)/shard_map/ppermute | solution.py:170
  22.3 2.7 %collective-permute-done.8.refs_2_ = f32[8,4,2,8,128]{4,3,2,1,0:T(8,128)S(1)} collective-permute-done((f32[8,4,2,8,128]{4,3,2,1,0:T(8,128)}, f32[8,4,2,8,128]{4,3,2,1,0:T(8,128)S(1)}, u32[]{:S(2)}, u32[]{:S(2)}) %collective-permute-start.8) | collective-permute-done | bytes 262176 | tf_op jit(solution)/shard_map/ppermute | solution.py:170
  26.8 3.1 %collective-permute-done.9.refs_3_ = f32[8,4,2,8,128]{4,3,2,1,0:T(8,128)S(1)} collective-permute-done((f32[8,4,2,8,128]{4,3,2,1,0:T(8,128)}, f32[8,4,2,8,128]{4,3,2,1,0:T(8,128)S(1)}, u32[]{:S(2)}, u32[]{:S(2)}) %collective-permute-start.9) | collective-permute-done | bytes 262176 | tf_op jit(solution)/shard_map/ppermute | solution.py:170
  29.9 3.9 %collective-permute-done.11.refs_5_ = f32[8,4,2,8,128]{4,3,2,1,0:T(8,128)S(1)} collective-permute-done((f32[8,4,2,8,128]{4,3,2,1,0:T(8,128)}, f32[8,4,2,8,128]{4,3,2,1,0:T(8,128)S(1)}, u32[]{:S(2)}, u32[]{:S(2)}) %collective-permute-start.11) | collective-permute-done | bytes 262176 | tf_op jit(solution)/shard_map/ppermute | solution.py:170
  33.8 6.1 %collective-permute-done.12.refs_6_ = f32[8,4,2,8,128]{4,3,2,1,0:T(8,128)S(1)} collective-permute-done((f32[8,4,2,8,128]{4,3,2,1,0:T(8,128)}, f32[8,4,2,8,128]{4,3,2,1,0:T(8,128)S(1)}, u32[]{:S(2)}, u32[]{:S(2)}) %collective-permute-start.12) | collective-permute-done | bytes 262176 | tf_op jit(solution)/shard_map/ppermute | solution.py:170
  39.9 5.5 %collective-permute-done.13.refs_7_ = f32[8,4,2,8,128]{4,3,2,1,0:T(8,128)S(1)} collective-permute-done((f32[8,4,2,8,128]{4,3,2,1,0:T(8,128)}, f32[8,4,2,8,128]{4,3,2,1,0:T(8,128)S(1)}, u32[]{:S(2)}, u32[]{:S(2)}) %collective-permute-start.13) | collective-permute-done | bytes 262176 | tf_op jit(solution)/shard_map/ppermute | solution.py:170
  45.5 16.6 %all-to-all-done = f32[32,64,256]{2,1,0:T(8,128)} async-done(((f32[32,64,256]{2,1,0:T(8,128)}), f32[32,64,256]{2,1,0:T(8,128)}, u32[]{:S(2)}, u32[]{:S(2)}) %all-to-all-start) | async-done | bytes 2097184 | tf_op jit(solution)/shard_map/all_to_all | solution.py:175
  62.1 3.1 %shard_map.98 = f32[8,4,8,2,8,128]{5,4,3,2,1,0:T(8,128)} custom-call(s32[1]{0:T(128)} %bitcast.me_ref, s32[8]{0:T(128)S(1)} %copy-done.2, s32[8]{0:T(128)S(1)} %copy-done.4, s32[256]{0:T(256)S(1)} %copy-done.1, s32[8]{0:T(128)S(1)} %copy-done.3, f32[8,4,8,2,8,128]{5,4,3,2,1,0:T(8,128)} %bitcast.10.r_ref, f32[8,4,2,8,128]{4,3,2,1,0:T(8,128)S(1)} %shard_map.97.refs_0_, ...), custom_call_target="tpu_custom_call" | custom-call | flops 6291456 | bytes 6291456 | tf_op jit(solution)/shard_map/pallas_call | solution.py:31
  65.2 6.1 %all-to-all-start.1 = ((f32[32,64,256]{2,1,0:T(8,128)}), f32[32,64,256]{2,1,0:T(8,128)S(1)}, u32[]{:S(2)}, u32[]{:S(2)}) async-start(f32[32,64,256]{2,1,0:T(8,128)} %bitcast.25), calls=%async_computation.1 | async-start | bytes 4194304 | tf_op jit(solution)/shard_map/all_to_all | solution.py:175
  71.3 3.1 %shard_map.94 = (f32[8,4,2,8,128]{4,3,2,1,0:T(8,128)}, f32[8,4,2,8,128]{4,3,2,1,0:T(8,128)}, f32[8,4,2,8,128]{4,3,2,1,0:T(8,128)}, f32[8,4,2,8,128]{4,3,2,1,0:T(...) custom-call(s32[1]{0:T(128)} %bitcast.me_ref, ...), custom_call_target="tpu_custom_call" | custom-call | flops 4194304 | bytes 4194304 | tf_op jit(solution)/shard_map/pallas_call | solution.py:31
  74.6 1.7 %collective-permute-start.1 = (f32[8,4,2,8,128]{4,3,2,1,0:T(8,128)}, f32[8,4,2,8,128]{4,3,2,1,0:T(8,128)S(1)}, u32[]{:S(2)}, u32[]{:S(2)}) collective-permute-start(f32[8,4,2,8,128]{4,3,2,1,0:T(8,128)} %get-tuple-element.23), channel_id=1, source_target_pairs={{0,2},{1,3},{2,4},{3,5},{4,6},{5,7},{6,0},{7,1},{8,10},{9,11},{10,... | collective-permute-start | bytes 786440 | tf_op jit(solution)/shard_map/ppermute | solution.py:170
  78.5 2.0 %collective-permute-start.4 = (f32[8,4,2,8,128]{4,3,2,1,0:T(8,128)}, f32[8,4,2,8,128]{4,3,2,1,0:T(8,128)}, u32[]{:S(2)}, u32[]{:S(2)}) collective-permute-start(f32[8,4,2,8,128]{4,3,2,1,0:T(8,128)} %get-tuple-element.26), channel_id=1, source_target_pairs={{0,5},{1,4},{2,7},{3,6},{4,1},{5,0},{6,3},{7,2},{8,13},{9,12},{10,... | collective-permute-start | bytes 786440 | tf_op jit(solution)/shard_map/ppermute | solution.py:170
  81.2 2.7 %collective-permute-done.1.refs_2_ = f32[8,4,2,8,128]{4,3,2,1,0:T(8,128)S(1)} collective-permute-done((f32[8,4,2,8,128]{4,3,2,1,0:T(8,128)}, f32[8,4,2,8,128]{4,3,2,1,0:T(8,128)S(1)}, u32[]{:S(2)}, u32[]{:S(2)}) %collective-permute-start.1) | collective-permute-done | bytes 262176 | tf_op jit(solution)/shard_map/ppermute | solution.py:170
  84.5 4.2 %collective-permute-done.2.refs_3_ = f32[8,4,2,8,128]{4,3,2,1,0:T(8,128)S(1)} collective-permute-done((f32[8,4,2,8,128]{4,3,2,1,0:T(8,128)}, f32[8,4,2,8,128]{4,3,2,1,0:T(8,128)S(1)}, u32[]{:S(2)}, u32[]{:S(2)}) %collective-permute-start.2) | collective-permute-done | bytes 262176 | tf_op jit(solution)/shard_map/ppermute | solution.py:170
  88.8 4.0 %collective-permute-done.4.refs_5_ = f32[8,4,2,8,128]{4,3,2,1,0:T(8,128)} collective-permute-done((f32[8,4,2,8,128]{4,3,2,1,0:T(8,128)}, f32[8,4,2,8,128]{4,3,2,1,0:T(8,128)}, u32[]{:S(2)}, u32[]{:S(2)}) %collective-permute-start.4) | collective-permute-done | bytes 262176 | tf_op jit(solution)/shard_map/ppermute | solution.py:170
  92.8 6.1 %collective-permute-done.5.refs_6_ = f32[8,4,2,8,128]{4,3,2,1,0:T(8,128)} collective-permute-done((f32[8,4,2,8,128]{4,3,2,1,0:T(8,128)}, f32[8,4,2,8,128]{4,3,2,1,0:T(8,128)}, u32[]{:S(2)}, u32[]{:S(2)}) %collective-permute-start.5) | collective-permute-done | bytes 262176 | tf_op jit(solution)/shard_map/ppermute | solution.py:170
  99.0 5.5 %collective-permute-done.6.refs_7_ = f32[8,4,2,8,128]{4,3,2,1,0:T(8,128)} collective-permute-done((f32[8,4,2,8,128]{4,3,2,1,0:T(8,128)}, f32[8,4,2,8,128]{4,3,2,1,0:T(8,128)}, u32[]{:S(2)}, u32[]{:S(2)}) %collective-permute-start.6) | collective-permute-done | bytes 262176 | tf_op jit(solution)/shard_map/ppermute | solution.py:170
  104.5 5.0 %shard_map.95 = (f32[8,4,8,2,8,128]{5,4,3,2,1,0:T(8,128)}, f32[8,4,8,2,8,128]{5,4,3,2,1,0:T(8,128)}) custom-call(s32[1]{0:T(128)} %bitcast.me_ref, f32[8,4,8,2,8,128]{5,4,3,2,1,0:T(8,128)} %bitcast.34, f32[8,4,8,2,8,128]{5,4,3,2,1,0:T(8,128)} %bitcast.36, f32[8,4,2,8,128]{4,3,2,1,0:T(8,128)} %get-tuple-element.21.refs_0_, f32[8,4,2,8,128]{4,3,2,1,0:T(8,128)} %copy-done.5, ...), custom_call_target="tpu_custom_call" | custom-call | flops 10485760 | bytes 10485760 | tf_op jit(solution)/shard_map/pallas_call | solution.py:31
  109.4 11.7 %all-to-all-done.1 = f32[32,64,256]{2,1,0:T(8,128)S(1)} async-done(((f32[32,64,256]{2,1,0:T(8,128)}), f32[32,64,256]{2,1,0:T(8,128)S(1)}, u32[]{:S(2)}, u32[]{:S(2)}) %all-to-all-start.1) | async-done | bytes 2097184 | tf_op jit(solution)/shard_map/all_to_all | solution.py:175
  121.1 1.3 %copy.11 = f32[1,2048,256]{2,1,0:T(8,128)} copy(f32[1,2048,256]{2,1,0:T(8,128)S(1)} %bitcast.37) | data formatting | bytes 4194304
  (30 shorter events, 7.3 us)
Async XLA Ops:
  0.6 61.5 %all-to-all-start = ((f32[32,64,256]{2,1,0:T(8,128)}), f32[32,64,256]{2,1,0:T(8,128)}, u32[]{:S(2)}, u32[]{:S(2)}) async-start(f32[32,64,256]{2,1,0:T(8,128)} %bitcast.38), calls=%async_computation | async-start | bytes 4194304 | tf_op jit(solution)/shard_map/all_to_all | solution.py:175
  12.1 50.0 %copy-start.1 = (s32[256]{0:T(256)S(1)}, s32[256]{0:T(256)}, u32[]{:S(2)}) copy-start(s32[256]{0:T(256)} %pm_ref.3) | copy-start | bytes 3076
  12.1 50.0 %copy-start.2 = (s32[8]{0:T(128)S(1)}, s32[8]{0:T(128)}, u32[]{:S(2)}) copy-start(s32[8]{0:T(128)} %old_ref.3) | copy-start | bytes 100
  12.1 50.0 %copy-start.3 = (s32[8]{0:T(128)S(1)}, s32[8]{0:T(128)}, u32[]{:S(2)}) copy-start(s32[8]{0:T(128)} %steps_ref.3) | copy-start | bytes 100
  12.1 50.0 %copy-start.4 = (s32[8]{0:T(128)S(1)}, s32[8]{0:T(128)}, u32[]{:S(2)}) copy-start(s32[8]{0:T(128)} %new_ref.1) | copy-start | bytes 100
  15.6 6.0 %collective-permute-start.7 = (f32[8,4,2,8,128]{4,3,2,1,0:T(8,128)}, f32[8,4,2,8,128]{4,3,2,1,0:T(8,128)S(1)}, u32[]{:S(2)}, u32[]{:S(2)}) collective-permute-start(f32[8,4,2,8,128]{4,3,2,1,0:T(8,128)} %get-tuple-element.32), channel_id=1, source_target_pairs={{0,1},{1,0},{2,3},{3,2},{4,5},{5,4},{6,7},{7,6},{8,9},{9,8},{10,11... | collective-permute-start | bytes 786440 | tf_op jit(solution)/shard_map/ppermute | solution.py:170
  15.7 9.4 %collective-permute-start.8 = (f32[8,4,2,8,128]{4,3,2,1,0:T(8,128)}, f32[8,4,2,8,128]{4,3,2,1,0:T(8,128)S(1)}, u32[]{:S(2)}, u32[]{:S(2)}) collective-permute-start(f32[8,4,2,8,128]{4,3,2,1,0:T(8,128)} %get-tuple-element.33), channel_id=1, source_target_pairs={{0,2},{1,3},{2,4},{3,5},{4,6},{5,7},{6,0},{7,1},{8,10},{9,11},{10,... | collective-permute-start | bytes 786440 | tf_op jit(solution)/shard_map/ppermute | solution.py:170
  17.3 12.5 %collective-permute-start.9 = (f32[8,4,2,8,128]{4,3,2,1,0:T(8,128)}, f32[8,4,2,8,128]{4,3,2,1,0:T(8,128)S(1)}, u32[]{:S(2)}, u32[]{:S(2)}) collective-permute-start(f32[8,4,2,8,128]{4,3,2,1,0:T(8,128)} %get-tuple-element.34), channel_id=1, source_target_pairs={{0,3},{1,2},{2,5},{3,4},{4,7},{5,6},{6,1},{7,0},{8,11},{9,10},{10,... | collective-permute-start | bytes 786440 | tf_op jit(solution)/shard_map/ppermute | solution.py:170
  18.4 11.5 %collective-permute-start.10 = (f32[8,4,2,8,128]{4,3,2,1,0:T(8,128)}, f32[8,4,2,8,128]{4,3,2,1,0:T(8,128)S(1)}, u32[]{:S(2)}, u32[]{:S(2)}) collective-permute-start(f32[8,4,2,8,128]{4,3,2,1,0:T(8,128)} %get-tuple-element.35), channel_id=1, source_target_pairs={{0,4},{1,5},{2,6},{3,7},{4,0},{5,1},{6,2},{7,3},{8,12},{9,13},{10,... | collective-permute-start | bytes 786440 | tf_op jit(solution)/shard_map/ppermute | solution.py:170
  19.6 14.2 %collective-permute-start.11 = (f32[8,4,2,8,128]{4,3,2,1,0:T(8,128)}, f32[8,4,2,8,128]{4,3,2,1,0:T(8,128)S(1)}, u32[]{:S(2)}, u32[]{:S(2)}) collective-permute-start(f32[8,4,2,8,128]{4,3,2,1,0:T(8,128)} %get-tuple-element.36), channel_id=1, source_target_pairs={{0,5},{1,4},{2,7},{3,6},{4,1},{5,0},{6,3},{7,2},{8,13},{9,12},{10,... | collective-permute-start | bytes 786440 | tf_op jit(solution)/shard_map/ppermute | solution.py:170
  21.6 18.3 %collective-permute-start.12 = (f32[8,4,2,8,128]{4,3,2,1,0:T(8,128)}, f32[8,4,2,8,128]{4,3,2,1,0:T(8,128)S(1)}, u32[]{:S(2)}, u32[]{:S(2)}) collective-permute-start(f32[8,4,2,8,128]{4,3,2,1,0:T(8,128)} %get-tuple-element.37), channel_id=1, source_target_pairs={{0,6},{1,7},{2,0},{3,1},{4,2},{5,3},{6,4},{7,5},{8,14},{9,15},{10,... | collective-permute-start | bytes 786440 | tf_op jit(solution)/shard_map/ppermute | solution.py:170
  25.1 20.4 %collective-permute-start.13 = (f32[8,4,2,8,128]{4,3,2,1,0:T(8,128)}, f32[8,4,2,8,128]{4,3,2,1,0:T(8,128)S(1)}, u32[]{:S(2)}, u32[]{:S(2)}) collective-permute-start(f32[8,4,2,8,128]{4,3,2,1,0:T(8,128)} %get-tuple-element.38), channel_id=1, source_target_pairs={{0,7},{1,6},{2,1},{3,0},{4,3},{5,2},{6,5},{7,4},{8,15},{9,14},{10,... | collective-permute-start | bytes 786440 | tf_op jit(solution)/shard_map/ppermute | solution.py:170
  25.7 0.9 copy-start
  65.2 55.9 %all-to-all-start.1 = ((f32[32,64,256]{2,1,0:T(8,128)}), f32[32,64,256]{2,1,0:T(8,128)S(1)}, u32[]{:S(2)}, u32[]{:S(2)}) async-start(f32[32,64,256]{2,1,0:T(8,128)} %bitcast.25), calls=%async_computation.1 | async-start | bytes 4194304 | tf_op jit(solution)/shard_map/all_to_all | solution.py:175
  74.5 6.0 %collective-permute-start = (f32[8,4,2,8,128]{4,3,2,1,0:T(8,128)}, f32[8,4,2,8,128]{4,3,2,1,0:T(8,128)S(1)}, u32[]{:S(2)}, u32[]{:S(2)}) collective-permute-start(f32[8,4,2,8,128]{4,3,2,1,0:T(8,128)} %get-tuple-element.22), channel_id=1, source_target_pairs={{0,1},{1,0},{2,3},{3,2},{4,5},{5,4},{6,7},{7,6},{8,9},{9,8},{10,11... | collective-permute-start | bytes 786440 | tf_op jit(solution)/shard_map/ppermute | solution.py:170
  74.6 9.4 %collective-permute-start.1 = (f32[8,4,2,8,128]{4,3,2,1,0:T(8,128)}, f32[8,4,2,8,128]{4,3,2,1,0:T(8,128)S(1)}, u32[]{:S(2)}, u32[]{:S(2)}) collective-permute-start(f32[8,4,2,8,128]{4,3,2,1,0:T(8,128)} %get-tuple-element.23), channel_id=1, source_target_pairs={{0,2},{1,3},{2,4},{3,5},{4,6},{5,7},{6,0},{7,1},{8,10},{9,11},{10,... | collective-permute-start | bytes 786440 | tf_op jit(solution)/shard_map/ppermute | solution.py:170
  76.2 12.5 %collective-permute-start.2 = (f32[8,4,2,8,128]{4,3,2,1,0:T(8,128)}, f32[8,4,2,8,128]{4,3,2,1,0:T(8,128)S(1)}, u32[]{:S(2)}, u32[]{:S(2)}) collective-permute-start(f32[8,4,2,8,128]{4,3,2,1,0:T(8,128)} %get-tuple-element.24), channel_id=1, source_target_pairs={{0,3},{1,2},{2,5},{3,4},{4,7},{5,6},{6,1},{7,0},{8,11},{9,10},{10,... | collective-permute-start | bytes 786440 | tf_op jit(solution)/shard_map/ppermute | solution.py:170
  77.3 11.5 %collective-permute-start.3 = (f32[8,4,2,8,128]{4,3,2,1,0:T(8,128)}, f32[8,4,2,8,128]{4,3,2,1,0:T(8,128)}, u32[]{:S(2)}, u32[]{:S(2)}) collective-permute-start(f32[8,4,2,8,128]{4,3,2,1,0:T(8,128)} %get-tuple-element.25), channel_id=1, source_target_pairs={{0,4},{1,5},{2,6},{3,7},{4,0},{5,1},{6,2},{7,3},{8,12},{9,13},{10,... | collective-permute-start | bytes 786440 | tf_op jit(solution)/shard_map/ppermute | solution.py:170
  78.5 14.3 %collective-permute-start.4 = (f32[8,4,2,8,128]{4,3,2,1,0:T(8,128)}, f32[8,4,2,8,128]{4,3,2,1,0:T(8,128)}, u32[]{:S(2)}, u32[]{:S(2)}) collective-permute-start(f32[8,4,2,8,128]{4,3,2,1,0:T(8,128)} %get-tuple-element.26), channel_id=1, source_target_pairs={{0,5},{1,4},{2,7},{3,6},{4,1},{5,0},{6,3},{7,2},{8,13},{9,12},{10,... | collective-permute-start | bytes 786440 | tf_op jit(solution)/shard_map/ppermute | solution.py:170
  80.5 24.0 %copy-start.5 = (f32[8,4,2,8,128]{4,3,2,1,0:T(8,128)}, f32[8,4,2,8,128]{4,3,2,1,0:T(8,128)S(1)}, u32[]{:S(2)}) copy-start(f32[8,4,2,8,128]{4,3,2,1,0:T(8,128)S(1)} %collective-permute-done.refs_1_) | copy-start | bytes 786436
  80.5 18.4 %collective-permute-start.5 = (f32[8,4,2,8,128]{4,3,2,1,0:T(8,128)}, f32[8,4,2,8,128]{4,3,2,1,0:T(8,128)}, u32[]{:S(2)}, u32[]{:S(2)}) collective-permute-start(f32[8,4,2,8,128]{4,3,2,1,0:T(8,128)} %get-tuple-element.27), channel_id=1, source_target_pairs={{0,6},{1,7},{2,0},{3,1},{4,2},{5,3},{6,4},{7,5},{8,14},{9,15},{10,... | collective-permute-start | bytes 786440 | tf_op jit(solution)/shard_map/ppermute | solution.py:170
  84.0 20.5 %copy-start.6 = (f32[8,4,2,8,128]{4,3,2,1,0:T(8,128)}, f32[8,4,2,8,128]{4,3,2,1,0:T(8,128)S(1)}, u32[]{:S(2)}) copy-start(f32[8,4,2,8,128]{4,3,2,1,0:T(8,128)S(1)} %collective-permute-done.1.refs_2_) | copy-start | bytes 786436
  84.0 20.5 %collective-permute-start.6 = (f32[8,4,2,8,128]{4,3,2,1,0:T(8,128)}, f32[8,4,2,8,128]{4,3,2,1,0:T(8,128)}, u32[]{:S(2)}, u32[]{:S(2)}) collective-permute-start(f32[8,4,2,8,128]{4,3,2,1,0:T(8,128)} %get-tuple-element.28), channel_id=1, source_target_pairs={{0,7},{1,6},{2,1},{3,0},{4,3},{5,2},{6,5},{7,4},{8,15},{9,14},{10,... | collective-permute-start | bytes 786440 | tf_op jit(solution)/shard_map/ppermute | solution.py:170
  88.8 15.7 %copy-start.7 = (f32[8,4,2,8,128]{4,3,2,1,0:T(8,128)}, f32[8,4,2,8,128]{4,3,2,1,0:T(8,128)S(1)}, u32[]{:S(2)}) copy-start(f32[8,4,2,8,128]{4,3,2,1,0:T(8,128)S(1)} %collective-permute-done.2.refs_3_) | copy-start | bytes 786436

commit v7 on v6

--- a/solution.py
+++ b/solution.py
@@ -72,60 +72,74 @@
         done.wait()
 
 
-def weigh(old_ref, pm_ref, steps_ref):
+def lookup_kernel(me_ref, old_ref, new_ref, pm_ref, steps_ref, table, weights):
     islands = steps_ref.shape[0]
+    table[0] = me_ref[0]
     old = [pm_ref[old_ref[j]] for j in range(islands)]
-    weights = []
     for j in range(islands):
         total = jnp.int32(0)
         for i in range(islands):
             total += jnp.where(old[i] == old[j], steps_ref[i], 0)
+        table[1 + j] = old[j]
+        table[1 + islands + j] = pm_ref[new_ref[j]]
         splat = lambda s: jnp.full(TILE, s, jnp.int32).astype(F32)
-        weights.append(splat(steps_ref[j]) / splat(jnp.maximum(total, 1)))
-    return list(zip(old, weights))
-
-
-def add_up(avg, deltas, weighted):
+        weights[j] = splat(steps_ref[j]) / splat(jnp.maximum(total, 1))
+
+
+def lookup(*scalars):
+    smem, vmem = (pl.BlockSpec(memory_space=m) for m in (pltpu.SMEM, pltpu.VMEM))
+    islands = scalars[-1].shape[0]
+    return pl.pallas_call(
+        lookup_kernel,
+        out_shape=[
+            jax.ShapeDtypeStruct((1 + 2 * islands,), jnp.int32),
+            jax.ShapeDtypeStruct((islands, *TILE), F32),
+        ],
+        in_specs=[smem] * len(scalars),
+        out_specs=[smem, vmem],
+        compiler_params=pltpu.CompilerParams(vmem_limit_bytes=4 * MIB),
+    )(*scalars)
+
+
+def add_up(avg, deltas, table, weights):
     avg[...] = jnp.zeros(avg.shape, F32)
-    for j, (k, w) in enumerate(weighted):
-        avg[k] += w * deltas[j]
+    for j in range(weights.shape[0]):
+        avg[table[1 + j]] += weights[j] * deltas[j]
 
 
 def hold_kernel(src, out, sem):
     out[...] = src[...]
 
 
-def pick_kernel(me_ref, old_ref, new_ref, pm_ref, steps_ref, r_ref, *refs):
-    me = me_ref[0]
+def pick_kernel(table, r_ref, weights, *refs):
+    me, islands = table[0], weights.shape[0]
     bases, (out, r_buf, o_buf, avg, sem) = refs[:NYC], refs[NYC:]
     copy = pltpu.make_async_copy
     rows = [behind(me, d) for d in range(NYC)]
     rs = started([copy(r_ref.at[:, :, rows[d]], r_buf.at[d], sem.at[0, d]) for d in range(NYC)])
-    weighted = weigh(old_ref, pm_ref, steps_ref)
     back = []
     for d in range(NYC):
         rs[d].wait()
-        add_up(avg, r_buf.at[d], weighted)
-        for j in range(steps_ref.shape[0]):
-            k = pm_ref[new_ref[j]]
+        add_up(avg, r_buf.at[d], table, weights)
+        for j in range(islands):
+            k = table[1 + islands + j]
             o_buf[d, j] = bases[d][k] - (0.7 * 1.9) * avg[k]
         back += started([copy(o_buf.at[d], out.at[:, :, rows[d]], sem.at[1, d])])
     for done in back:
         done.wait()
 
 
-def average_kernel(me_ref, old_ref, pm_ref, steps_ref, r_ref, *refs):
+def average_kernel(table, r_ref, weights, *refs):
     averages, (r_buf, a_buf, sem) = refs[:NYC], refs[NYC:]
     copy = pltpu.make_async_copy
-    rows = [ahead(me_ref[0], d) for d in range(NYC)]
+    rows = [ahead(table[0], d) for d in range(NYC)]
     order = (*SHIFTS, 0)
     rs = [copy(r_ref.at[:, :, rows[d]], r_buf.at[d], sem.at[0, d]) for d in range(NYC)]
     started([rs[d] for d in order])
-    weighted = weigh(old_ref, pm_ref, steps_ref)
     back = []
     for d in order:
         rs[d].wait()
-        add_up(a_buf.at[d], r_buf.at[d], weighted)
+        add_up(a_buf.at[d], r_buf.at[d], table, weights)
         back += started([copy(a_buf.at[d], averages[d], sem.at[1, d])])
     for done in back:
         done.wait()
@@ -187,26 +201,28 @@
     slots = (NYC, *piece)
     base = along_yc(call(base_kernel, [me, m, v], [piece] * NYC, 1, [slots] * 2, 3, WHOLE))
     base[0:1] = call(hold_kernel, base[0:1], [piece], 0, [], 1, 4 * MIB, (0,), (0,))
+    table, weights = lookup(me, old_path, new_path, path_module, island_steps)
     isles = (8, 4, NYC, 2, *TILE)
     mixed = tiles(got).reshape(isles)
     [out] = call(
         pick_kernel,
-        [me, old_path, new_path, path_module, island_steps, mixed, *base],
+        [table, mixed, weights, *base],
         [isles],
-        5,
+        1,
         [slots, slots, piece],
         2,
         20 * MIB,
-        range(6, 6 + NYC),
+        range(2, 3 + NYC),
     )
     avg = call(
         average_kernel,
-        [me, old_path, path_module, island_steps, mixed],
+        [table, mixed, weights],
         [piece] * NYC,
-        4,
+        1,
         [slots] * 2,
         2,
         61 * MIB,
+        (2,),
     )
     out = jnp.swapaxes(out.reshape(32, NYC, 2, *TILE), 2, 3).reshape(32, 64, 256)
     landed = across(out)

time: 123 us -> 123 us (level)
  waiting for transfers between devices: 72.4 us -> 67.4 us
  starting transfers between devices: 32.3 us -> 35.9 us
  Pallas kernels: 14.7 us -> 16 us
    ppermute x14, waiting for transfers between devices: 44.1 us -> 35.8 us  [along_yc(): got[d] = lax.ppermute(pieces[d], YC, [(i, ahead(i, d)) for i in range(NYC)])]
    ppermute x14, starting transfers between devices: 14.7 us -> 18.3 us  [along_yc(): got[d] = lax.ppermute(pieces[d], YC, [(i, ahead(i, d)) for i in range(NYC)])]
    all_to_all x2, waiting for transfers between devices: 28.3 us -> 31.7 us  [across(): return lax.all_to_all(value, XZ, split_axis=0, concat_axis=0, tiled=True)]
    pallas_call x0 -> x1, Pallas kernels: none -> 1.25 us  [lookup(): pl.pallas_call(lookup_kernel, out_shape=[jax.ShapeDtypeStruct((1 + 2 * is...]
  transfers between devices with their start and end apart: 16 -> 16, of which waited for: 12 -> 11; matrix products, arithmetic and copies ran while one was open for 0% -> 0% of each run, Pallas kernels for 9% -> 11%
where the time goes in v7:
time: 123 us; the launch traced here: 122 us
  waiting for transfers between devices  67.4 us (55%)
  starting transfers between devices  35.9 us (29%)
  Pallas kernels  16 us (13%)
  local copies, waits for them, and re-layouts  2.31 us (2%)
    ppermute x14, waiting for transfers between devices, along_yc(): got[d] = lax.ppermute(pieces[d], YC, [(i, ahead(i, d)) for i in range(NYC)])  35.8 us
    all_to_all x2, waiting for transfers between devices, across(): return lax.all_to_all(value, XZ, split_axis=0, concat_axis=0, tiled=True)  31.7 us
    ppermute x14, starting transfers between devices, along_yc(): got[d] = lax.ppermute(pieces[d], YC, [(i, ahead(i, d)) for i in range(NYC)])  18.3 us
    all_to_all x2, starting transfers between devices, across(): return lax.all_to_all(value, XZ, split_axis=0, concat_axis=0, tiled=True)  17.6 us
    pallas_call x5, Pallas kernels, call(): pl.pallas_call(body, out_shape=[jax.ShapeDtypeStruct(s, F32) for s in out...  14.8 us
  transfers between devices with their start and end apart: 16, of which 11 were waited for; matrix products, arithmetic and copies ran while one was open for 0% of the time, Pallas kernels for 11%

profile of v7, /device:TPU:8, one launch (start us, length us, event | category | flops | bytes accessed | tf_op | source)
XLA Modules:
  0.0 122.4 jit_solution(1229880731038960960)
XLA Ops:
  0.6 11.5 %all-to-all-start = ((f32[32,64,256]{2,1,0:T(8,128)}), f32[32,64,256]{2,1,0:T(8,128)}, u32[]{:S(2)}, u32[]{:S(2)}) async-start(f32[32,64,256]{2,1,0:T(8,128)} %bitcast.38), calls=%async_computation | async-start | bytes 4194304 | tf_op jit(solution)/shard_map/all_to_all | solution.py:189
  12.1 3.4 %shard_map.97 = (f32[8,4,2,8,128]{4,3,2,1,0:T(8,128)}, f32[8,4,2,8,128]{4,3,2,1,0:T(8,128)}, f32[8,4,2,8,128]{4,3,2,1,0:T(8,128)}, f32[8,4,2,8,128]{4,3,2,1,0:T(...) custom-call(s32[1]{0:T(128)} %bitcast.me_ref, ...), custom_call_target="tpu_custom_call" | custom-call | flops 6291456 | bytes 6291456 | tf_op jit(solution)/shard_map/pallas_call | solution.py:31
  15.6 2.4 %collective-permute-start.10 = (f32[8,4,2,8,128]{4,3,2,1,0:T(8,128)}, f32[8,4,2,8,128]{4,3,2,1,0:T(8,128)S(1)}, u32[]{:S(2)}, u32[]{:S(2)}) collective-permute-start(f32[8,4,2,8,128]{4,3,2,1,0:T(8,128)} %get-tuple-element.39), channel_id=1, source_target_pairs={{0,4},{1,5},{2,6},{3,7},{4,0},{5,1},{6,2},{7,3},{8,12},{9,13},{10,... | collective-permute-start | bytes 786440 | tf_op jit(solution)/shard_map/ppermute | solution.py:184
  19.3 2.8 %collective-permute-start.13 = (f32[8,4,2,8,128]{4,3,2,1,0:T(8,128)}, f32[8,4,2,8,128]{4,3,2,1,0:T(8,128)S(1)}, u32[]{:S(2)}, u32[]{:S(2)}) collective-permute-start(f32[8,4,2,8,128]{4,3,2,1,0:T(8,128)} %get-tuple-element.42), channel_id=1, source_target_pairs={{0,7},{1,6},{2,1},{3,0},{4,3},{5,2},{6,5},{7,4},{8,15},{9,14},{10,... | collective-permute-start | bytes 786440 | tf_op jit(solution)/shard_map/ppermute | solution.py:184
  22.1 4.6 %collective-permute-done.10.refs_4_ = f32[8,4,2,8,128]{4,3,2,1,0:T(8,128)S(1)} collective-permute-done((f32[8,4,2,8,128]{4,3,2,1,0:T(8,128)}, f32[8,4,2,8,128]{4,3,2,1,0:T(8,128)S(1)}, u32[]{:S(2)}, u32[]{:S(2)}) %collective-permute-start.10) | collective-permute-done | bytes 262176 | tf_op jit(solution)/shard_map/ppermute | solution.py:184
  26.7 1.5 %collective-permute-start.8 = (f32[8,4,2,8,128]{4,3,2,1,0:T(8,128)}, f32[8,4,2,8,128]{4,3,2,1,0:T(8,128)S(1)}, u32[]{:S(2)}, u32[]{:S(2)}) collective-permute-start(f32[8,4,2,8,128]{4,3,2,1,0:T(8,128)} %get-tuple-element.37), channel_id=1, source_target_pairs={{0,2},{1,3},{2,4},{3,5},{4,6},{5,7},{6,0},{7,1},{8,10},{9,11},{10,... | collective-permute-start | bytes 786440 | tf_op jit(solution)/shard_map/ppermute | solution.py:184
  28.2 2.5 %collective-permute-done.11.refs_5_ = f32[8,4,2,8,128]{4,3,2,1,0:T(8,128)S(1)} collective-permute-done((f32[8,4,2,8,128]{4,3,2,1,0:T(8,128)}, f32[8,4,2,8,128]{4,3,2,1,0:T(8,128)S(1)}, u32[]{:S(2)}, u32[]{:S(2)}) %collective-permute-start.11) | collective-permute-done | bytes 262176 | tf_op jit(solution)/shard_map/ppermute | solution.py:184
  30.7 3.0 %collective-permute-start.9 = (f32[8,4,2,8,128]{4,3,2,1,0:T(8,128)}, f32[8,4,2,8,128]{4,3,2,1,0:T(8,128)S(1)}, u32[]{:S(2)}, u32[]{:S(2)}) collective-permute-start(f32[8,4,2,8,128]{4,3,2,1,0:T(8,128)} %get-tuple-element.38), channel_id=1, source_target_pairs={{0,3},{1,2},{2,5},{3,4},{4,7},{5,6},{6,1},{7,0},{8,11},{9,10},{10,... | collective-permute-start | bytes 786440 | tf_op jit(solution)/shard_map/ppermute | solution.py:184
  36.4 5.6 %collective-permute-done.13.refs_7_ = f32[8,4,2,8,128]{4,3,2,1,0:T(8,128)S(1)} collective-permute-done((f32[8,4,2,8,128]{4,3,2,1,0:T(8,128)}, f32[8,4,2,8,128]{4,3,2,1,0:T(8,128)S(1)}, u32[]{:S(2)}, u32[]{:S(2)}) %collective-permute-start.13) | collective-permute-done | bytes 262176 | tf_op jit(solution)/shard_map/ppermute | solution.py:184
  42.0 20.1 %all-to-all-done = f32[32,64,256]{2,1,0:T(8,128)} async-done(((f32[32,64,256]{2,1,0:T(8,128)}), f32[32,64,256]{2,1,0:T(8,128)}, u32[]{:S(2)}, u32[]{:S(2)}) %all-to-all-start) | async-done | bytes 2097184 | tf_op jit(solution)/shard_map/all_to_all | solution.py:189
  62.1 3.1 %shard_map.99 = f32[8,4,8,2,8,128]{5,4,3,2,1,0:T(8,128)} custom-call(s32[17]{0:T(128)S(1)} %get-tuple-element.23.table, f32[8,4,8,2,8,128]{5,4,3,2,1,0:T(8,128)} %bitcast.10.r_ref, f32[8,8,128]{2,1,0:T(8,128)S(1)} %get-tuple-element.24.weights, f32[8,4,2,8,128]{4,3,2,1,0:T(8,128)S(1)} %shard_map.98.refs_0_, ...), custom_call_target="tpu_custom_call" | custom-call | flops 6324224 | bytes 6324224 | tf_op jit(solution)/shard_map/pallas_call | solution.py:31
  65.2 6.1 %all-to-all-start.1 = ((f32[32,64,256]{2,1,0:T(8,128)}), f32[32,64,256]{2,1,0:T(8,128)S(1)}, u32[]{:S(2)}, u32[]{:S(2)}) async-start(f32[32,64,256]{2,1,0:T(8,128)} %bitcast.25), calls=%async_computation.1 | async-start | bytes 4194304 | tf_op jit(solution)/shard_map/all_to_all | solution.py:189
  71.3 3.2 %shard_map.95 = (f32[8,4,2,8,128]{4,3,2,1,0:T(8,128)}, f32[8,4,2,8,128]{4,3,2,1,0:T(8,128)}, f32[8,4,2,8,128]{4,3,2,1,0:T(8,128)}, f32[8,4,2,8,128]{4,3,2,1,0:T(...) custom-call(s32[17]{0:T(128)} %copy-done.2, ...), custom_call_target="tpu_custom_call" | custom-call | flops 4227072 | bytes 4227072 | tf_op jit(solution)/shard_map/pallas_call | solution.py:31
  74.7 1.7 %collective-permute-start.1 = (f32[8,4,2,8,128]{4,3,2,1,0:T(8,128)}, f32[8,4,2,8,128]{4,3,2,1,0:T(8,128)S(1)}, u32[]{:S(2)}, u32[]{:S(2)}) collective-permute-start(f32[8,4,2,8,128]{4,3,2,1,0:T(8,128)} %get-tuple-element.27), channel_id=1, source_target_pairs={{0,2},{1,3},{2,4},{3,5},{4,6},{5,7},{6,0},{7,1},{8,10},{9,11},{10,... | collective-permute-start | bytes 786440 | tf_op jit(solution)/shard_map/ppermute | solution.py:184
  77.4 1.2 %collective-permute-start.3 = (f32[8,4,2,8,128]{4,3,2,1,0:T(8,128)}, f32[8,4,2,8,128]{4,3,2,1,0:T(8,128)}, u32[]{:S(2)}, u32[]{:S(2)}) collective-permute-start(f32[8,4,2,8,128]{4,3,2,1,0:T(8,128)} %get-tuple-element.29), channel_id=1, source_target_pairs={{0,4},{1,5},{2,6},{3,7},{4,0},{5,1},{6,2},{7,3},{8,12},{9,13},{10,... | collective-permute-start | bytes 786440 | tf_op jit(solution)/shard_map/ppermute | solution.py:184
  78.6 2.0 %collective-permute-start.4 = (f32[8,4,2,8,128]{4,3,2,1,0:T(8,128)}, f32[8,4,2,8,128]{4,3,2,1,0:T(8,128)}, u32[]{:S(2)}, u32[]{:S(2)}) collective-permute-start(f32[8,4,2,8,128]{4,3,2,1,0:T(8,128)} %get-tuple-element.30), channel_id=1, source_target_pairs={{0,5},{1,4},{2,7},{3,6},{4,1},{5,0},{6,3},{7,2},{8,13},{9,12},{10,... | collective-permute-start | bytes 786440 | tf_op jit(solution)/shard_map/ppermute | solution.py:184
  81.3 2.7 %collective-permute-done.1.refs_2_ = f32[8,4,2,8,128]{4,3,2,1,0:T(8,128)S(1)} collective-permute-done((f32[8,4,2,8,128]{4,3,2,1,0:T(8,128)}, f32[8,4,2,8,128]{4,3,2,1,0:T(8,128)S(1)}, u32[]{:S(2)}, u32[]{:S(2)}) %collective-permute-start.1) | collective-permute-done | bytes 262176 | tf_op jit(solution)/shard_map/ppermute | solution.py:184
  84.6 4.2 %collective-permute-done.2.refs_3_ = f32[8,4,2,8,128]{4,3,2,1,0:T(8,128)S(1)} collective-permute-done((f32[8,4,2,8,128]{4,3,2,1,0:T(8,128)}, f32[8,4,2,8,128]{4,3,2,1,0:T(8,128)S(1)}, u32[]{:S(2)}, u32[]{:S(2)}) %collective-permute-start.2) | collective-permute-done | bytes 262176 | tf_op jit(solution)/shard_map/ppermute | solution.py:184
  88.9 4.0 %collective-permute-done.4.refs_5_ = f32[8,4,2,8,128]{4,3,2,1,0:T(8,128)} collective-permute-done((f32[8,4,2,8,128]{4,3,2,1,0:T(8,128)}, f32[8,4,2,8,128]{4,3,2,1,0:T(8,128)}, u32[]{:S(2)}, u32[]{:S(2)}) %collective-permute-start.4) | collective-permute-done | bytes 262176 | tf_op jit(solution)/shard_map/ppermute | solution.py:184
  92.9 6.1 %collective-permute-done.5.refs_6_ = f32[8,4,2,8,128]{4,3,2,1,0:T(8,128)} collective-permute-done((f32[8,4,2,8,128]{4,3,2,1,0:T(8,128)}, f32[8,4,2,8,128]{4,3,2,1,0:T(8,128)}, u32[]{:S(2)}, u32[]{:S(2)}) %collective-permute-start.5) | collective-permute-done | bytes 262176 | tf_op jit(solution)/shard_map/ppermute | solution.py:184
  99.0 5.5 %collective-permute-done.6.refs_7_ = f32[8,4,2,8,128]{4,3,2,1,0:T(8,128)} collective-permute-done((f32[8,4,2,8,128]{4,3,2,1,0:T(8,128)}, f32[8,4,2,8,128]{4,3,2,1,0:T(8,128)}, u32[]{:S(2)}, u32[]{:S(2)}) %collective-permute-start.6) | collective-permute-done | bytes 262176 | tf_op jit(solution)/shard_map/ppermute | solution.py:184
  104.6 5.0 %shard_map.96 = (f32[8,4,8,2,8,128]{5,4,3,2,1,0:T(8,128)}, f32[8,4,8,2,8,128]{5,4,3,2,1,0:T(8,128)}) custom-call(s32[1]{0:T(128)} %bitcast.me_ref, f32[8,4,8,2,8,128]{5,4,3,2,1,0:T(8,128)} %bitcast.34, f32[8,4,8,2,8,128]{5,4,3,2,1,0:T(8,128)} %bitcast.36, f32[8,4,2,8,128]{4,3,2,1,0:T(8,128)} %get-tuple-element.25.refs_0_, f32[8,4,2,8,128]{4,3,2,1,0:T(8,128)} %copy-done.7, ...), custom_call_target="tpu_custom_call" | custom-call | flops 10485760 | bytes 10485760 | tf_op jit(solution)/shard_map/pallas_call | solution.py:31
  109.5 11.6 %all-to-all-done.1 = f32[32,64,256]{2,1,0:T(8,128)S(1)} async-done(((f32[32,64,256]{2,1,0:T(8,128)}), f32[32,64,256]{2,1,0:T(8,128)S(1)}, u32[]{:S(2)}, u32[]{:S(2)}) %all-to-all-start.1) | async-done | bytes 2097184 | tf_op jit(solution)/shard_map/all_to_all | solution.py:189
  121.1 1.3 %copy.11 = f32[1,2048,256]{2,1,0:T(8,128)} copy(f32[1,2048,256]{2,1,0:T(8,128)S(1)} %bitcast.37) | data formatting | bytes 4194304
  (35 shorter events, 6.5 us)
Async XLA Ops:
  0.6 61.5 %all-to-all-start = ((f32[32,64,256]{2,1,0:T(8,128)}), f32[32,64,256]{2,1,0:T(8,128)}, u32[]{:S(2)}, u32[]{:S(2)}) async-start(f32[32,64,256]{2,1,0:T(8,128)} %bitcast.38), calls=%async_computation | async-start | bytes 4194304 | tf_op jit(solution)/shard_map/all_to_all | solution.py:189
  12.1 21.6 %copy-start.3 = (s32[256]{0:T(256)S(1)}, s32[256]{0:T(256)}, u32[]{:S(2)}) copy-start(s32[256]{0:T(256)} %pm_ref.1) | copy-start | bytes 3076
  12.1 21.6 %copy-start.4 = (s32[8]{0:T(128)S(1)}, s32[8]{0:T(128)}, u32[]{:S(2)}) copy-start(s32[8]{0:T(128)} %old_ref.1) | copy-start | bytes 100
  12.1 21.6 %copy-start.5 = (s32[8]{0:T(128)S(1)}, s32[8]{0:T(128)}, u32[]{:S(2)}) copy-start(s32[8]{0:T(128)} %new_ref.1) | copy-start | bytes 100
  12.1 21.6 %copy-start.6 = (s32[8]{0:T(128)S(1)}, s32[8]{0:T(128)}, u32[]{:S(2)}) copy-start(s32[8]{0:T(128)} %steps_ref.1) | copy-start | bytes 100
  15.6 11.1 %collective-permute-start.10 = (f32[8,4,2,8,128]{4,3,2,1,0:T(8,128)}, f32[8,4,2,8,128]{4,3,2,1,0:T(8,128)S(1)}, u32[]{:S(2)}, u32[]{:S(2)}) collective-permute-start(f32[8,4,2,8,128]{4,3,2,1,0:T(8,128)} %get-tuple-element.39), channel_id=1, source_target_pairs={{0,4},{1,5},{2,6},{3,7},{4,0},{5,1},{6,2},{7,3},{8,12},{9,13},{10,... | collective-permute-start | bytes 786440 | tf_op jit(solution)/shard_map/ppermute | solution.py:184
  18.0 12.7 %collective-permute-start.11 = (f32[8,4,2,8,128]{4,3,2,1,0:T(8,128)}, f32[8,4,2,8,128]{4,3,2,1,0:T(8,128)S(1)}, u32[]{:S(2)}, u32[]{:S(2)}) collective-permute-start(f32[8,4,2,8,128]{4,3,2,1,0:T(8,128)} %get-tuple-element.40), channel_id=1, source_target_pairs={{0,5},{1,4},{2,7},{3,6},{4,1},{5,0},{6,3},{7,2},{8,13},{9,12},{10,... | collective-permute-start | bytes 786440 | tf_op jit(solution)/shard_map/ppermute | solution.py:184
  18.1 18.3 %collective-permute-start.12 = (f32[8,4,2,8,128]{4,3,2,1,0:T(8,128)}, f32[8,4,2,8,128]{4,3,2,1,0:T(8,128)S(1)}, u32[]{:S(2)}, u32[]{:S(2)}) collective-permute-start(f32[8,4,2,8,128]{4,3,2,1,0:T(8,128)} %get-tuple-element.41), channel_id=1, source_target_pairs={{0,6},{1,7},{2,0},{3,1},{4,2},{5,3},{6,4},{7,5},{8,14},{9,15},{10,... | collective-permute-start | bytes 786440 | tf_op jit(solution)/shard_map/ppermute | solution.py:184
  19.3 22.7 %collective-permute-start.13 = (f32[8,4,2,8,128]{4,3,2,1,0:T(8,128)}, f32[8,4,2,8,128]{4,3,2,1,0:T(8,128)S(1)}, u32[]{:S(2)}, u32[]{:S(2)}) collective-permute-start(f32[8,4,2,8,128]{4,3,2,1,0:T(8,128)} %get-tuple-element.42), channel_id=1, source_target_pairs={{0,7},{1,6},{2,1},{3,0},{4,3},{5,2},{6,5},{7,4},{8,15},{9,14},{10,... | collective-permute-start | bytes 786440 | tf_op jit(solution)/shard_map/ppermute | solution.py:184
  22.1 19.9 %collective-permute-start.7 = (f32[8,4,2,8,128]{4,3,2,1,0:T(8,128)}, f32[8,4,2,8,128]{4,3,2,1,0:T(8,128)S(1)}, u32[]{:S(2)}, u32[]{:S(2)}) collective-permute-start(f32[8,4,2,8,128]{4,3,2,1,0:T(8,128)} %get-tuple-element.36), channel_id=1, source_target_pairs={{0,1},{1,0},{2,3},{3,2},{4,5},{5,4},{6,7},{7,6},{8,9},{9,8},{10,11... | collective-permute-start | bytes 786440 | tf_op jit(solution)/shard_map/ppermute | solution.py:184
  26.7 15.3 %collective-permute-start.8 = (f32[8,4,2,8,128]{4,3,2,1,0:T(8,128)}, f32[8,4,2,8,128]{4,3,2,1,0:T(8,128)S(1)}, u32[]{:S(2)}, u32[]{:S(2)}) collective-permute-start(f32[8,4,2,8,128]{4,3,2,1,0:T(8,128)} %get-tuple-element.37), channel_id=1, source_target_pairs={{0,2},{1,3},{2,4},{3,5},{4,6},{5,7},{6,0},{7,1},{8,10},{9,11},{10,... | collective-permute-start | bytes 786440 | tf_op jit(solution)/shard_map/ppermute | solution.py:184
  30.7 11.3 %collective-permute-start.9 = (f32[8,4,2,8,128]{4,3,2,1,0:T(8,128)}, f32[8,4,2,8,128]{4,3,2,1,0:T(8,128)S(1)}, u32[]{:S(2)}, u32[]{:S(2)}) collective-permute-start(f32[8,4,2,8,128]{4,3,2,1,0:T(8,128)} %get-tuple-element.38), channel_id=1, source_target_pairs={{0,3},{1,2},{2,5},{3,4},{4,7},{5,6},{6,1},{7,0},{8,11},{9,10},{10,... | collective-permute-start | bytes 786440 | tf_op jit(solution)/shard_map/ppermute | solution.py:184
  35.0 30.2 %copy-start.1 = (f32[8,8,128]{2,1,0:T(8,128)}, f32[8,8,128]{2,1,0:T(8,128)S(1)}, u32[]{:S(2)}) copy-start(f32[8,8,128]{2,1,0:T(8,128)S(1)} %get-tuple-element.24.weights) | copy-start | bytes 98308
  35.0 30.2 %copy-start.2 = (s32[17]{0:T(128)}, s32[17]{0:T(128)S(1)}, u32[]{:S(2)}) copy-start(s32[17]{0:T(128)S(1)} %get-tuple-element.23.table) | copy-start | bytes 208
  65.2 55.9 %all-to-all-start.1 = ((f32[32,64,256]{2,1,0:T(8,128)}), f32[32,64,256]{2,1,0:T(8,128)S(1)}, u32[]{:S(2)}, u32[]{:S(2)}) async-start(f32[32,64,256]{2,1,0:T(8,128)} %bitcast.25), calls=%async_computation.1 | async-start | bytes 4194304 | tf_op jit(solution)/shard_map/all_to_all | solution.py:189
  74.6 6.0 %collective-permute-start = (f32[8,4,2,8,128]{4,3,2,1,0:T(8,128)}, f32[8,4,2,8,128]{4,3,2,1,0:T(8,128)S(1)}, u32[]{:S(2)}, u32[]{:S(2)}) collective-permute-start(f32[8,4,2,8,128]{4,3,2,1,0:T(8,128)} %get-tuple-element.26), channel_id=1, source_target_pairs={{0,1},{1,0},{2,3},{3,2},{4,5},{5,4},{6,7},{7,6},{8,9},{9,8},{10,11... | collective-permute-start | bytes 786440 | tf_op jit(solution)/shard_map/ppermute | solution.py:184
  74.7 9.4 %collective-permute-start.1 = (f32[8,4,2,8,128]{4,3,2,1,0:T(8,128)}, f32[8,4,2,8,128]{4,3,2,1,0:T(8,128)S(1)}, u32[]{:S(2)}, u32[]{:S(2)}) collective-permute-start(f32[8,4,2,8,128]{4,3,2,1,0:T(8,128)} %get-tuple-element.27), channel_id=1, source_target_pairs={{0,2},{1,3},{2,4},{3,5},{4,6},{5,7},{6,0},{7,1},{8,10},{9,11},{10,... | collective-permute-start | bytes 786440 | tf_op jit(solution)/shard_map/ppermute | solution.py:184
  76.3 12.5 %collective-permute-start.2 = (f32[8,4,2,8,128]{4,3,2,1,0:T(8,128)}, f32[8,4,2,8,128]{4,3,2,1,0:T(8,128)S(1)}, u32[]{:S(2)}, u32[]{:S(2)}) collective-permute-start(f32[8,4,2,8,128]{4,3,2,1,0:T(8,128)} %get-tuple-element.28), channel_id=1, source_target_pairs={{0,3},{1,2},{2,5},{3,4},{4,7},{5,6},{6,1},{7,0},{8,11},{9,10},{10,... | collective-permute-start | bytes 786440 | tf_op jit(solution)/shard_map/ppermute | solution.py:184
  77.4 11.5 %collective-permute-start.3 = (f32[8,4,2,8,128]{4,3,2,1,0:T(8,128)}, f32[8,4,2,8,128]{4,3,2,1,0:T(8,128)}, u32[]{:S(2)}, u32[]{:S(2)}) collective-permute-start(f32[8,4,2,8,128]{4,3,2,1,0:T(8,128)} %get-tuple-element.29), channel_id=1, source_target_pairs={{0,4},{1,5},{2,6},{3,7},{4,0},{5,1},{6,2},{7,3},{8,12},{9,13},{10,... | collective-permute-start | bytes 786440 | tf_op jit(solution)/shard_map/ppermute | solution.py:184
  78.6 14.3 %collective-permute-start.4 = (f32[8,4,2,8,128]{4,3,2,1,0:T(8,128)}, f32[8,4,2,8,128]{4,3,2,1,0:T(8,128)}, u32[]{:S(2)}, u32[]{:S(2)}) collective-permute-start(f32[8,4,2,8,128]{4,3,2,1,0:T(8,128)} %get-tuple-element.30), channel_id=1, source_target_pairs={{0,5},{1,4},{2,7},{3,6},{4,1},{5,0},{6,3},{7,2},{8,13},{9,12},{10,... | collective-permute-start | bytes 786440 | tf_op jit(solution)/shard_map/ppermute | solution.py:184
  80.6 24.0 %copy-start.7 = (f32[8,4,2,8,128]{4,3,2,1,0:T(8,128)}, f32[8,4,2,8,128]{4,3,2,1,0:T(8,128)S(1)}, u32[]{:S(2)}) copy-start(f32[8,4,2,8,128]{4,3,2,1,0:T(8,128)S(1)} %collective-permute-done.refs_1_) | copy-start | bytes 786436
  80.6 18.4 %collective-permute-start.5 = (f32[8,4,2,8,128]{4,3,2,1,0:T(8,128)}, f32[8,4,2,8,128]{4,3,2,1,0:T(8,128)}, u32[]{:S(2)}, u32[]{:S(2)}) collective-permute-start(f32[8,4,2,8,128]{4,3,2,1,0:T(8,128)} %get-tuple-element.31), channel_id=1, source_target_pairs={{0,6},{1,7},{2,0},{3,1},{4,2},{5,3},{6,4},{7,5},{8,14},{9,15},{10,... | collective-permute-start | bytes 786440 | tf_op jit(solution)/shard_map/ppermute | solution.py:184
  84.1 20.5 %copy-start.8 = (f32[8,4,2,8,128]{4,3,2,1,0:T(8,128)}, f32[8,4,2,8,128]{4,3,2,1,0:T(8,128)S(1)}, u32[]{:S(2)}) copy-start(f32[8,4,2,8,128]{4,3,2,1,0:T(8,128)S(1)} %collective-permute-done.1.refs_2_) | copy-start | bytes 786436
  84.1 20.5 %collective-permute-start.6 = (f32[8,4,2,8,128]{4,3,2,1,0:T(8,128)}, f32[8,4,2,8,128]{4,3,2,1,0:T(8,128)}, u32[]{:S(2)}, u32[]{:S(2)}) collective-permute-start(f32[8,4,2,8,128]{4,3,2,1,0:T(8,128)} %get-tuple-element.32), channel_id=1, source_target_pairs={{0,7},{1,6},{2,1},{3,0},{4,3},{5,2},{6,5},{7,4},{8,15},{9,14},{10,... | collective-permute-start | bytes 786440 | tf_op jit(solution)/shard_map/ppermute | solution.py:184
  (2 other events, 16.7 us)
